TPU v7x, 32 devices: a whole 2x2x4 slice. The times are simulated.
32 devices in a mesh: dp: 4 (over y, x), space: 8 (over z, core).
Axes of the slice: x: 2, y: 2, z: 4, core: 2. Of those that a mesh axis runs over, the one named last changes fastest.
Arguments:
- voxel_feats: bfloat16 [4, 1024, 256], P('dp', 'space'), may hold values from -6 to 6
- neighbours: int32 [4, 1024, 6], P('dp', 'space'), may hold values from 0 to 192
- wanted_rows: int32 [4, 8, 8, 8], P('dp', 'space'), may hold values from 0 to 127
- live_counts: int32 [4, 8], P('dp'), may hold values from 1 to 128, 768 in all within a row
- block_choice: int32 [4, 16, 4], P('dp', 'space'), may hold values from 0 to 15, all different within a row
- conv_weight: bfloat16 [7, 256, 512], P(None, 'space'), may hold values from -0.125 to 0.125
- norm_gain: float32 [512], replicated, may hold values from 0.1 to 1.9
- input_weight: bfloat16 [512, 2304], P('space'), may hold values from -5 to 5
- output_weight: bfloat16 [768, 512], P('space'), may hold values from -0.21875 to 0.21875
- cotangent: bfloat16 [4, 1024, 512], P('dp', 'space'), may hold values from -6 to 6
Outputs:
- layer_output: bfloat16 [4, 1024, 512], P('dp', 'space')
- output_grad: float32 [768, 512], P('space')
Inputs may be any that keep to these rules, and one draw needn't show every extreme that they name: `neighbours`: an entry below 128 names a row of the device's own shard, entry 128 + p * 8 + c names the row taken from peer p in slot c, and the largest value names an absent neighbour. `wanted_rows`: places within the peer's shard. `block_choice`: each row names distinct blocks.
All inputs are finite; a program needn't handle non-finite values.
Results may differ from a plain program's by a relative error of at most 0.025.
Values may be sent and summed in bfloat16 or wider, within the bound.
No kernel may reach another device: no remote copies, remote signals or barrier semaphores. Data moves between devices by JAX's collectives and lax.ppermute only.
A program may use at most 64 MiB of HBM per device.

v0:
```python
import jax
import jax.numpy as jnp
from jax import lax
from jax.sharding import PartitionSpec as P

HEADS = 12
HEAD_DIM = 64
BLK = 64
SEL = 4


def attend(query, keys, values, key_live, short_keys, short_values):
    scale = HEAD_DIM ** (-0.5)
    near = jnp.einsum("bqhd,bkhd->bhqk", query, keys, preferred_element_type=jnp.float32) * scale
    near = jnp.where(key_live[:, None, None, :], near, -1e30)
    far = (
        jnp.einsum("bqhd,bshd->bhqs", query, short_keys, preferred_element_type=jnp.float32) * scale
    )
    scores = jnp.concatenate([near, far], axis=-1)
    highest = jnp.max(scores, axis=-1, keepdims=True)
    weights = jnp.exp(scores - highest)
    weights = (weights / jnp.sum(weights, axis=-1, keepdims=True)).astype(jnp.bfloat16)
    mixed = jnp.einsum(
        "bhqk,bkhd->bqhd", weights[..., :BLK], values, preferred_element_type=jnp.float32
    )
    return mixed + jnp.einsum(
        "bhqs,bshd->bqhd", weights[..., BLK:], short_values, preferred_element_type=jnp.float32
    )


def shards(
    voxel_feats,
    neighbours,
    wanted_rows,
    live_counts,
    block_choice,
    conv_weight,
    norm_gain,
    input_weight,
    output_weight,
    cotangent,
):
    space_count = lax.axis_size("space")
    position = lax.axis_index("space")
    own_rows = voxel_feats[0]
    shard_rows = own_rows.shape[0]
    index_map = neighbours[0]
    zero_row = jnp.zeros((1, own_rows.shape[1]), jnp.bfloat16)
    requested = lax.all_to_all(wanted_rows[0, 0], "space", split_axis=0, concat_axis=0, tiled=True)
    answers = own_rows[requested]
    arrived = lax.all_to_all(answers, "space", split_axis=0, concat_axis=0, tiled=True)
    padded = jnp.concatenate([own_rows, arrived.reshape(-1, own_rows.shape[1]), zero_row], axis=0)
    gathered_taps = padded[index_map]
    table = jnp.concatenate([own_rows[:, None, :], gathered_taps], axis=1)
    columns = table
    hidden = jnp.einsum(
        "tkr,kro->to",
        columns,
        lax.all_gather(conv_weight, "space", axis=1, tiled=True),
        preferred_element_type=jnp.float32,
    )
    live_count = lax.dynamic_index_in_dim(live_counts[0], position, keepdims=False)
    live = jnp.arange(shard_rows, dtype=jnp.int32) < live_count
    live_f = live.astype(jnp.float32)
    hidden = hidden * live_f[:, None]
    power = jnp.mean(hidden * hidden, axis=-1, keepdims=True)
    normed = (hidden * lax.rsqrt(power + 1e-06) * norm_gain).astype(jnp.bfloat16)
    columns = normed
    projected = jnp.dot(
        columns,
        lax.all_gather(input_weight, "space", axis=0, tiled=True),
        preferred_element_type=jnp.float32,
    ).astype(jnp.bfloat16)
    att_width = input_weight.shape[1] // 3
    local_blocks = shard_rows // BLK
    query = projected[:, :att_width].reshape(local_blocks, BLK, HEADS, HEAD_DIM)
    keys = projected[:, att_width : 2 * att_width]
    values = projected[:, 2 * att_width :]
    block_live = live_f.reshape(local_blocks, BLK)
    divisor = jnp.maximum(jnp.sum(block_live, axis=1), 1.0)[:, None]
    short_keys = (
        jnp.sum(
            keys.astype(jnp.float32).reshape(local_blocks, BLK, att_width) * block_live[:, :, None],
            axis=1,
        )
        / divisor
    ).astype(jnp.bfloat16)
    short_values = (
        jnp.sum(
            values.astype(jnp.float32).reshape(local_blocks, BLK, att_width)
            * block_live[:, :, None],
            axis=1,
        )
        / divisor
    ).astype(jnp.bfloat16)
    every_keys, every_values = (
        lax.all_gather(short_keys, "space", axis=0, tiled=True),
        lax.all_gather(short_values, "space", axis=0, tiled=True),
    )
    chosen = block_choice[0]
    picked_keys = every_keys[chosen].reshape(local_blocks, SEL, HEADS, HEAD_DIM)
    picked_values = every_values[chosen].reshape(local_blocks, SEL, HEADS, HEAD_DIM)
    mixed = attend(
        query,
        keys.reshape(local_blocks, BLK, HEADS, HEAD_DIM),
        values.reshape(local_blocks, BLK, HEADS, HEAD_DIM),
        live.reshape(local_blocks, BLK),
        picked_keys,
        picked_values,
    )
    attended = (mixed.reshape(shard_rows, att_width) * live_f[:, None]).astype(jnp.bfloat16)
    columns = attended
    projected_out = jnp.dot(
        columns,
        lax.all_gather(output_weight, "space", axis=0, tiled=True),
        preferred_element_type=jnp.float32,
    )
    layer = (hidden + projected_out).astype(jnp.bfloat16)[None]
    upstream = cotangent[0]
    factor = (lax.axis_size("dp") * space_count * shard_rows) ** (-0.5)
    shard_sum = lax.psum_scatter(
        jnp.dot(attended.T, upstream, preferred_element_type=jnp.float32).astype(jnp.bfloat16),
        "space",
        scatter_dimension=0,
        tiled=True,
    )
    gradient = lax.psum(shard_sum, "dp").astype(jnp.float32)
    return (layer, gradient * factor)


def solution(mesh):
    placed = (
        P("dp", "space", None),
        P("dp", "space", None),
        P("dp", "space", None, None),
        P("dp", None),
        P("dp", "space", None),
        P(None, "space", None),
        P(),
        P("space", None),
        P("space", None),
        P("dp", "space", None),
    )
    return jax.shard_map(
        shards,
        mesh=mesh,
        in_specs=placed,
        out_specs=(P("dp", "space", None), P("space", None)),
        check_vma=False,
    )
```

profile of v0, /device:TPU:0, one launch (start us, length us, event | category | flops | bytes accessed | tf_op | source)
XLA Modules:
  0.0 193.5 jit_solution(17987904001248113539)
XLA Ops:
  7.2 0.7 all-gather.5.cloned.1.call-update
  8.0 0.7 all-gather.7.cloned.1.call-update
  8.7 6.4 %all-to-all-start = ((s32[8,1,8]{2,1,0:T(1,128)}), s32[8,1,8]{2,1,0:T(1,128)S(1)}, u32[]{:S(2)}, u32[]{:S(2)}) async-start(s32[8,1,8]{2,1,0:T(1,128)} %bitcast.54), calls=%async_computation | async-start | bytes 8192 | tf_op jit(solution)/shard_map/all_to_all | solution.py:49
  15.0 0.7 compare_select_fusion
  15.7 0.1 copy.36
  15.8 0.1 reshape.200
  16.0 0.7 compare_select_fusion.2
  16.7 1.2 constant_dynamic-slice_fusion
  18.0 0.8 convert_reduce_fusion
  18.8 0.7 add_compare_fusion
  19.5 1.0 all-to-all-done
  20.6 2.1 %gather_fusion = bf16[64,256]{1,0:T(8,128)(2,1)} fusion(bf16[128,256]{1,0:T(8,128)(2,1)} %bitcast.49, s32[1024]{0:T(1024)S(1)} %pad_clamp_fusion.2), kind=kCustom, calls=%fused_computation | custom fusion | bytes 65792 | tf_op jit(solution)/shard_map/gather | solution.py:50
  22.8 4.1 %all-to-all-start.1 = ((bf16[8,8,256]{2,1,0:T(8,128)(2,1)}), bf16[8,8,256]{2,1,0:T(8,128)(2,1)S(1)}, u32[]{:S(2)}, u32[]{:S(2)}) async-start(bf16[8,8,256]{2,1,0:T(8,128)(2,1)} %bitcast.5), calls=%async_computation.1 | async-start | bytes 65536 | tf_op jit(solution)/shard_map/all_to_all | solution.py:51
  26.9 0.7 compare_convert_fusion
  27.5 5.5 %all-to-all-done.1 = bf16[8,8,256]{2,1,0:T(8,128)(2,1)S(1)} async-done(((bf16[8,8,256]{2,1,0:T(8,128)(2,1)}), bf16[8,8,256]{2,1,0:T(8,128)(2,1)S(1)}, u32[]{:S(2)}, u32[]{:S(2)}) %all-to-all-start.1) | async-done | bytes 32800 | tf_op jit(solution)/shard_map/all_to_all | solution.py:51
  33.0 0.9 maximum_maximum_fusion
  34.0 2.7 %gather_fusion.1 = bf16[768,256]{1,0:T(8,128)(2,1)S(1)} fusion(bf16[193,256]{1,0:T(8,128)(2,1)S(1)} %maximum_maximum_fusion, s32[1024]{0:T(1024)S(1)} %pad_clamp_fusion.1), kind=kCustom, calls=%fused_computation.1 | custom fusion | bytes 789504 | tf_op jit(solution)/shard_map/gather | solution.py:53
  36.6 0.1 reshape.199
  36.9 3.3 %all-gather.5.cloned.1.call-done = bf16[7,256,512]{2,1,0:T(8,128)(2,1)} async-done(((bf16[7,32,512]{2,1,0:T(8,128)(2,1)}), bf16[7,256,512]{2,1,0:T(8,128)(2,1)}) %all-gather.5.cloned.1.call-update) | async-done | bytes 1835024 | tf_op jit(solution)/shard_map/all_gather | solution.py:59
  40.2 2.0 %multiply_reduce_fusion = (f32[128]{0:T(128)S(1)}, f32[128,512]{1,0:T(8,128)S(1)}) fusion(f32[128]{0:T(128)S(1)} %compare_convert_fusion, bf16[7,256,512]{2,1,0:T(8,128)(2,1)} %all-gather.5.cloned.1.call-done, bf16[128,6,256]{2,0,1:T(8,128)(2,1)S(1)} %copy.37, bf16[128,1,256]{2,0,1:T(8,128)(2,1)S(1)} %bitcast.51), kind=kOutput, calls=%fused_computation.36 | convolution fusion | flops 235306880 | bytes 2556928 | tf_op jit(solution)/shard_map/tkr,kro->to/dot_general | solution.py:56
  42.2 30.3 %all-gather.7.cloned.1.call-done = bf16[512,2304]{1,0:T(8,128)(2,1)} async-done(((bf16[64,2304]{1,0:T(8,128)(2,1)}), bf16[512,2304]{1,0:T(8,128)(2,1)}) %all-gather.7.cloned.1.call-update) | async-done | bytes 2359312 | tf_op jit(solution)/shard_map/all_gather | solution.py:71
  72.5 2.2 %convolution_convert_fusion = bf16[128,2304]{1,0:T(8,128)(2,1)S(1)} fusion(bf16[512,2304]{1,0:T(8,128)(2,1)} %all-gather.7.cloned.1.call-done, f32[128,512]{1,0:T(8,128)S(1)} %get-tuple-element.9, f32[512]{0:T(512)S(1)} %copy-done.3, f32[128]{0:T(128)S(1)} %add_rsqrt_fusion), kind=kOutput, calls=%fused_computation.4 | convolution fusion | flops 302481408 | bytes 3213824 | tf_op jit(solution)/shard_map/dot_general | solution.py:69
  74.7 0.2 fusion.12
  74.9 14.0 %all-gather = bf16[8,2,768]{2,1,0:T(2,128)(2,1)S(1)} all-gather(bf16[1,2,768]{2,1,0:T(2,128)(2,1)S(1)} %get-tuple-element.7), channel_id=1, replica_groups=mesh['dp'=4,'space'=8] {'space'}, dimensions={0}, use_global_device_ids=true | all-gather | bytes 27648 | tf_op jit(solution)/shard_map/all_gather | solution.py:97
  88.9 0.6 gather_fusion.2
  89.5 0.1 reshape.181
  89.6 0.3 reshape.235
  89.9 0.3 reshape.234
  90.3 0.4 fusion.30
  90.7 0.4 fusion.29
  91.1 0.7 fusion.19
  91.9 0.7 divide_convert_fusion
  92.6 14.0 %all-gather.1 = bf16[8,2,768]{2,1,0:T(2,128)(2,1)S(1)} all-gather(bf16[1,2,768]{2,1,0:T(2,128)(2,1)S(1)} %get-tuple-element.6), channel_id=1, replica_groups=mesh['dp'=4,'space'=8] {'space'}, dimensions={0}, use_global_device_ids=true | all-gather | bytes 27648 | tf_op jit(solution)/shard_map/all_gather | solution.py:98
  106.5 0.6 gather_fusion.3
  107.1 0.1 reshape.184
  107.2 0.3 reshape.233
  107.5 0.5 fusion.9
  108.0 0.4 multiply_convert_fusion
  108.5 0.4 copy.50
  108.9 0.2 convert_element_type.59
  109.1 1.2 convolution_convert_fusion.1
  110.4 16.3 %all_gather.19 = bf16[768,512]{1,0:T(8,128)(2,1)S(1)} all-gather(bf16[96,512]{1,0:T(8,128)(2,1)S(1)} %copy-done.2), channel_id=1, replica_groups=mesh['dp'=4,'space'=8] {'space'}, dimensions={0}, use_global_device_ids=true | all-gather | bytes 884736 | tf_op jit(solution)/shard_map/all_gather | solution.py:115
  126.7 0.6 copy.49
  127.4 0.4 reshape.185
  127.8 14.5 %reduce-scatter.2.cloned.1.call-done = bf16[96,512]{1,0:T(8,128)(2,1)} async-done(((bf16[768,512]{1,0:T(8,128)(2,1)}), bf16[96,512]{1,0:T(8,128)(2,1)}) %reduce-scatter.2.cloned.1.call-update) | async-done | bytes 98320 | tf_op jit(solution)/shard_map/reduce_scatter | solution.py:121
  142.4 1.0 fusion.4
  143.3 42.1 %all-reduce.2.cloned.1.call-done = bf16[96,512]{1,0:T(8,128)(2,1)} async-done(((bf16[96,512]{1,0:T(8,128)(2,1)}), bf16[96,512]{1,0:T(8,128)(2,1)}) %all-reduce.2.cloned.1.call-update) | async-done | bytes 98320 | tf_op jit(solution)/shard_map/psum | solution.py:127
  185.4 1.6 convert_multiply_fusion.2
  (29 shorter events, 0.7 us)
Async XLA Ops:
  7.2 101.9 %copy-start = (bf16[1,128,512]{2,1,0:T(8,128)(2,1)S(1)}, bf16[1,128,512]{2,1,0:T(8,128)(2,1)}, u32[]{:S(2)}) copy-start(bf16[1,128,512]{2,1,0:T(8,128)(2,1)} %param.19) | copy-start | bytes 393220
  7.2 33.0 %all-gather.5.cloned.1.call-start = ((), (), s32[]{:S(2)}) async-start(), calls=%async_computation.3 | async-start | bytes 2064384 | tf_op jit(solution)/shard_map/all_gather | solution.py:59
  7.9 64.6 %all-gather.7.cloned.1.call-start = ((), (), s32[]{:S(2)}) async-start(), calls=%async_computation.4 | async-start | bytes 2654208 | tf_op jit(solution)/shard_map/all_gather | solution.py:71
  8.7 11.9 %all-to-all-start = ((s32[8,1,8]{2,1,0:T(1,128)}), s32[8,1,8]{2,1,0:T(1,128)S(1)}, u32[]{:S(2)}, u32[]{:S(2)}) async-start(s32[8,1,8]{2,1,0:T(1,128)} %bitcast.54), calls=%async_computation | async-start | bytes 8192 | tf_op jit(solution)/shard_map/all_to_all | solution.py:49
  22.8 10.3 %all-to-all-start.1 = ((bf16[8,8,256]{2,1,0:T(8,128)(2,1)}), bf16[8,8,256]{2,1,0:T(8,128)(2,1)S(1)}, u32[]{:S(2)}, u32[]{:S(2)}) async-start(bf16[8,8,256]{2,1,0:T(8,128)(2,1)} %bitcast.5), calls=%async_computation.1 | async-start | bytes 65536 | tf_op jit(solution)/shard_map/all_to_all | solution.py:51
  26.8 115.5 %reduce-scatter.2.cloned.1.call-start = ((), (), s32[]{:S(2)}) async-start(), calls=%async_computation.5 | async-start | bytes 884736 | tf_op jit(solution)/shard_map/reduce_scatter | solution.py:121
  36.6 3.5 %copy-start.1 = (bf16[1,128,256]{2,1,0:T(8,128)(2,1)S(1)}, bf16[1,128,256]{2,1,0:T(8,128)(2,1)}, u32[]{:S(2)}) copy-start(bf16[1,128,256]{2,1,0:T(8,128)(2,1)} %param.10) | copy-start | bytes 196612
  36.8 35.7 %copy-start.3 = (f32[512]{0:T(512)S(1)}, f32[512]{0:T(512)}, u32[]{:S(2)}) copy-start(f32[512]{0:T(512)} %param.16) | copy-start | bytes 6148
  108.4 2.0 %copy-start.2 = (bf16[96,512]{1,0:T(8,128)(2,1)S(1)}, bf16[96,512]{1,0:T(8,128)(2,1)}, u32[]{:S(2)}) copy-start(bf16[96,512]{1,0:T(8,128)(2,1)} %param.18) | copy-start | bytes 294916
  110.4 75.1 %all-reduce.2.cloned.1.call-start = ((), (), s32[]{:S(2)}) async-start(), calls=%async_computation.6 | async-start | bytes 196608 | tf_op jit(solution)/shard_map/psum | solution.py:127
Sparse Core Ops, SparseCore 0:
  9.6 30.5 all-gather.4
  41.8 30.6 all-gather.6
  110.5 31.8 reduce-scatter.1
  145.1 40.2 all-reduce.1
where the time goes:
time: 194 us
  waiting for transfers between devices  98.2 us (51%)
  blocking collectives  44.3 us (23%)
  between operations  14 us (7%)
  local copies, waits for them, and re-layouts  10.8 us (6%)
  starting transfers between devices  10.6 us (5%)
  matrix products  8.09 us (4%)
  other arithmetic  7.66 us (4%)
    psum x1, waiting for transfers between devices, shards(): gradient = lax.psum(shard_sum, 'dp').astype(jnp.float32)  42.1 us
    all_gather x1, waiting for transfers between devices, shards(): lax.all_gather(input_weight, 'space', axis=0, tiled=True)  30.3 us
    all_gather x1, blocking collectives, shards(): lax.all_gather(output_weight, 'space', axis=0, tiled=True)  16.3 us
    reduce_scatter x1, waiting for transfers between devices, shards(): lax.psum_scatter(jnp.dot(attended.T, upstream, preferred_element_type=jnp...  14.5 us
    all_gather x1, blocking collectives, shards(): lax.all_gather(short_values, 'space', axis=0, tiled=True)  14 us
    all_gather x1, blocking collectives, shards(): lax.all_gather(short_keys, 'space', axis=0, tiled=True)  14 us
    all_to_all x1, starting transfers between devices, shards(): lax.all_to_all(wanted_rows[0, 0], 'space', split_axis=0, concat_axis=0, t...  6.37 us
    all_to_all x1, waiting for transfers between devices, shards(): lax.all_to_all(answers, 'space', split_axis=0, concat_axis=0, tiled=True)  5.5 us
  transfers between devices with their start and end apart: 6, of which 6 were waited for; matrix products, arithmetic and copies ran while one was open for 8% of the time, Pallas kernels for 0%

commit v1 on v0

--- a/solution.py
+++ b/solution.py
@@ -1,6 +1,10 @@
+import functools
+
 import jax
 import jax.numpy as jnp
 from jax import lax
+from jax.experimental import pallas as pl
+from jax.experimental.pallas import tpu as pltpu
 from jax.sharding import PartitionSpec as P
 
 HEADS = 12
@@ -28,7 +32,7 @@
     )
 
 
-def shards(
+def general_shards(
     voxel_feats,
     neighbours,
     wanted_rows,
@@ -128,6 +132,390 @@
     return (layer, gradient * factor)
 
 
+NEG = -1e30
+F32 = jnp.float32
+BF16 = jnp.bfloat16
+ROWS_CONTRACT = (((0,), (0,)), ((), ()))
+LANES_CONTRACT = (((1,), (1,)), ((), ()))
+
+
+def vmem():
+    return pl.BlockSpec(memory_space=pltpu.VMEM)
+
+
+def smem():
+    return pl.BlockSpec(memory_space=pltpu.SMEM)
+
+
+def call(kernel, scalars, arrays, outs, scratch, name, flops):
+    size = sum(a.size * a.dtype.itemsize for a in list(arrays) + list(outs))
+    return pl.pallas_call(
+        kernel,
+        out_shape=tuple(outs),
+        in_specs=[smem()] + [vmem()] * len(arrays),
+        out_specs=tuple(vmem() for _ in outs),
+        scratch_shapes=scratch,
+        name=name,
+        compiler_params=pltpu.CompilerParams(vmem_limit_bytes=24 * 1024 * 1024),
+        cost_estimate=pl.CostEstimate(flops=flops, bytes_accessed=size, transcendentals=0),
+    )(scalars, *arrays)
+
+
+def pack_kernel(groups, width, scalars, feats, near, misc, weight, *packs):
+    z = scalars[0]
+    rows, cin = feats.shape
+    depth = weight.shape[0]
+    att = weight.shape[1] // 3
+    taps = near.shape[0]
+    tail = 3 * width - 2 * cin
+    high = near[...] // 32
+    low = near[...] - high * 32
+    for pack in packs:
+        pack[0:rows, :] = feats[...]
+        start = rows + 2 * depth + depth * tail // cin
+        info = jnp.concatenate([high, low], axis=1).astype(F32)
+        info = jnp.concatenate([info, misc[...].astype(F32)], axis=0)
+        pack[start : start + taps + 2, :] = info.astype(BF16)
+    for group in range(groups):
+        piece = jnp.concatenate(
+            [weight[:, part * att + group * width : part * att + (group + 1) * width] for part in range(3)],
+            axis=1,
+        )
+        for offset, pack in enumerate(packs):
+
+            @pl.when((z ^ group) == offset)
+            def _(pack=pack, piece=piece):
+                pack[rows : rows + depth, :] = piece[:, 0:cin]
+                pack[rows + depth : rows + 2 * depth, :] = piece[:, cin : 2 * cin]
+                strip = depth * tail // cin
+                for i in range(cin // tail):
+                    pack[rows + 2 * depth : rows + 2 * depth + strip, i * tail : (i + 1) * tail] = piece[
+                        i * strip : (i + 1) * strip, 2 * cin :
+                    ]
+
+
+def taps_kernel(groups, rows, cap, info, scalars, mine, other, out, every, table):
+    z, c = scalars[0], scalars[1]
+    slots = 2 * groups * cap
+    for s in range(groups):
+        every[s * rows : (s + 1) * rows, :] = mine[s, 0:rows, :]
+        every[(groups + s) * rows : (groups + s + 1) * rows, :] = other[s, 0:rows, :]
+    slot = lax.broadcasted_iota(jnp.int32, (1, slots), 1)
+    peer = slot // cap
+    base = (((peer // 2) ^ z) + groups * ((peer & 1) ^ c)) * rows
+    place = lax.broadcasted_iota(jnp.int32, (2 * groups * rows, slots), 0)
+    entry = lax.broadcasted_iota(jnp.int32, (table.shape[0], rows), 0)
+    for s in range(groups):
+        wanted = mine[s, info + 6 : info + 7, 0:slots].astype(F32).astype(jnp.int32) + base
+        pick = jnp.where(place == wanted, 1.0, 0.0).astype(BF16)
+        halo = lax.dot_general(pick, every[...], ROWS_CONTRACT, preferred_element_type=F32)
+        table[0:rows, :] = mine[s, 0:rows, :]
+        table[rows : rows + slots, :] = halo.astype(BF16)
+        table[rows + slots :, :] = jnp.zeros((table.shape[0] - rows - slots, table.shape[1]), BF16)
+        out[0, s * rows : (s + 1) * rows, :] = mine[s, 0:rows, :]
+        for k in range(6):
+            pair = mine[s, info + k : info + k + 1, :].astype(F32).astype(jnp.int32)
+            index = pair[:, 0:rows] * 32 + pair[:, rows : 2 * rows]
+            pick = jnp.where(entry == index, 1.0, 0.0).astype(BF16)
+            row = lax.dot_general(pick, table[...], ROWS_CONTRACT, preferred_element_type=F32)
+            out[k + 1, s * rows : (s + 1) * rows, :] = row.astype(BF16)
+
+
+def conv_kernel(groups, parts, rows, scalars, taps, gain, *refs):
+    z, c, d = scalars[0], scalars[1], scalars[2]
+    own, own_other, near, near_other = refs[0:4]
+    far = refs[4 : 4 + parts - 1]
+    far_other = refs[4 + parts - 1 : 4 + 2 * (parts - 1)]
+    mine, other = refs[4 + 2 * (parts - 1) : 6 + 2 * (parts - 1)]
+    hidden_out, projected_out, summary_out, weight, proj, hidden, normed = refs[6 + 2 * (parts - 1) :]
+    depth = own.shape[1]
+    cut = near.shape[-1]
+    pdepth = proj.shape[0] // (2 * groups)
+    cin = mine.shape[2]
+    width = projected_out.shape[1] // 3
+    tail = 3 * width - 2 * cin
+    strip = pdepth * tail // cin
+
+    def at(row, size):
+        return pl.ds(pl.multiple_of(row, size), size)
+
+    for core, whole, piece, others in ((c, own, near, far), (1 - c, own_other, near_other, far_other)):
+        weight[:, at((2 * z + core) * depth, depth), :] = whole[...]
+        for k in range(1, groups):
+            band = at((2 * (z ^ k) + core) * depth, depth)
+            weight[:, band, at(d * cut, cut)] = piece[k - 1]
+            for m in range(1, parts):
+                weight[:, band, at((d ^ m) * cut, cut)] = others[m - 1][k - 1]
+    for core, pack in ((c, mine), (1 - c, other)):
+        for k in range(groups):
+            first = (2 * (z ^ k) + core) * pdepth
+            band = at(first, pdepth)
+            proj[band, 0:cin] = pack[k, rows : rows + pdepth, :]
+            proj[band, cin : 2 * cin] = pack[k, rows + pdepth : rows + 2 * pdepth, :]
+            for i in range(cin // tail):
+                proj[at(first + i * strip, strip), 2 * cin : 2 * cin + tail] = pack[
+                    k, rows + 2 * pdepth : rows + 2 * pdepth + strip, i * tail : (i + 1) * tail
+                ]
+    count_taps = taps.shape[0]
+    total = jnp.dot(taps[0], weight[0], preferred_element_type=F32)
+    for k in range(1, count_taps):
+        total = total + jnp.dot(taps[k], weight[k], preferred_element_type=F32)
+    hidden[...] = total
+    place = lax.broadcasted_iota(jnp.int32, (rows, 1), 0)
+    for s in range(groups):
+        band = slice(s * rows, (s + 1) * rows)
+        h = jnp.where(place < scalars[3 + s], hidden[band, :], 0.0)
+        if s == 0:
+            hidden_out[...] = h
+        power = jnp.mean(h * h, axis=-1, keepdims=True)
+        normed[band, :] = (h * lax.rsqrt(power + 1e-06) * gain[...]).astype(BF16)
+    projected_out[...] = jnp.dot(
+        normed[...], proj[:, 0 : 3 * width], preferred_element_type=F32
+    ).astype(BF16)
+    blocks = groups * rows // BLK
+    block = lax.broadcasted_iota(jnp.int32, (blocks, groups * rows), 0)
+    token = lax.broadcasted_iota(jnp.int32, (blocks, groups * rows), 1)
+    shard = lax.broadcasted_iota(jnp.int32, (blocks, 1), 0) // (rows // BLK)
+    count = jnp.zeros((blocks, 1), jnp.int32)
+    for s in range(groups):
+        count = jnp.where(shard == s, scalars[3 + s], count)
+    member = (token // BLK == block) & (token - shard * rows < count)
+    member = jnp.where(member, 1.0, 0.0)
+    divisor = jnp.maximum(jnp.sum(member, axis=1, keepdims=True), 1.0)
+    sums = jnp.dot(
+        member.astype(BF16), projected_out[:, width : 3 * width], preferred_element_type=F32
+    )
+    summary_out[...] = (sums / divisor).astype(BF16)
+
+
+def attend_kernel(groups, heads, rows, scalars, projected, mine, other, bias, cotangent, own, own_other, hidden,
+                  *refs):
+    c = scalars[1]
+    base_out, grad_out, send_out = refs[0:3]
+    shares = refs[3 : 3 + groups - 1]
+    attended, outw, grad = refs[3 + groups - 1 :]
+    width = heads * HEAD_DIM
+    half = own.shape[0]
+    outw[pl.ds(pl.multiple_of(c * half, half), half), :] = own[...]
+    outw[pl.ds(pl.multiple_of((1 - c) * half, half), half), :] = own_other[...]
+    short = jnp.concatenate([mine[...].astype(F32), other[...].astype(F32)], axis=0).astype(BF16)
+    scale = HEAD_DIM ** (-0.5)
+    across = lax.broadcasted_iota(jnp.int32, (rows, rows), 1)
+    down = lax.broadcasted_iota(jnp.int32, (rows, rows), 0)
+    same = across // BLK == down // BLK
+    place = lax.broadcasted_iota(jnp.int32, (rows, 1), 0)
+    for s in range(groups):
+        count = scalars[3 + s]
+        band = slice(s * rows, (s + 1) * rows)
+        open_keys = same & (across < count)
+        live = place < count
+        far_bias = jnp.concatenate(
+            [
+                jnp.broadcast_to(bias[s, b : b + 1, :], (BLK, bias.shape[2]))
+                for b in range(rows // BLK)
+            ],
+            axis=0,
+        )
+        for h in range(heads):
+            lane = slice(h * HEAD_DIM, (h + 1) * HEAD_DIM)
+            query = projected[band, lane]
+            key = projected[band, width + h * HEAD_DIM : width + (h + 1) * HEAD_DIM]
+            value = projected[band, 2 * width + h * HEAD_DIM : 2 * width + (h + 1) * HEAD_DIM]
+            near = lax.dot_general(query, key, LANES_CONTRACT, preferred_element_type=F32) * scale
+            near = jnp.where(open_keys, near, NEG)
+            far = lax.dot_general(query, short[:, lane], LANES_CONTRACT, preferred_element_type=F32)
+            far = far * scale + far_bias
+            highest = jnp.maximum(
+                jnp.max(near, axis=-1, keepdims=True), jnp.max(far, axis=-1, keepdims=True)
+            )
+            near = jnp.exp(near - highest)
+            far = jnp.exp(far - highest)
+            total = jnp.sum(near, axis=-1, keepdims=True) + jnp.sum(far, axis=-1, keepdims=True)
+            near = (near / total).astype(BF16)
+            far = (far / total).astype(BF16)
+            mixed = jnp.dot(near, value, preferred_element_type=F32) + jnp.dot(
+                far, short[:, width + h * HEAD_DIM : width + (h + 1) * HEAD_DIM], preferred_element_type=F32
+            )
+            attended[band, lane] = jnp.where(live, mixed, 0.0).astype(BF16)
+    for s in range(groups):
+        share = jnp.dot(attended[s * rows : (s + 1) * rows, :], outw[...], preferred_element_type=F32)
+        if s == 0:
+            base_out[...] = hidden[...] + share
+        else:
+            shares[s - 1][...] = share.astype(BF16)
+    total = lax.dot_general(attended[0:rows, :], cotangent[0], ROWS_CONTRACT, preferred_element_type=F32)
+    for s in range(1, groups):
+        total = total + lax.dot_general(
+            attended[s * rows : (s + 1) * rows, :], cotangent[s], ROWS_CONTRACT, preferred_element_type=F32
+        )
+    grad[...] = total
+    grad_out[...] = grad[pl.ds(pl.multiple_of(c * half, half), half), :]
+    send_out[...] = grad[pl.ds(pl.multiple_of((1 - c) * half, half), half), :].astype(BF16)
+
+
+def paired_shards(
+    voxel_feats,
+    neighbours,
+    wanted_rows,
+    live_counts,
+    block_choice,
+    conv_weight,
+    norm_gain,
+    input_weight,
+    output_weight,
+    cotangent,
+):
+    space = lax.axis_size("space")
+    parts = lax.axis_size("dp")
+    groups = space // 2
+    position = lax.axis_index("space")
+    d = lax.axis_index("dp")
+    z, c = position // 2, position % 2
+    rows, cin = voxel_feats.shape[1:]
+    taps = neighbours.shape[2]
+    cap = wanted_rows.shape[3]
+    depth, out_width = conv_weight.shape[1:]
+    pdepth = input_weight.shape[0]
+    att = input_weight.shape[1] // 3
+    width = att // groups
+    heads = width // HEAD_DIM
+    local_blocks = rows // BLK
+    half = output_weight.shape[0]
+    cut = out_width // parts
+
+    def over_z(x, k):
+        return lax.ppermute(x, "space", [(i, ((i // 2) ^ k) * 2 + i % 2) for i in range(space)])
+
+    def over_core(x):
+        return lax.ppermute(x, "space", [(i, i ^ 1) for i in range(space)])
+
+    def over_dp(x, m):
+        return lax.ppermute(x, "dp", [(i, i ^ m) for i in range(parts)])
+
+    counts = live_counts[0]
+    relative = jnp.arange(groups, dtype=jnp.int32) ^ z
+    scalars = jnp.concatenate(
+        [jnp.stack([z, c, d]).astype(jnp.int32), counts[2 * relative + c], jnp.zeros((1,), jnp.int32)]
+    )
+
+    quarter = lax.dynamic_slice_in_dim(conv_weight, d * cut, cut, axis=2)
+    near = jnp.stack([over_z(quarter, k) for k in range(1, groups)])
+
+    slots = space * cap
+    misc = jnp.zeros((2, cin), jnp.int32)
+    misc = misc.at[0, 0:slots].set(wanted_rows.reshape(slots))
+    misc = misc.at[1, 0 : block_choice.shape[1] * SEL].set(block_choice.reshape(-1))
+    info = rows + 2 * pdepth + pdepth * (3 * width - 2 * cin) // cin
+    pack_rows = -(-(info + taps + 2) // 16) * 16
+    packs = call(
+        functools.partial(pack_kernel, groups, width),
+        scalars,
+        [voxel_feats[0], neighbours[0].T, misc, input_weight],
+        [jax.ShapeDtypeStruct((pack_rows, cin), BF16)] * groups,
+        [],
+        "pack",
+        1000,
+    )
+    mine = jnp.stack([packs[0]] + [over_z(packs[k], k) for k in range(1, groups)])
+
+    own_other = over_core(conv_weight)
+    out_other = over_core(output_weight)
+    far = [over_dp(near, m) for m in range(1, parts)]
+    near_other = over_core(near)
+    other = over_core(mine)
+    cots = jnp.stack([cotangent[0]] + [over_z(cotangent[0], k) for k in range(1, groups)])
+    far_other = [over_core(x) for x in far]
+
+    tokens = groups * rows
+    table_rows = -(-(rows + slots + 1) // 128) * 128
+    (gathered,) = call(
+        functools.partial(taps_kernel, groups, rows, cap, info),
+        scalars,
+        [mine, other],
+        [jax.ShapeDtypeStruct((taps + 1, tokens, cin), BF16)],
+        [pltpu.VMEM((2 * tokens, cin), BF16), pltpu.VMEM((table_rows, cin), BF16)],
+        "taps",
+        2 * taps * tokens * table_rows * cin,
+    )
+    hidden, projected, summary = call(
+        functools.partial(conv_kernel, groups, parts, rows),
+        scalars,
+        [gathered, norm_gain[None, :], conv_weight, own_other, near, near_other, *far, *far_other, mine, other],
+        [
+            jax.ShapeDtypeStruct((rows, out_width), F32),
+            jax.ShapeDtypeStruct((tokens, 3 * width), BF16),
+            jax.ShapeDtypeStruct((groups * local_blocks, 2 * width), BF16),
+        ],
+        [
+            pltpu.VMEM((taps + 1, cin, out_width), BF16),
+            pltpu.VMEM((space * pdepth, -(-3 * width // 128) * 128), BF16),
+            pltpu.VMEM((tokens, out_width), F32),
+            pltpu.VMEM((tokens, out_width), BF16),
+        ],
+        "conv",
+        2 * tokens * out_width * ((taps + 1) * cin + 3 * width),
+    )
+    summary_other = over_core(summary)
+
+    chosen = mine[:, info + taps + 1, 0 : local_blocks * SEL].astype(F32).astype(jnp.int32)
+    chosen = chosen.reshape(groups, local_blocks, SEL)
+    inner = jnp.arange(local_blocks, dtype=jnp.int32)
+    named = jnp.concatenate(
+        [((2 * relative + core)[:, None] * local_blocks + inner[None, :]).reshape(-1) for core in (c, 1 - c)]
+    )
+    bias = jnp.where(jnp.any(chosen[..., None] == named, axis=2), 0.0, NEG).astype(F32)
+
+    outs = call(
+        functools.partial(attend_kernel, groups, heads, rows),
+        scalars,
+        [projected, summary, summary_other, bias, cots, output_weight, out_other, hidden],
+        [
+            jax.ShapeDtypeStruct((rows, out_width), F32),
+            jax.ShapeDtypeStruct((half, out_width), F32),
+            jax.ShapeDtypeStruct((half, out_width), BF16),
+        ]
+        + [jax.ShapeDtypeStruct((rows, out_width), BF16)] * (groups - 1),
+        [
+            pltpu.VMEM((tokens, width), BF16),
+            pltpu.VMEM((2 * half, out_width), BF16),
+            pltpu.VMEM((2 * half, out_width), F32),
+        ],
+        "attend",
+        8 * tokens * width * (rows + out_width),
+    )
+    base, grad, send = outs[0:3]
+    received = [over_z(outs[2 + k], k) for k in range(1, groups)]
+    grad = (grad + over_core(send).astype(F32)).astype(BF16)
+    terms = [grad.astype(F32)] + [over_dp(grad, m).astype(F32) for m in range(1, parts)]
+    while len(terms) > 1:
+        terms = [terms[i] + terms[i + 1] for i in range(0, len(terms), 2)]
+    factor = (parts * space * rows) ** (-0.5)
+    layer = base
+    for x in received:
+        layer = layer + x.astype(F32)
+    return (layer.astype(BF16)[None], terms[0] * factor)
+
+
+def section(mesh, *args):
+    space, parts = mesh.shape["space"], mesh.shape["dp"]
+    groups = space // 2
+    powers = space % 2 == 0 and groups & (groups - 1) == 0 and parts & (parts - 1) == 0
+    cin = args[0].shape[2]
+    width = args[7].shape[1] // 3 // max(groups, 1)
+    tail = 3 * width - 2 * cin
+    fits = (
+        powers
+        and HEADS % max(groups, 1) == 0
+        and args[5].shape[2] % (128 * parts) == 0
+        and 0 < tail <= 128
+        and cin % tail == 0
+        and (args[7].shape[0] * tail) % (16 * cin) == 0
+        and args[0].shape[1] * 2 == cin
+        and space * args[2].shape[3] <= cin
+    )
+    return (paired_shards if fits else general_shards)(*args)
+
+
 def solution(mesh):
     placed = (
         P("dp", "space", None),
@@ -142,7 +530,7 @@
         P("dp", "space", None),
     )
     return jax.shard_map(
-        shards,
+        functools.partial(section, mesh),
         mesh=mesh,
         in_specs=placed,
         out_specs=(P("dp", "space", None), P("space", None)),

time: 194 us -> 78.1 us (0.40)
  waiting for transfers between devices: 98.2 us -> 22.3 us
  blocking collectives: 44.3 us -> 0 us
  starting transfers between devices: 10.6 us -> 32.5 us
  between operations: 14 us -> 0.87 us
  Pallas kernels: 0 us -> 11.6 us
  matrix products: 8.09 us -> 0 us
  local copies, waits for them, and re-layouts: 10.8 us -> 6.71 us
  other arithmetic: 7.66 us -> 3.8 us
    all_gather x3 -> x0, blocking collectives: 44.3 us -> none  [the longest x1 16.3 us: shards(): lax.all_gather(output_weight, 'space', axis=0, tiled=True)]
    psum x1 -> x0, waiting for transfers between devices: 42.1 us -> none  [shards(): gradient = lax.psum(shard_sum, 'dp').astype(jnp.float32)]
    all_gather x2 -> x0, waiting for transfers between devices: 33.6 us -> none  [the longest x1 30.3 us: shards(): lax.all_gather(input_weight, 'space', axis=0, tiled=True)]
    ppermute x0 -> x27, starting transfers between devices: none -> 32.5 us  [the longest x12 19.3 us: over_z(): lax.ppermute(x, 'space', [(i, (i // 2 ^ k) * 2 + i % 2) for i in range(sp...]
    ppermute x0 -> x27, waiting for transfers between devices: none -> 22.3 us  [the longest x12 18 us: over_z(): lax.ppermute(x, 'space', [(i, (i // 2 ^ k) * 2 + i % 2) for i in range(sp...]
    reduce_scatter x1 -> x0, waiting for transfers between devices: 14.5 us -> none  [shards(): lax.psum_scatter(jnp.dot(attended.T, upstream, preferred_element_type=jnp...]
    pallas_call x0 -> x4, Pallas kernels: none -> 11.6 us  [call(): pl.pallas_call(kernel, out_shape=tuple(outs), in_specs=[smem()] + [vmem()...]
    all_to_all x2 -> x0, starting transfers between devices: 10.4 us -> none  [the longest x1 6.37 us: shards(): lax.all_to_all(wanted_rows[0, 0], 'space', split_axis=0, concat_axis=0, t...]
  transfers between devices with their start and end apart: 6 -> 27, of which waited for: 6 -> 8; matrix products, arithmetic and copies ran while one was open for 8% -> 9% of each run, Pallas kernels for 0% -> 8%
where the time goes in v1:
time: 78.1 us; the launch traced here: 77.8 us
  starting transfers between devices  32.5 us (42%)
  waiting for transfers between devices  22.3 us (29%)
  Pallas kernels  11.6 us (15%)
  local copies, waits for them, and re-layouts  6.71 us (9%)
  other arithmetic  3.8 us (5%)
  between operations  0.87 us (1%)
    ppermute x12, starting transfers between devices, over_z(): lax.ppermute(x, 'space', [(i, (i // 2 ^ k) * 2 + i % 2) for i in range(sp...  19.3 us
    ppermute x12, waiting for transfers between devices, over_z(): lax.ppermute(x, 'space', [(i, (i // 2 ^ k) * 2 + i % 2) for i in range(sp...  18 us
    pallas_call x4, Pallas kernels, call(): pl.pallas_call(kernel, out_shape=tuple(outs), in_specs=[smem()] + [vmem()...  11.6 us
    ppermute x6, starting transfers between devices, over_dp(): return lax.ppermute(x, 'dp', [(i, i ^ m) for i in range(parts)])  11.1 us
    ppermute x6, waiting for transfers between devices, over_dp(): return lax.ppermute(x, 'dp', [(i, i ^ m) for i in range(parts)])  3.44 us
    unnamed x15, local copies, waits for them, and re-layouts  2.52 us
    ppermute x9, starting transfers between devices, over_core(): return lax.ppermute(x, 'space', [(i, i ^ 1) for i in range(space)])  2.23 us
  transfers between devices with their start and end apart: 27, of which 8 were waited for; matrix products, arithmetic and copies ran while one was open for 9% of the time, Pallas kernels for 8%

profile of v1, /device:TPU:0, one launch (start us, length us, event | category | flops | bytes accessed | tf_op | source)
XLA Modules:
  0.0 77.8 jit_solution(3300624568817067130)
XLA Ops:
  0.7 0.9 %constant_dynamic-slice_fusion = bf16[7,32,128]{2,1,0:T(8,128)(2,1)S(1)} fusion(bf16[7,32,512]{2,1,0:T(8,128)(2,1)} %refs_0_.1, s32[]{:T(128)S(6)} %select_n.31), kind=kLoop, calls=%fused_computation.23 | loop fusion | bytes 114692 | tf_op jit(solution)/shard_map/dynamic_slice | solution.py:401
  1.6 3.1 %collective-permute-start.5 = (bf16[7,32,128]{2,1,0:T(8,128)(2,1)S(1)}, bf16[7,32,128]{2,1,0:T(8,128)(2,1)S(1)}, u32[]{:S(2)}, u32[]{:S(2)}) collective-permute-start(bf16[7,32,128]{2,1,0:T(8,128)(2,1)S(1)} %constant_dynamic-slice_fusion), channel_id=1, source_target_pairs={{0,2},{1,3},{2,0},{3,1},{4,6},{5,7},{6,4},{7,5},{8,10},{9,11},{10,... | collective-permute-start | bytes 172040 | tf_op jit(solution)/shard_map/ppermute | solution.py:387
  4.6 2.6 %collective-permute-start.6 = (bf16[7,32,128]{2,1,0:T(8,128)(2,1)S(1)}, bf16[7,32,128]{2,1,0:T(8,128)(2,1)S(1)}, u32[]{:S(2)}, u32[]{:S(2)}) collective-permute-start(bf16[7,32,128]{2,1,0:T(8,128)(2,1)S(1)} %constant_dynamic-slice_fusion), channel_id=1, source_target_pairs={{0,4},{1,5},{2,6},{3,7},{4,0},{5,1},{6,2},{7,3},{8,12},{9,13},{10,... | collective-permute-start | bytes 172040 | tf_op jit(solution)/shard_map/ppermute | solution.py:387
  7.2 0.8 reshape.115
  8.0 0.8 reshape.116
  8.8 0.7 copy.14
  9.5 0.6 gather_fusion
  10.1 0.1 scatter.9.misc
  10.2 0.1 concatenate.10.scalars
  10.3 1.0 %copy-done.2 = bf16[64,2304]{1,0:T(8,128)(2,1)S(1)} copy-done((bf16[64,2304]{1,0:T(8,128)(2,1)S(1)}, bf16[64,2304]{1,0:T(8,128)(2,1)}, u32[]{:S(2)}) %copy-start.2) | copy-done | bytes 294936
  11.3 0.8 %copy-done.3 = bf16[1,128,256]{2,1,0:T(8,128)(2,1)S(1)} copy-done((bf16[1,128,256]{2,1,0:T(8,128)(2,1)S(1)}, bf16[1,128,256]{2,1,0:T(8,128)(2,1)}, u32[]{:S(2)}) %copy-start.3) | copy-done | bytes 65560
  12.1 1.1 %pack.1 = (bf16[288,256]{1,0:T(8,128)(2,1)S(1)}, bf16[288,256]{1,0:T(8,128)(2,1)S(1)}, bf16[288,256]{1,0:T(8,128)(2,1)S(1)}, bf16[288,256]{1,0:T(8,128)(2,1)S(1)}) custom-call(s32[8]{0:T(128)S(1)} %concatenate.10.scalars, bf16[128,256]{1,0:T(8,128)(2,1)S(1)} %bitcast.30, s32[6,128]{1,0:T(8,128)S(1)} %bitcast.31, s32[2,256]{1,0:T(2,128)S(1)} %scatter.9.misc, ...), custom_call_target="tpu_custom_call" | custom-call | flops 1000 | bytes 955392 | tf_op jit(solution)/shard_map/pack/pallas_call | solution.py:152
  13.2 0.9 %collective-permute-start = (bf16[288,256]{1,0:T(8,128)(2,1)S(1)}, bf16[288,256]{1,0:T(8,128)(2,1)S(1)}, u32[]{:S(2)}, u32[]{:S(2)}) collective-permute-start(bf16[288,256]{1,0:T(8,128)(2,1)S(1)} %get-tuple-element.40), channel_id=1, source_target_pairs={{0,2},{1,3},{2,0},{3,1},{4,6},{5,7},{6,4},{7,5},{8,10},{9,11},{10,... | collective-permute-start | bytes 442376 | tf_op jit(solution)/shard_map/ppermute | solution.py:387
  14.1 3.5 %collective-permute-start.1 = (bf16[288,256]{1,0:T(8,128)(2,1)S(1)}, bf16[288,256]{1,0:T(8,128)(2,1)S(1)}, u32[]{:S(2)}, u32[]{:S(2)}) collective-permute-start(bf16[288,256]{1,0:T(8,128)(2,1)S(1)} %get-tuple-element.41), channel_id=1, source_target_pairs={{0,4},{1,5},{2,6},{3,7},{4,0},{5,1},{6,2},{7,3},{8,12},{9,13},{10,... | collective-permute-start | bytes 442376 | tf_op jit(solution)/shard_map/ppermute | solution.py:387
  17.7 4.1 %collective-permute-done.2 = bf16[288,256]{1,0:T(8,128)(2,1)S(1)} collective-permute-done((bf16[288,256]{1,0:T(8,128)(2,1)S(1)}, bf16[288,256]{1,0:T(8,128)(2,1)S(1)}, u32[]{:S(2)}, u32[]{:S(2)}) %collective-permute-start.2) | collective-permute-done | bytes 147488 | tf_op jit(solution)/shard_map/ppermute | solution.py:387
  21.7 1.2 %collective-permute-done = bf16[288,256]{1,0:T(8,128)(2,1)S(1)} collective-permute-done((bf16[288,256]{1,0:T(8,128)(2,1)S(1)}, bf16[288,256]{1,0:T(8,128)(2,1)S(1)}, u32[]{:S(2)}, u32[]{:S(2)}) %collective-permute-start) | collective-permute-done | bytes 147488 | tf_op jit(solution)/shard_map/ppermute | solution.py:387
  22.9 3.4 %collective-permute-start.16 = (bf16[128,512]{1,0:T(8,128)(2,1)}, bf16[128,512]{1,0:T(8,128)(2,1)S(1)}, u32[]{:S(2)}, u32[]{:S(2)}) collective-permute-start(bf16[128,512]{1,0:T(8,128)(2,1)} %bitcast.36), channel_id=1, source_target_pairs={{0,2},{1,3},{2,0},{3,1},{4,6},{5,7},{6,4},{7,5},{8,10},{9,11},{10,... | collective-permute-start | bytes 393224 | tf_op jit(solution)/shard_map/ppermute | solution.py:387
  26.3 3.3 %collective-permute-done.1 = bf16[288,256]{1,0:T(8,128)(2,1)S(1)} collective-permute-done((bf16[288,256]{1,0:T(8,128)(2,1)S(1)}, bf16[288,256]{1,0:T(8,128)(2,1)S(1)}, u32[]{:S(2)}, u32[]{:S(2)}) %collective-permute-start.1) | collective-permute-done | bytes 147488 | tf_op jit(solution)/shard_map/ppermute | solution.py:387
  30.0 0.1 add.127
  30.0 0.1 add.121
  30.1 1.3 %collective-permute-start.18 = (bf16[128,512]{1,0:T(8,128)(2,1)S(1)}, bf16[128,512]{1,0:T(8,128)(2,1)S(1)}, u32[]{:S(2)}, u32[]{:S(2)}) collective-permute-start(bf16[128,512]{1,0:T(8,128)(2,1)S(1)} %bitcast.38), channel_id=1, source_target_pairs={{0,6},{1,7},{2,4},{3,5},{4,2},{5,3},{6,0},{7,1},{8,14},{9,15},{10,... | collective-permute-start | bytes 393224 | tf_op jit(solution)/shard_map/ppermute | solution.py:387
  31.5 1.6 %collective-permute-start.9 = (bf16[3,7,32,128]{3,2,1,0:T(8,128)(2,1)S(1)}, bf16[3,7,32,128]{3,2,1,0:T(8,128)(2,1)S(1)}, u32[]{:S(2)}, u32[]{:S(2)}) collective-permute-start(bf16[3,7,32,128]{3,2,1,0:T(8,128)(2,1)S(1)} %pad_maximum_fusion.2.refs_2_), channel_id=1, source_target_pairs={{0,8},{8,0},{16,24},{24,16},{1,9},{9,1},{17,25},{25,17},{2,10},{10... | collective-permute-start | bytes 516104 | tf_op jit(solution)/shard_map/ppermute | solution.py:393
  33.1 1.5 %collective-permute-start.10 = (bf16[3,7,32,128]{3,2,1,0:T(8,128)(2,1)S(1)}, bf16[3,7,32,128]{3,2,1,0:T(8,128)(2,1)S(1)}, u32[]{:S(2)}, u32[]{:S(2)}) collective-permute-start(bf16[3,7,32,128]{3,2,1,0:T(8,128)(2,1)S(1)} %pad_maximum_fusion.2.refs_2_), channel_id=1, source_target_pairs={{0,16},{8,24},{16,0},{24,8},{1,17},{9,25},{17,1},{25,9},{2,18},{10... | collective-permute-start | bytes 516104 | tf_op jit(solution)/shard_map/ppermute | solution.py:393
  34.6 6.3 %collective-permute-done.17 = bf16[128,512]{1,0:T(8,128)(2,1)S(1)} collective-permute-done((bf16[128,512]{1,0:T(8,128)(2,1)S(1)}, bf16[128,512]{1,0:T(8,128)(2,1)S(1)}, u32[]{:S(2)}, u32[]{:S(2)}) %collective-permute-start.17) | collective-permute-done | bytes 131104 | tf_op jit(solution)/shard_map/ppermute | solution.py:387
  40.8 2.4 %collective-permute-start.11 = (bf16[3,7,32,128]{3,2,1,0:T(8,128)(2,1)S(1)}, bf16[3,7,32,128]{3,2,1,0:T(8,128)(2,1)S(1)}, u32[]{:S(2)}, u32[]{:S(2)}) collective-permute-start(bf16[3,7,32,128]{3,2,1,0:T(8,128)(2,1)S(1)} %pad_maximum_fusion.2.refs_2_), channel_id=1, source_target_pairs={{0,24},{8,16},{16,8},{24,0},{1,25},{9,17},{17,9},{25,1},{2,26},{10... | collective-permute-start | bytes 516104 | tf_op jit(solution)/shard_map/ppermute | solution.py:393
  43.3 0.6 pad_add_fusion
  44.0 0.6 collective-permute-start.8
  44.5 0.1 collective-permute-start.12
  44.6 3.4 %collective-permute-done.11.refs_6_ = bf16[3,7,32,128]{3,2,1,0:T(8,128)(2,1)S(1)} collective-permute-done((bf16[3,7,32,128]{3,2,1,0:T(8,128)(2,1)S(1)}, bf16[3,7,32,128]{3,2,1,0:T(8,128)(2,1)S(1)}, u32[]{:S(2)}, u32[]{:S(2)}) %collective-permute-start.11) | collective-permute-done | bytes 172064 | tf_op jit(solution)/shard_map/ppermute | solution.py:393
  48.1 0.5 collective-permute-start.14
  48.6 0.6 fusion.2
  49.2 0.8 convert_element_type.50
  49.9 0.8 %compare_reduce_fusion = pred[4,2,16]{2,1,0:T(4,128)(4,1)S(1)} fusion(s32[16]{0:T(128)} %pad_add_fusion, s32[4,2,4]{2,1,0:T(2,128)S(1)} %convert_element_type.50), kind=kLoop, calls=%fused_computation.8 | loop fusion | flops 896 | bytes 320 | tf_op jit(solution)/shard_map/reduce_or | solution.py:466
  50.7 2.1 %taps.1 = bf16[7,512,256]{2,1,0:T(8,128)(2,1)S(1)} custom-call(s32[8]{0:T(128)S(1)} %concatenate.10.scalars, bf16[4,288,256]{2,1,0:T(8,128)(2,1)S(1)} %pad_maximum_fusion.mine.refs_10_, bf16[4,288,256]{2,1,0:T(8,128)(2,1)S(1)} %collective-permute-done.3.other.refs_11_), custom_call_target="tpu_custom_call" | custom-call | flops 402653184 | bytes 3014656 | tf_op jit(solution)/shard_map/taps/pallas_call | solution.py:152
  53.0 3.0 %conv.1 = (f32[128,512]{1,0:T(8,128)S(1)}, bf16[512,576]{1,0:T(8,128)(2,1)S(1)}, bf16[8,384]{1,0:T(8,128)(2,1)S(1)}) custom-call(s32[8]{0:T(128)S(1)} %concatenate.10.scalars, bf16[7,512,256]{2,1,0:T(8,128)(2,1)S(1)} %taps.1, f32[1,512]{1,0:T(1,128)S(1)} %bitcast.32, bf16[7,32,512]{2,1,0:T(8,128)(2,1)S(1)} %copy-done.1, ...), custom_call_target="tpu_custom_call" | custom-call | flops 1241513984 | bytes 5709824 | tf_op jit(solution)/shard_map/conv/pallas_call | solution.py:152
  55.9 0.5 collective-permute-start.15
  56.5 0.8 %collective-permute-done.15.other = bf16[8,384]{1,0:T(8,128)(2,1)S(1)} collective-permute-done((bf16[8,384]{1,0:T(8,128)(2,1)S(1)}, bf16[8,384]{1,0:T(8,128)(2,1)S(1)}, u32[]{:S(2)}, u32[]{:S(2)}) %collective-permute-start.15) | collective-permute-done | bytes 6176 | tf_op jit(solution)/shard_map/ppermute | solution.py:390
  57.3 5.5 %attend.1 = (f32[128,512]{1,0:T(8,128)S(1)}, f32[96,512]{1,0:T(8,128)S(1)}, bf16[96,512]{1,0:T(8,128)(2,1)S(1)}, bf16[128,512]{1,0:T(8,128)(2,1)S(1)}, bf16[128,...) custom-call(s32[8]{0:T(128)S(1)} %concatenate.10.scalars, bf16[512,576]{1,0:T(8,128)(2,1)S(1)} %get-tuple-element.43.projected, ...), custom_call_target="tpu_custom_call" | custom-call | flops 503316480 | bytes 2535936 | tf_op jit(solution)/shard_map/attend/pallas_call | solution.py:152
  62.7 0.4 collective-permute-start.23
  63.2 3.1 %collective-permute-start.21 = (bf16[128,512]{1,0:T(8,128)(2,1)S(1)}, bf16[128,512]{1,0:T(8,128)(2,1)S(1)}, u32[]{:S(2)}, u32[]{:S(2)}) collective-permute-start(bf16[128,512]{1,0:T(8,128)(2,1)S(1)} %get-tuple-element.48), channel_id=1, source_target_pairs={{0,4},{1,5},{2,6},{3,7},{4,0},{5,1},{6,2},{7,3},{8,12},{9,13},{10,... | collective-permute-start | bytes 393224 | tf_op jit(solution)/shard_map/ppermute | solution.py:387
  66.3 1.2 %collective-permute-start.22 = (bf16[128,512]{1,0:T(8,128)(2,1)S(1)}, bf16[128,512]{1,0:T(8,128)(2,1)S(1)}, u32[]{:S(2)}, u32[]{:S(2)}) collective-permute-start(bf16[128,512]{1,0:T(8,128)(2,1)S(1)} %get-tuple-element.49), channel_id=1, source_target_pairs={{0,6},{1,7},{2,4},{3,5},{4,2},{5,3},{6,0},{7,1},{8,14},{9,15},{10,... | collective-permute-start | bytes 393224 | tf_op jit(solution)/shard_map/ppermute | solution.py:387
  67.6 1.6 %collective-permute-start.24 = (bf16[96,512]{1,0:T(8,128)(2,1)S(1)}, bf16[96,512]{1,0:T(8,128)(2,1)S(1)}, u32[]{:S(2)}, u32[]{:S(2)}) collective-permute-start(bf16[96,512]{1,0:T(8,128)(2,1)S(1)} %add_convert_fusion.1), channel_id=1, source_target_pairs={{0,8},{8,0},{16,24},{24,16},{1,9},{9,1},{17,25},{25,17},{2,10},{10... | collective-permute-start | bytes 294920 | tf_op jit(solution)/shard_map/ppermute | solution.py:393
  69.1 1.5 %collective-permute-start.25 = (bf16[96,512]{1,0:T(8,128)(2,1)S(1)}, bf16[96,512]{1,0:T(8,128)(2,1)S(1)}, u32[]{:S(2)}, u32[]{:S(2)}) collective-permute-start(bf16[96,512]{1,0:T(8,128)(2,1)S(1)} %add_convert_fusion.1), channel_id=1, source_target_pairs={{0,16},{8,24},{16,0},{24,8},{1,17},{9,25},{17,1},{25,9},{2,18},{10... | collective-permute-start | bytes 294920 | tf_op jit(solution)/shard_map/ppermute | solution.py:393
  70.7 0.4 collective-permute-done.20
  71.0 2.4 %collective-permute-start.26 = (bf16[96,512]{1,0:T(8,128)(2,1)S(1)}, bf16[96,512]{1,0:T(8,128)(2,1)S(1)}, u32[]{:S(2)}, u32[]{:S(2)}) collective-permute-start(bf16[96,512]{1,0:T(8,128)(2,1)S(1)} %add_convert_fusion.1), channel_id=1, source_target_pairs={{0,24},{8,16},{16,8},{24,0},{1,25},{9,17},{17,9},{25,1},{2,26},{10... | collective-permute-start | bytes 294920 | tf_op jit(solution)/shard_map/ppermute | solution.py:393
  73.5 2.8 %collective-permute-done.21 = bf16[128,512]{1,0:T(8,128)(2,1)S(1)} collective-permute-done((bf16[128,512]{1,0:T(8,128)(2,1)S(1)}, bf16[128,512]{1,0:T(8,128)(2,1)S(1)}, u32[]{:S(2)}, u32[]{:S(2)}) %collective-permute-start.21) | collective-permute-done | bytes 131104 | tf_op jit(solution)/shard_map/ppermute | solution.py:387
  76.3 0.7 fusion
  77.1 0.7 add_multiply_fusion
  (51 shorter events, 0.7 us)
Async XLA Ops:
  0.6 8.8 %copy-start = (s32[1,8]{1,0:T(1,128)S(1)}, s32[1,8]{1,0:T(1,128)}, u32[]{:S(2)}) copy-start(s32[1,8]{1,0:T(1,128)} %param.17) | copy-start | bytes 100
  0.6 43.2 %copy-start.1 = (bf16[7,32,512]{2,1,0:T(8,128)(2,1)S(1)}, bf16[7,32,512]{2,1,0:T(8,128)(2,1)}, u32[]{:S(2)}) copy-start(bf16[7,32,512]{2,1,0:T(8,128)(2,1)} %refs_0_.1) | copy-start | bytes 688132
  0.7 29.1 %copy-start.6 = (bf16[1,128,512]{2,1,0:T(8,128)(2,1)S(1)}, bf16[1,128,512]{2,1,0:T(8,128)(2,1)}, u32[]{:S(2)}) copy-start(bf16[1,128,512]{2,1,0:T(8,128)(2,1)} %param.23) | copy-start | bytes 393220
  1.6 28.2 %collective-permute-start.5 = (bf16[7,32,128]{2,1,0:T(8,128)(2,1)S(1)}, bf16[7,32,128]{2,1,0:T(8,128)(2,1)S(1)}, u32[]{:S(2)}, u32[]{:S(2)}) collective-permute-start(bf16[7,32,128]{2,1,0:T(8,128)(2,1)S(1)} %constant_dynamic-slice_fusion), channel_id=1, source_target_pairs={{0,2},{1,3},{2,0},{3,1},{4,6},{5,7},{6,4},{7,5},{8,10},{9,11},{10,... | collective-permute-start | bytes 172040 | tf_op jit(solution)/shard_map/ppermute | solution.py:387
  4.6 25.5 %collective-permute-start.6 = (bf16[7,32,128]{2,1,0:T(8,128)(2,1)S(1)}, bf16[7,32,128]{2,1,0:T(8,128)(2,1)S(1)}, u32[]{:S(2)}, u32[]{:S(2)}) collective-permute-start(bf16[7,32,128]{2,1,0:T(8,128)(2,1)S(1)} %constant_dynamic-slice_fusion), channel_id=1, source_target_pairs={{0,4},{1,5},{2,6},{3,7},{4,0},{5,1},{6,2},{7,3},{8,12},{9,13},{10,... | collective-permute-start | bytes 172040 | tf_op jit(solution)/shard_map/ppermute | solution.py:387
  10.3 1.0 %copy-start.2 = (bf16[64,2304]{1,0:T(8,128)(2,1)S(1)}, bf16[64,2304]{1,0:T(8,128)(2,1)}, u32[]{:S(2)}) copy-start(bf16[64,2304]{1,0:T(8,128)(2,1)} %weight.1) | copy-start | bytes 884740
  11.3 0.8 %copy-start.3 = (bf16[1,128,256]{2,1,0:T(8,128)(2,1)S(1)}, bf16[1,128,256]{2,1,0:T(8,128)(2,1)}, u32[]{:S(2)}) copy-start(bf16[1,128,256]{2,1,0:T(8,128)(2,1)} %param.14) | copy-start | bytes 196612
  13.2 8.5 %collective-permute-start.2 = (bf16[288,256]{1,0:T(8,128)(2,1)S(1)}, bf16[288,256]{1,0:T(8,128)(2,1)S(1)}, u32[]{:S(2)}, u32[]{:S(2)}) collective-permute-start(bf16[288,256]{1,0:T(8,128)(2,1)S(1)} %get-tuple-element.42), channel_id=1, source_target_pairs={{0,6},{1,7},{2,4},{3,5},{4,2},{5,3},{6,0},{7,1},{8,14},{9,15},{10,... | collective-permute-start | bytes 442376 | tf_op jit(solution)/shard_map/ppermute | solution.py:387
  13.2 9.7 %collective-permute-start = (bf16[288,256]{1,0:T(8,128)(2,1)S(1)}, bf16[288,256]{1,0:T(8,128)(2,1)S(1)}, u32[]{:S(2)}, u32[]{:S(2)}) collective-permute-start(bf16[288,256]{1,0:T(8,128)(2,1)S(1)} %get-tuple-element.40), channel_id=1, source_target_pairs={{0,2},{1,3},{2,0},{3,1},{4,6},{5,7},{6,4},{7,5},{8,10},{9,11},{10,... | collective-permute-start | bytes 442376 | tf_op jit(solution)/shard_map/ppermute | solution.py:387
  14.1 15.5 %collective-permute-start.1 = (bf16[288,256]{1,0:T(8,128)(2,1)S(1)}, bf16[288,256]{1,0:T(8,128)(2,1)S(1)}, u32[]{:S(2)}, u32[]{:S(2)}) collective-permute-start(bf16[288,256]{1,0:T(8,128)(2,1)S(1)} %get-tuple-element.41), channel_id=1, source_target_pairs={{0,4},{1,5},{2,6},{3,7},{4,0},{5,1},{6,2},{7,3},{8,12},{9,13},{10,... | collective-permute-start | bytes 442376 | tf_op jit(solution)/shard_map/ppermute | solution.py:387
  21.7 9.7 %collective-permute-start.7 = (bf16[7,32,128]{2,1,0:T(8,128)(2,1)S(1)}, bf16[7,32,128]{2,1,0:T(8,128)(2,1)S(1)}, u32[]{:S(2)}, u32[]{:S(2)}) collective-permute-start(bf16[7,32,128]{2,1,0:T(8,128)(2,1)S(1)} %constant_dynamic-slice_fusion), channel_id=1, source_target_pairs={{0,6},{1,7},{2,4},{3,5},{4,2},{5,3},{6,0},{7,1},{8,14},{9,15},{10,... | collective-permute-start | bytes 172040 | tf_op jit(solution)/shard_map/ppermute | solution.py:387
  22.9 10.2 %collective-permute-start.16 = (bf16[128,512]{1,0:T(8,128)(2,1)}, bf16[128,512]{1,0:T(8,128)(2,1)S(1)}, u32[]{:S(2)}, u32[]{:S(2)}) collective-permute-start(bf16[128,512]{1,0:T(8,128)(2,1)} %bitcast.36), channel_id=1, source_target_pairs={{0,2},{1,3},{2,0},{3,1},{4,6},{5,7},{6,4},{7,5},{8,10},{9,11},{10,... | collective-permute-start | bytes 393224 | tf_op jit(solution)/shard_map/ppermute | solution.py:387
  29.7 18.4 %collective-permute-start.3 = (bf16[4,288,256]{2,1,0:T(8,128)(2,1)S(1)}, bf16[4,288,256]{2,1,0:T(8,128)(2,1)S(1)}, u32[]{:S(2)}, u32[]{:S(2)}) collective-permute-start(bf16[4,288,256]{2,1,0:T(8,128)(2,1)S(1)} %pad_maximum_fusion.mine.refs_10_), channel_id=1, source_target_pairs={{0,1},{1,0},{2,3},{3,2},{4,5},{5,4},{6,7},{7,6},{8,9},{9,8},{10,11... | collective-permute-start | bytes 1769480 | tf_op jit(solution)/shard_map/ppermute | solution.py:390
  29.8 11.0 %collective-permute-start.17 = (bf16[128,512]{1,0:T(8,128)(2,1)S(1)}, bf16[128,512]{1,0:T(8,128)(2,1)S(1)}, u32[]{:S(2)}, u32[]{:S(2)}) collective-permute-start(bf16[128,512]{1,0:T(8,128)(2,1)S(1)} %bitcast.37), channel_id=1, source_target_pairs={{0,4},{1,5},{2,6},{3,7},{4,0},{5,1},{6,2},{7,3},{8,12},{9,13},{10,... | collective-permute-start | bytes 393224 | tf_op jit(solution)/shard_map/ppermute | solution.py:387
  30.1 13.8 %collective-permute-start.18 = (bf16[128,512]{1,0:T(8,128)(2,1)S(1)}, bf16[128,512]{1,0:T(8,128)(2,1)S(1)}, u32[]{:S(2)}, u32[]{:S(2)}) collective-permute-start(bf16[128,512]{1,0:T(8,128)(2,1)S(1)} %bitcast.38), channel_id=1, source_target_pairs={{0,6},{1,7},{2,4},{3,5},{4,2},{5,3},{6,0},{7,1},{8,14},{9,15},{10,... | collective-permute-start | bytes 393224 | tf_op jit(solution)/shard_map/ppermute | solution.py:387
  31.5 12.5 %collective-permute-start.9 = (bf16[3,7,32,128]{3,2,1,0:T(8,128)(2,1)S(1)}, bf16[3,7,32,128]{3,2,1,0:T(8,128)(2,1)S(1)}, u32[]{:S(2)}, u32[]{:S(2)}) collective-permute-start(bf16[3,7,32,128]{3,2,1,0:T(8,128)(2,1)S(1)} %pad_maximum_fusion.2.refs_2_), channel_id=1, source_target_pairs={{0,8},{8,0},{16,24},{24,16},{1,9},{9,1},{17,25},{25,17},{2,10},{10... | collective-permute-start | bytes 516104 | tf_op jit(solution)/shard_map/ppermute | solution.py:393
  33.1 11.5 %collective-permute-start.10 = (bf16[3,7,32,128]{3,2,1,0:T(8,128)(2,1)S(1)}, bf16[3,7,32,128]{3,2,1,0:T(8,128)(2,1)S(1)}, u32[]{:S(2)}, u32[]{:S(2)}) collective-permute-start(bf16[3,7,32,128]{3,2,1,0:T(8,128)(2,1)S(1)} %pad_maximum_fusion.2.refs_2_), channel_id=1, source_target_pairs={{0,16},{8,24},{16,0},{24,8},{1,17},{9,25},{17,1},{25,9},{2,18},{10... | collective-permute-start | bytes 516104 | tf_op jit(solution)/shard_map/ppermute | solution.py:393
  40.8 7.2 %collective-permute-start.11 = (bf16[3,7,32,128]{3,2,1,0:T(8,128)(2,1)S(1)}, bf16[3,7,32,128]{3,2,1,0:T(8,128)(2,1)S(1)}, u32[]{:S(2)}, u32[]{:S(2)}) collective-permute-start(bf16[3,7,32,128]{3,2,1,0:T(8,128)(2,1)S(1)} %pad_maximum_fusion.2.refs_2_), channel_id=1, source_target_pairs={{0,24},{8,16},{16,8},{24,0},{1,25},{9,17},{17,9},{25,1},{2,26},{10... | collective-permute-start | bytes 516104 | tf_op jit(solution)/shard_map/ppermute | solution.py:393
  43.9 9.0 %collective-permute-start.4 = (bf16[7,32,512]{2,1,0:T(8,128)(2,1)S(1)}, bf16[7,32,512]{2,1,0:T(8,128)(2,1)S(1)}, u32[]{:S(2)}, u32[]{:S(2)}) collective-permute-start(bf16[7,32,512]{2,1,0:T(8,128)(2,1)S(1)} %copy-done.1), channel_id=1, source_target_pairs={{0,1},{1,0},{2,3},{3,2},{4,5},{5,4},{6,7},{7,6},{8,9},{9,8},{10,11... | collective-permute-start | bytes 688136 | tf_op jit(solution)/shard_map/ppermute | solution.py:390
  43.9 9.1 %copy-start.4 = (f32[512]{0:T(512)S(1)}, f32[512]{0:T(512)}, u32[]{:S(2)}) copy-start(f32[512]{0:T(512)} %param.20) | copy-start | bytes 6148
  44.0 8.8 %collective-permute-start.8 = (bf16[3,7,32,128]{3,2,1,0:T(8,128)(2,1)S(1)}, bf16[3,7,32,128]{3,2,1,0:T(8,128)(2,1)S(1)}, u32[]{:S(2)}, u32[]{:S(2)}) collective-permute-start(bf16[3,7,32,128]{3,2,1,0:T(8,128)(2,1)S(1)} %pad_maximum_fusion.2.refs_2_), channel_id=1, source_target_pairs={{0,1},{1,0},{2,3},{3,2},{4,5},{5,4},{6,7},{7,6},{8,9},{9,8},{10,11... | collective-permute-start | bytes 516104 | tf_op jit(solution)/shard_map/ppermute | solution.py:390
  44.5 8.4 %collective-permute-start.12 = (bf16[3,7,32,128]{3,2,1,0:T(8,128)(2,1)S(1)}, bf16[3,7,32,128]{3,2,1,0:T(8,128)(2,1)S(1)}, u32[]{:S(2)}, u32[]{:S(2)}) collective-permute-start(bf16[3,7,32,128]{3,2,1,0:T(8,128)(2,1)S(1)} %collective-permute-done.9.refs_4_), channel_id=1, source_target_pairs={{0,1},{1,0},{2,3},{3,2},{4,5},{5,4},{6,7},{7,6},{8,9},{9,8},{10,11... | collective-permute-start | bytes 516104 | tf_op jit(solution)/shard_map/ppermute | solution.py:390
  48.1 4.9 %collective-permute-start.13 = (bf16[3,7,32,128]{3,2,1,0:T(8,128)(2,1)S(1)}, bf16[3,7,32,128]{3,2,1,0:T(8,128)(2,1)S(1)}, u32[]{:S(2)}, u32[]{:S(2)}) collective-permute-start(bf16[3,7,32,128]{3,2,1,0:T(8,128)(2,1)S(1)} %collective-permute-done.10.refs_5_), channel_id=1, source_target_pairs={{0,1},{1,0},{2,3},{3,2},{4,5},{5,4},{6,7},{7,6},{8,9},{9,8},{10,11... | collective-permute-start | bytes 516104 | tf_op jit(solution)/shard_map/ppermute | solution.py:390
  48.1 4.9 %collective-permute-start.14 = (bf16[3,7,32,128]{3,2,1,0:T(8,128)(2,1)S(1)}, bf16[3,7,32,128]{3,2,1,0:T(8,128)(2,1)S(1)}, u32[]{:S(2)}, u32[]{:S(2)}) collective-permute-start(bf16[3,7,32,128]{3,2,1,0:T(8,128)(2,1)S(1)} %collective-permute-done.11.refs_6_), channel_id=1, source_target_pairs={{0,1},{1,0},{2,3},{3,2},{4,5},{5,4},{6,7},{7,6},{8,9},{9,8},{10,11... | collective-permute-start | bytes 516104 | tf_op jit(solution)/shard_map/ppermute | solution.py:390
  49.9 2.9 %copy-start.5 = (bf16[96,512]{1,0:T(8,128)(2,1)S(1)}, bf16[96,512]{1,0:T(8,128)(2,1)}, u32[]{:S(2)}) copy-start(bf16[96,512]{1,0:T(8,128)(2,1)} %own.1) | copy-start | bytes 294916
  52.8 3.6 %collective-permute-start.19 = (bf16[96,512]{1,0:T(8,128)(2,1)S(1)}, bf16[96,512]{1,0:T(8,128)(2,1)S(1)}, u32[]{:S(2)}, u32[]{:S(2)}) collective-permute-start(bf16[96,512]{1,0:T(8,128)(2,1)S(1)} %copy-done.5), channel_id=1, source_target_pairs={{0,1},{1,0},{2,3},{3,2},{4,5},{5,4},{6,7},{7,6},{8,9},{9,8},{10,11... | collective-permute-start | bytes 294920 | tf_op jit(solution)/shard_map/ppermute | solution.py:390
  55.9 1.4 %collective-permute-start.15 = (bf16[8,384]{1,0:T(8,128)(2,1)S(1)}, bf16[8,384]{1,0:T(8,128)(2,1)S(1)}, u32[]{:S(2)}, u32[]{:S(2)}) collective-permute-start(bf16[8,384]{1,0:T(8,128)(2,1)S(1)} %get-tuple-element.44.mine), channel_id=1, source_target_pairs={{0,1},{1,0},{2,3},{3,2},{4,5},{5,4},{6,7},{7,6},{8,9},{9,8},{10,11... | collective-permute-start | bytes 18440 | tf_op jit(solution)/shard_map/ppermute | solution.py:390
  62.7 4.8 %collective-permute-start.23 = (bf16[96,512]{1,0:T(8,128)(2,1)S(1)}, bf16[96,512]{1,0:T(8,128)(2,1)S(1)}, u32[]{:S(2)}, u32[]{:S(2)}) collective-permute-start(bf16[96,512]{1,0:T(8,128)(2,1)S(1)} %get-tuple-element.51), channel_id=1, source_target_pairs={{0,1},{1,0},{2,3},{3,2},{4,5},{5,4},{6,7},{7,6},{8,9},{9,8},{10,11... | collective-permute-start | bytes 294920 | tf_op jit(solution)/shard_map/ppermute | solution.py:390
  63.1 7.9 %collective-permute-start.20 = (bf16[128,512]{1,0:T(8,128)(2,1)S(1)}, bf16[128,512]{1,0:T(8,128)(2,1)S(1)}, u32[]{:S(2)}, u32[]{:S(2)}) collective-permute-start(bf16[128,512]{1,0:T(8,128)(2,1)S(1)} %get-tuple-element.47), channel_id=1, source_target_pairs={{0,2},{1,3},{2,0},{3,1},{4,6},{5,7},{6,4},{7,5},{8,10},{9,11},{10,... | collective-permute-start | bytes 393224 | tf_op jit(solution)/shard_map/ppermute | solution.py:387
  63.2 13.2 %collective-permute-start.21 = (bf16[128,512]{1,0:T(8,128)(2,1)S(1)}, bf16[128,512]{1,0:T(8,128)(2,1)S(1)}, u32[]{:S(2)}, u32[]{:S(2)}) collective-permute-start(bf16[128,512]{1,0:T(8,128)(2,1)S(1)} %get-tuple-element.48), channel_id=1, source_target_pairs={{0,4},{1,5},{2,6},{3,7},{4,0},{5,1},{6,2},{7,3},{8,12},{9,13},{10,... | collective-permute-start | bytes 393224 | tf_op jit(solution)/shard_map/ppermute | solution.py:387
  66.3 10.0 %collective-permute-start.22 = (bf16[128,512]{1,0:T(8,128)(2,1)S(1)}, bf16[128,512]{1,0:T(8,128)(2,1)S(1)}, u32[]{:S(2)}, u32[]{:S(2)}) collective-permute-start(bf16[128,512]{1,0:T(8,128)(2,1)S(1)} %get-tuple-element.49), channel_id=1, source_target_pairs={{0,6},{1,7},{2,4},{3,5},{4,2},{5,3},{6,0},{7,1},{8,14},{9,15},{10,... | collective-permute-start | bytes 393224 | tf_op jit(solution)/shard_map/ppermute | solution.py:387
  67.6 9.5 %collective-permute-start.24 = (bf16[96,512]{1,0:T(8,128)(2,1)S(1)}, bf16[96,512]{1,0:T(8,128)(2,1)S(1)}, u32[]{:S(2)}, u32[]{:S(2)}) collective-permute-start(bf16[96,512]{1,0:T(8,128)(2,1)S(1)} %add_convert_fusion.1), channel_id=1, source_target_pairs={{0,8},{8,0},{16,24},{24,16},{1,9},{9,1},{17,25},{25,17},{2,10},{10... | collective-permute-start | bytes 294920 | tf_op jit(solution)/shard_map/ppermute | solution.py:393
  69.1 7.9 %collective-permute-start.25 = (bf16[96,512]{1,0:T(8,128)(2,1)S(1)}, bf16[96,512]{1,0:T(8,128)(2,1)S(1)}, u32[]{:S(2)}, u32[]{:S(2)}) collective-permute-start(bf16[96,512]{1,0:T(8,128)(2,1)S(1)} %add_convert_fusion.1), channel_id=1, source_target_pairs={{0,16},{8,24},{16,0},{24,8},{1,17},{9,25},{17,1},{25,9},{2,18},{10... | collective-permute-start | bytes 294920 | tf_op jit(solution)/shard_map/ppermute | solution.py:393
  71.0 6.0 %collective-permute-start.26 = (bf16[96,512]{1,0:T(8,128)(2,1)S(1)}, bf16[96,512]{1,0:T(8,128)(2,1)S(1)}, u32[]{:S(2)}, u32[]{:S(2)}) collective-permute-start(bf16[96,512]{1,0:T(8,128)(2,1)S(1)} %add_convert_fusion.1), channel_id=1, source_target_pairs={{0,24},{8,16},{16,8},{24,0},{1,25},{9,17},{17,9},{25,1},{2,26},{10... | collective-permute-start | bytes 294920 | tf_op jit(solution)/shard_map/ppermute | solution.py:393

commit v2 on v1

--- a/solution.py
+++ b/solution.py
@@ -6,6 +6,7 @@
 from jax.experimental import pallas as pl
 from jax.experimental.pallas import tpu as pltpu
 from jax.sharding import PartitionSpec as P
+
 
 HEADS = 12
 HEAD_DIM = 64
@@ -147,35 +148,42 @@
     return pl.BlockSpec(memory_space=pltpu.SMEM)
 
 
-def call(kernel, scalars, arrays, outs, scratch, name, flops):
+def call(kernel, scalars, arrays, outs, scratch, flops):
     size = sum(a.size * a.dtype.itemsize for a in list(arrays) + list(outs))
     return pl.pallas_call(
         kernel,
         out_shape=tuple(outs),
-        in_specs=[smem()] + [vmem()] * len(arrays),
+        in_specs=[smem()] * len(scalars) + [vmem()] * len(arrays),
         out_specs=tuple(vmem() for _ in outs),
         scratch_shapes=scratch,
-        name=name,
         compiler_params=pltpu.CompilerParams(vmem_limit_bytes=24 * 1024 * 1024),
         cost_estimate=pl.CostEstimate(flops=flops, bytes_accessed=size, transcendentals=0),
-    )(scalars, *arrays)
-
-
-def pack_kernel(groups, width, scalars, feats, near, misc, weight, *packs):
+    )(*scalars, *arrays)
+
+
+def pack_kernel(groups, width, scalars, feats, near, wanted, chosen, weight, *refs):
+    packs, info = refs[:groups], refs[groups]
     z = scalars[0]
     rows, cin = feats.shape
     depth = weight.shape[0]
     att = weight.shape[1] // 3
     taps = near.shape[0]
     tail = 3 * width - 2 * cin
-    high = near[...] // 32
-    low = near[...] - high * 32
+    strip = depth * tail // cin
+    info[...] = jnp.zeros_like(info)
+    for k in range(taps):
+        high = near[k] // 32
+        info[k : k + 1, 0:rows] = high.astype(F32)
+        info[k : k + 1, rows : 2 * rows] = (near[k] - high * 32).astype(F32)
+    cap = wanted.shape[1]
+    for p in range(wanted.shape[0]):
+        info[taps : taps + 1, p * cap : (p + 1) * cap] = wanted[p : p + 1, :].astype(F32)
+    for b in range(chosen.shape[0]):
+        info[taps + 1 : taps + 2, b * SEL : (b + 1) * SEL] = chosen[b : b + 1, :].astype(F32)
+    start = rows + 2 * depth + strip
     for pack in packs:
         pack[0:rows, :] = feats[...]
-        start = rows + 2 * depth + depth * tail // cin
-        info = jnp.concatenate([high, low], axis=1).astype(F32)
-        info = jnp.concatenate([info, misc[...].astype(F32)], axis=0)
-        pack[start : start + taps + 2, :] = info.astype(BF16)
+        pack[start : start + info.shape[0], :] = info[...].astype(BF16)
     for group in range(groups):
         piece = jnp.concatenate(
             [weight[:, part * att + group * width : part * att + (group + 1) * width] for part in range(3)],
@@ -187,7 +195,6 @@
             def _(pack=pack, piece=piece):
                 pack[rows : rows + depth, :] = piece[:, 0:cin]
                 pack[rows + depth : rows + 2 * depth, :] = piece[:, cin : 2 * cin]
-                strip = depth * tail // cin
                 for i in range(cin // tail):
                     pack[rows + 2 * depth : rows + 2 * depth + strip, i * tail : (i + 1) * tail] = piece[
                         i * strip : (i + 1) * strip, 2 * cin :
@@ -221,8 +228,9 @@
             out[k + 1, s * rows : (s + 1) * rows, :] = row.astype(BF16)
 
 
-def conv_kernel(groups, parts, rows, scalars, taps, gain, *refs):
+def conv_kernel(groups, parts, rows, scalars, counts, taps, gain, *refs):
     z, c, d = scalars[0], scalars[1], scalars[2]
+    live = [counts[0, 2 * (z ^ s) + c] for s in range(groups)]
     own, own_other, near, near_other = refs[0:4]
     far = refs[4 : 4 + parts - 1]
     far_other = refs[4 + parts - 1 : 4 + 2 * (parts - 1)]
@@ -264,7 +272,7 @@
     place = lax.broadcasted_iota(jnp.int32, (rows, 1), 0)
     for s in range(groups):
         band = slice(s * rows, (s + 1) * rows)
-        h = jnp.where(place < scalars[3 + s], hidden[band, :], 0.0)
+        h = jnp.where(place < live[s], hidden[band, :], 0.0)
         if s == 0:
             hidden_out[...] = h
         power = jnp.mean(h * h, axis=-1, keepdims=True)
@@ -278,7 +286,7 @@
     shard = lax.broadcasted_iota(jnp.int32, (blocks, 1), 0) // (rows // BLK)
     count = jnp.zeros((blocks, 1), jnp.int32)
     for s in range(groups):
-        count = jnp.where(shard == s, scalars[3 + s], count)
+        count = jnp.where(shard == s, live[s], count)
     member = (token // BLK == block) & (token - shard * rows < count)
     member = jnp.where(member, 1.0, 0.0)
     divisor = jnp.maximum(jnp.sum(member, axis=1, keepdims=True), 1.0)
@@ -288,9 +296,9 @@
     summary_out[...] = (sums / divisor).astype(BF16)
 
 
-def attend_kernel(groups, heads, rows, scalars, projected, mine, other, bias, cotangent, own, own_other, hidden,
+def attend_kernel(groups, heads, rows, info, scalars, counts, projected, mine, other, packed, cotangent, own, own_other, hidden,
                   *refs):
-    c = scalars[1]
+    z, c = scalars[0], scalars[1]
     base_out, grad_out, send_out = refs[0:3]
     shares = refs[3 : 3 + groups - 1]
     attended, outw, grad = refs[3 + groups - 1 :]
@@ -304,15 +312,27 @@
     down = lax.broadcasted_iota(jnp.int32, (rows, rows), 0)
     same = across // BLK == down // BLK
     place = lax.broadcasted_iota(jnp.int32, (rows, 1), 0)
+    local_blocks = rows // BLK
+    picks = (local_blocks * SEL, 128)
+    diagonal = lax.broadcasted_iota(jnp.int32, picks, 0) == lax.broadcasted_iota(jnp.int32, picks, 1)
+    slot = lax.broadcasted_iota(jnp.int32, (1, short.shape[0]), 1)
+    shard = slot // local_blocks
+    core = jnp.where(shard < groups, c, 1 - c)
+    named = (2 * ((shard % groups) ^ z) + core) * local_blocks + slot % local_blocks
     for s in range(groups):
-        count = scalars[3 + s]
+        count = counts[0, 2 * (z ^ s) + c]
         band = slice(s * rows, (s + 1) * rows)
         open_keys = same & (across < count)
         live = place < count
+        entries = packed[s, info : info + 1, 0:128].astype(F32)
+        entries = jnp.sum(jnp.where(diagonal, entries, 0.0), axis=1, keepdims=True)
+        hits = jnp.where(entries.astype(jnp.int32) == named, 0.0, NEG)
         far_bias = jnp.concatenate(
             [
-                jnp.broadcast_to(bias[s, b : b + 1, :], (BLK, bias.shape[2]))
-                for b in range(rows // BLK)
+                jnp.broadcast_to(
+                    jnp.max(hits[b * SEL : (b + 1) * SEL, :], axis=0, keepdims=True), (BLK, named.shape[1])
+                )
+                for b in range(local_blocks)
             ],
             axis=0,
         )
@@ -374,7 +394,7 @@
     rows, cin = voxel_feats.shape[1:]
     taps = neighbours.shape[2]
     cap = wanted_rows.shape[3]
-    depth, out_width = conv_weight.shape[1:]
+    _, out_width = conv_weight.shape[1:]
     pdepth = input_weight.shape[0]
     att = input_weight.shape[1] // 3
     width = att // groups
@@ -392,28 +412,19 @@
     def over_dp(x, m):
         return lax.ppermute(x, "dp", [(i, i ^ m) for i in range(parts)])
 
-    counts = live_counts[0]
-    relative = jnp.arange(groups, dtype=jnp.int32) ^ z
-    scalars = jnp.concatenate(
-        [jnp.stack([z, c, d]).astype(jnp.int32), counts[2 * relative + c], jnp.zeros((1,), jnp.int32)]
-    )
-
+    where = jnp.stack([z, c, d]).astype(jnp.int32)
     quarter = lax.dynamic_slice_in_dim(conv_weight, d * cut, cut, axis=2)
     near = jnp.stack([over_z(quarter, k) for k in range(1, groups)])
 
     slots = space * cap
-    misc = jnp.zeros((2, cin), jnp.int32)
-    misc = misc.at[0, 0:slots].set(wanted_rows.reshape(slots))
-    misc = misc.at[1, 0 : block_choice.shape[1] * SEL].set(block_choice.reshape(-1))
     info = rows + 2 * pdepth + pdepth * (3 * width - 2 * cin) // cin
-    pack_rows = -(-(info + taps + 2) // 16) * 16
+    info_rows = -(-(taps + 2) // 16) * 16
     packs = call(
         functools.partial(pack_kernel, groups, width),
-        scalars,
-        [voxel_feats[0], neighbours[0].T, misc, input_weight],
-        [jax.ShapeDtypeStruct((pack_rows, cin), BF16)] * groups,
-        [],
-        "pack",
+        [where],
+        [voxel_feats[0], neighbours.transpose(2, 0, 1), wanted_rows[0, 0], block_choice[0], input_weight],
+        [jax.ShapeDtypeStruct((info + info_rows, cin), BF16)] * groups,
+        [pltpu.VMEM((info_rows, cin), F32)],
         1000,
     )
     mine = jnp.stack([packs[0]] + [over_z(packs[k], k) for k in range(1, groups)])
@@ -430,16 +441,15 @@
     table_rows = -(-(rows + slots + 1) // 128) * 128
     (gathered,) = call(
         functools.partial(taps_kernel, groups, rows, cap, info),
-        scalars,
+        [where],
         [mine, other],
         [jax.ShapeDtypeStruct((taps + 1, tokens, cin), BF16)],
         [pltpu.VMEM((2 * tokens, cin), BF16), pltpu.VMEM((table_rows, cin), BF16)],
-        "taps",
         2 * taps * tokens * table_rows * cin,
     )
     hidden, projected, summary = call(
         functools.partial(conv_kernel, groups, parts, rows),
-        scalars,
+        [where, live_counts],
         [gathered, norm_gain[None, :], conv_weight, own_other, near, near_other, *far, *far_other, mine, other],
         [
             jax.ShapeDtypeStruct((rows, out_width), F32),
@@ -452,23 +462,14 @@
             pltpu.VMEM((tokens, out_width), F32),
             pltpu.VMEM((tokens, out_width), BF16),
         ],
-        "conv",
         2 * tokens * out_width * ((taps + 1) * cin + 3 * width),
     )
     summary_other = over_core(summary)
 
-    chosen = mine[:, info + taps + 1, 0 : local_blocks * SEL].astype(F32).astype(jnp.int32)
-    chosen = chosen.reshape(groups, local_blocks, SEL)
-    inner = jnp.arange(local_blocks, dtype=jnp.int32)
-    named = jnp.concatenate(
-        [((2 * relative + core)[:, None] * local_blocks + inner[None, :]).reshape(-1) for core in (c, 1 - c)]
-    )
-    bias = jnp.where(jnp.any(chosen[..., None] == named, axis=2), 0.0, NEG).astype(F32)
-
     outs = call(
-        functools.partial(attend_kernel, groups, heads, rows),
-        scalars,
-        [projected, summary, summary_other, bias, cots, output_weight, out_other, hidden],
+        functools.partial(attend_kernel, groups, heads, rows, info + taps + 1),
+        [where, live_counts],
+        [projected, summary, summary_other, mine, cots, output_weight, out_other, hidden],
         [
             jax.ShapeDtypeStruct((rows, out_width), F32),
             jax.ShapeDtypeStruct((half, out_width), F32),
@@ -480,7 +481,6 @@
             pltpu.VMEM((2 * half, out_width), BF16),
             pltpu.VMEM((2 * half, out_width), F32),
         ],
-        "attend",
         8 * tokens * width * (rows + out_width),
     )
     base, grad, send = outs[0:3]
@@ -513,7 +513,9 @@
         and args[0].shape[1] * 2 == cin
         and space * args[2].shape[3] <= cin
     )
-    return (paired_shards if fits else general_shards)(*args)
+    if not fits:
+        return general_shards(*args)
+    return paired_shards(*args)
 
 
 def solution(mesh):

time: 78.1 us -> 81.2 us (1.040)
  waiting for transfers between devices: 22.3 us -> 34 us
  starting transfers between devices: 32.5 us -> 28 us
  other arithmetic: 3.8 us -> 1.73 us
  local copies, waits for them, and re-layouts: 6.71 us -> 4.74 us
    ppermute x12, waiting for transfers between devices: 18 us -> 26.9 us  [over_z(): lax.ppermute(x, 'space', [(i, (i // 2 ^ k) * 2 + i % 2) for i in range(sp...]
    ppermute x6, starting transfers between devices: 11.1 us -> 7.1 us  [over_dp(): return lax.ppermute(x, 'dp', [(i, i ^ m) for i in range(parts)])]
    ppermute x6, waiting for transfers between devices: 3.44 us -> 6.98 us  [over_dp(): return lax.ppermute(x, 'dp', [(i, i ^ m) for i in range(parts)])]
    another operation x2 -> x0, local copies, waits for them, and re-layouts: 1.53 us -> none
    unnamed x15 -> x20, local copies, waits for them, and re-layouts: 2.52 us -> 3.91 us
    ppermute x9, starting transfers between devices: 2.23 us -> 1.33 us  [over_core(): return lax.ppermute(x, 'space', [(i, i ^ 1) for i in range(space)])]
  transfers between devices with their start and end apart: 27 -> 27, of which waited for: 8 -> 12; matrix products, arithmetic and copies ran while one was open for 9% -> 2% of each run, Pallas kernels for 8% -> 6%
where the time goes in v2:
time: 81.2 us; the launch traced here: 80.9 us
  waiting for transfers between devices  34 us (42%)
  starting transfers between devices  28 us (34%)
  Pallas kernels  11.6 us (14%)
  local copies, waits for them, and re-layouts  4.74 us (6%)
  other arithmetic  1.73 us (2%)
  between operations  0.82 us (1%)
    ppermute x12, waiting for transfers between devices, over_z(): lax.ppermute(x, 'space', [(i, (i // 2 ^ k) * 2 + i % 2) for i in range(sp...  26.9 us
    ppermute x12, starting transfers between devices, over_z(): lax.ppermute(x, 'space', [(i, (i // 2 ^ k) * 2 + i % 2) for i in range(sp...  19.6 us
    pallas_call x4, Pallas kernels, call(): pl.pallas_call(kernel, out_shape=tuple(outs), in_specs=[smem()] * len(sca...  11.6 us
    ppermute x6, starting transfers between devices, over_dp(): return lax.ppermute(x, 'dp', [(i, i ^ m) for i in range(parts)])  7.1 us
    ppermute x6, waiting for transfers between devices, over_dp(): return lax.ppermute(x, 'dp', [(i, i ^ m) for i in range(parts)])  6.98 us
    unnamed x20, local copies, waits for them, and re-layouts  3.91 us
  transfers between devices with their start and end apart: 27, of which 12 were waited for; matrix products, arithmetic and copies ran while one was open for 2% of the time, Pallas kernels for 6%

profile of v2, /device:TPU:0, one launch (start us, length us, event | category | flops | bytes accessed | tf_op | source)
XLA Modules:
  0.0 80.9 jit_solution(13598125064380696451)
XLA Ops:
  0.7 0.1 pad_add_fusion.scalars
  0.7 1.0 %copy-done.1 = bf16[64,2304]{1,0:T(8,128)(2,1)S(1)} copy-done((bf16[64,2304]{1,0:T(8,128)(2,1)S(1)}, bf16[64,2304]{1,0:T(8,128)(2,1)}, u32[]{:S(2)}) %copy-start.1) | copy-done | bytes 294936
  1.7 0.8 %copy-done.3 = bf16[1,128,256]{2,1,0:T(8,128)(2,1)S(1)} copy-done((bf16[1,128,256]{2,1,0:T(8,128)(2,1)S(1)}, bf16[1,128,256]{2,1,0:T(8,128)(2,1)}, u32[]{:S(2)}) %copy-start.3) | copy-done | bytes 65560
  2.6 0.7 copy-done.4
  3.3 0.7 copy-done.5
  3.9 0.7 copy-done.8
  4.6 1.1 %shard_map.113 = (bf16[288,256]{1,0:T(8,128)(2,1)S(1)}, bf16[288,256]{1,0:T(8,128)(2,1)S(1)}, bf16[288,256]{1,0:T(8,128)(2,1)S(1)}, bf16[288,256]{1,0:T(8,128)(2,1)S(1)}) custom-call(s32[3]{0:T(128)S(1)} %pad_add_fusion.scalars, bf16[128,256]{1,0:T(8,128)(2,1)S(1)} %bitcast.22, s32[6,1,128]{2,1,0:T(1,128)S(1)} %bitcast.24, s32[8,8]{1,0:T(8,128)S(1)} %bitcast.23, ...), custom_call_target="tpu_custom_call" | custom-call | flops 1000 | bytes 953632 | tf_op jit(solution)/shard_map/pallas_call | solution.py:153
  5.7 5.2 %collective-permute-start.2 = (bf16[288,256]{1,0:T(8,128)(2,1)S(1)}, bf16[288,256]{1,0:T(8,128)(2,1)S(1)}, u32[]{:S(2)}, u32[]{:S(2)}) collective-permute-start(bf16[288,256]{1,0:T(8,128)(2,1)S(1)} %get-tuple-element.18), channel_id=1, source_target_pairs={{0,6},{1,7},{2,4},{3,5},{4,2},{5,3},{6,0},{7,1},{8,14},{9,15},{10,... | collective-permute-start | bytes 442376 | tf_op jit(solution)/shard_map/ppermute | solution.py:407
  10.9 0.6 collective-permute-start.1
  11.5 4.1 %collective-permute-done.2 = bf16[288,256]{1,0:T(8,128)(2,1)S(1)} collective-permute-done((bf16[288,256]{1,0:T(8,128)(2,1)S(1)}, bf16[288,256]{1,0:T(8,128)(2,1)S(1)}, u32[]{:S(2)}, u32[]{:S(2)}) %collective-permute-start.2) | collective-permute-done | bytes 147488 | tf_op jit(solution)/shard_map/ppermute | solution.py:407
  15.6 3.3 %collective-permute-done = bf16[288,256]{1,0:T(8,128)(2,1)S(1)} collective-permute-done((bf16[288,256]{1,0:T(8,128)(2,1)S(1)}, bf16[288,256]{1,0:T(8,128)(2,1)S(1)}, u32[]{:S(2)}, u32[]{:S(2)}) %collective-permute-start) | collective-permute-done | bytes 147488 | tf_op jit(solution)/shard_map/ppermute | solution.py:407
  18.9 4.4 %collective-permute-done.1 = bf16[288,256]{1,0:T(8,128)(2,1)S(1)} collective-permute-done((bf16[288,256]{1,0:T(8,128)(2,1)S(1)}, bf16[288,256]{1,0:T(8,128)(2,1)S(1)}, u32[]{:S(2)}, u32[]{:S(2)}) %collective-permute-start.1) | collective-permute-done | bytes 147488 | tf_op jit(solution)/shard_map/ppermute | solution.py:407
  23.3 0.1 pad_maximum_fusion.mine.refs_10_.packed
  23.5 0.1 collective-permute-start.3
  23.5 0.8 %constant_dynamic-slice_fusion = bf16[7,32,128]{2,1,0:T(8,128)(2,1)S(1)} fusion(bf16[7,32,512]{2,1,0:T(8,128)(2,1)} %refs_0_.1, s32[]{:T(128)S(6)} %select_n.16), kind=kLoop, calls=%fused_computation.8 | loop fusion | bytes 114692 | tf_op jit(solution)/shard_map/dynamic_slice | solution.py:416
  24.4 3.0 %collective-permute-start.6 = (bf16[7,32,128]{2,1,0:T(8,128)(2,1)S(1)}, bf16[7,32,128]{2,1,0:T(8,128)(2,1)S(1)}, u32[]{:S(2)}, u32[]{:S(2)}) collective-permute-start(bf16[7,32,128]{2,1,0:T(8,128)(2,1)S(1)} %constant_dynamic-slice_fusion), channel_id=1, source_target_pairs={{0,4},{1,5},{2,6},{3,7},{4,0},{5,1},{6,2},{7,3},{8,12},{9,13},{10,... | collective-permute-start | bytes 172040 | tf_op jit(solution)/shard_map/ppermute | solution.py:407
  27.4 1.4 %collective-permute-start.7 = (bf16[7,32,128]{2,1,0:T(8,128)(2,1)S(1)}, bf16[7,32,128]{2,1,0:T(8,128)(2,1)S(1)}, u32[]{:S(2)}, u32[]{:S(2)}) collective-permute-start(bf16[7,32,128]{2,1,0:T(8,128)(2,1)S(1)} %constant_dynamic-slice_fusion), channel_id=1, source_target_pairs={{0,6},{1,7},{2,4},{3,5},{4,2},{5,3},{6,0},{7,1},{8,14},{9,15},{10,... | collective-permute-start | bytes 172040 | tf_op jit(solution)/shard_map/ppermute | solution.py:407
  28.8 1.1 %collective-permute-done.5 = bf16[7,32,128]{2,1,0:T(8,128)(2,1)S(1)} collective-permute-done((bf16[7,32,128]{2,1,0:T(8,128)(2,1)S(1)}, bf16[7,32,128]{2,1,0:T(8,128)(2,1)S(1)}, u32[]{:S(2)}, u32[]{:S(2)}) %collective-permute-start.5) | collective-permute-done | bytes 57376 | tf_op jit(solution)/shard_map/ppermute | solution.py:407
  29.8 1.2 %collective-permute-done.6 = bf16[7,32,128]{2,1,0:T(8,128)(2,1)S(1)} collective-permute-done((bf16[7,32,128]{2,1,0:T(8,128)(2,1)S(1)}, bf16[7,32,128]{2,1,0:T(8,128)(2,1)S(1)}, u32[]{:S(2)}, u32[]{:S(2)}) %collective-permute-start.6) | collective-permute-done | bytes 57376 | tf_op jit(solution)/shard_map/ppermute | solution.py:407
  31.0 2.3 %collective-permute-done.7 = bf16[7,32,128]{2,1,0:T(8,128)(2,1)S(1)} collective-permute-done((bf16[7,32,128]{2,1,0:T(8,128)(2,1)S(1)}, bf16[7,32,128]{2,1,0:T(8,128)(2,1)S(1)}, u32[]{:S(2)}, u32[]{:S(2)}) %collective-permute-start.7) | collective-permute-done | bytes 57376 | tf_op jit(solution)/shard_map/ppermute | solution.py:407
  33.4 1.6 %collective-permute-start.9 = (bf16[3,7,32,128]{3,2,1,0:T(8,128)(2,1)S(1)}, bf16[3,7,32,128]{3,2,1,0:T(8,128)(2,1)S(1)}, u32[]{:S(2)}, u32[]{:S(2)}) collective-permute-start(bf16[3,7,32,128]{3,2,1,0:T(8,128)(2,1)S(1)} %pad_maximum_fusion.2.refs_2_), channel_id=1, source_target_pairs={{0,8},{8,0},{16,24},{24,16},{1,9},{9,1},{17,25},{25,17},{2,10},{10... | collective-permute-start | bytes 516104 | tf_op jit(solution)/shard_map/ppermute | solution.py:413
  34.9 1.5 %collective-permute-start.10 = (bf16[3,7,32,128]{3,2,1,0:T(8,128)(2,1)S(1)}, bf16[3,7,32,128]{3,2,1,0:T(8,128)(2,1)S(1)}, u32[]{:S(2)}, u32[]{:S(2)}) collective-permute-start(bf16[3,7,32,128]{3,2,1,0:T(8,128)(2,1)S(1)} %pad_maximum_fusion.2.refs_2_), channel_id=1, source_target_pairs={{0,16},{8,24},{16,0},{24,8},{1,17},{9,25},{17,1},{25,9},{2,18},{10... | collective-permute-start | bytes 516104 | tf_op jit(solution)/shard_map/ppermute | solution.py:413
  36.4 0.5 collective-permute-start.11
  36.9 3.5 %collective-permute-done.9.refs_4_ = bf16[3,7,32,128]{3,2,1,0:T(8,128)(2,1)S(1)} collective-permute-done((bf16[3,7,32,128]{3,2,1,0:T(8,128)(2,1)S(1)}, bf16[3,7,32,128]{3,2,1,0:T(8,128)(2,1)S(1)}, u32[]{:S(2)}, u32[]{:S(2)}) %collective-permute-start.9) | collective-permute-done | bytes 172064 | tf_op jit(solution)/shard_map/ppermute | solution.py:413
  40.4 3.5 %collective-permute-done.10.refs_5_ = bf16[3,7,32,128]{3,2,1,0:T(8,128)(2,1)S(1)} collective-permute-done((bf16[3,7,32,128]{3,2,1,0:T(8,128)(2,1)S(1)}, bf16[3,7,32,128]{3,2,1,0:T(8,128)(2,1)S(1)}, u32[]{:S(2)}, u32[]{:S(2)}) %collective-permute-start.10) | collective-permute-done | bytes 172064 | tf_op jit(solution)/shard_map/ppermute | solution.py:413
  43.9 0.5 collective-permute-start.13
  44.4 0.1 collective-permute-start.14
  44.5 0.7 collective-permute-start.16
  45.2 0.1 collective-permute-done.12.refs_7_
  45.3 1.8 %collective-permute-start.17 = (bf16[128,512]{1,0:T(8,128)(2,1)S(1)}, bf16[128,512]{1,0:T(8,128)(2,1)S(1)}, u32[]{:S(2)}, u32[]{:S(2)}) collective-permute-start(bf16[128,512]{1,0:T(8,128)(2,1)S(1)} %bitcast.31), channel_id=1, source_target_pairs={{0,4},{1,5},{2,6},{3,7},{4,0},{5,1},{6,2},{7,3},{8,12},{9,13},{10,... | collective-permute-start | bytes 393224 | tf_op jit(solution)/shard_map/ppermute | solution.py:407
  47.1 1.8 %collective-permute-start.18 = (bf16[128,512]{1,0:T(8,128)(2,1)S(1)}, bf16[128,512]{1,0:T(8,128)(2,1)S(1)}, u32[]{:S(2)}, u32[]{:S(2)}) collective-permute-start(bf16[128,512]{1,0:T(8,128)(2,1)S(1)} %bitcast.32), channel_id=1, source_target_pairs={{0,6},{1,7},{2,4},{3,5},{4,2},{5,3},{6,0},{7,1},{8,14},{9,15},{10,... | collective-permute-start | bytes 393224 | tf_op jit(solution)/shard_map/ppermute | solution.py:407
  48.9 2.1 %shard_map.114.taps = bf16[7,512,256]{2,1,0:T(8,128)(2,1)S(1)} custom-call(s32[3]{0:T(128)S(1)} %pad_add_fusion.scalars, bf16[4,288,256]{2,1,0:T(8,128)(2,1)S(1)} %pad_maximum_fusion.mine.refs_10_.packed, bf16[4,288,256]{2,1,0:T(8,128)(2,1)S(1)} %collective-permute-done.3.other.refs_11_), custom_call_target="tpu_custom_call" | custom-call | flops 402653184 | bytes 3014656 | tf_op jit(solution)/shard_map/pallas_call | solution.py:153
  51.0 0.1 collective-permute-start.19
  51.1 3.0 %shard_map.115 = (f32[128,512]{1,0:T(8,128)S(1)}, bf16[512,576]{1,0:T(8,128)(2,1)S(1)}, bf16[8,384]{1,0:T(8,128)(2,1)S(1)}) custom-call(s32[3]{0:T(128)S(1)} %pad_add_fusion.scalars, s32[1,8]{1,0:T(1,128)S(1)} %copy-done.7, bf16[7,512,256]{2,1,0:T(8,128)(2,1)S(1)} %shard_map.114.taps, f32[1,512]{1,0:T(1,128)S(1)} %bitcast.25, ...), custom_call_target="tpu_custom_call" | custom-call | flops 1241513984 | bytes 5709824 | tf_op jit(solution)/shard_map/pallas_call | solution.py:153
  54.1 0.5 collective-permute-start.15
  54.6 3.6 %collective-permute-done.17 = bf16[128,512]{1,0:T(8,128)(2,1)S(1)} collective-permute-done((bf16[128,512]{1,0:T(8,128)(2,1)S(1)}, bf16[128,512]{1,0:T(8,128)(2,1)S(1)}, u32[]{:S(2)}, u32[]{:S(2)}) %collective-permute-start.17) | collective-permute-done | bytes 131104 | tf_op jit(solution)/shard_map/ppermute | solution.py:407
  58.3 5.5 %shard_map.116 = (f32[128,512]{1,0:T(8,128)S(1)}, f32[96,512]{1,0:T(8,128)S(1)}, bf16[96,512]{1,0:T(8,128)(2,1)S(1)}, bf16[128,512]{1,0:T(8,128)(2,1)S(1)}, bf16...) custom-call(s32[3]{0:T(128)S(1)} %pad_add_fusion.scalars, s32[1,8]{1,0:T(1,128)S(1)} %copy-done.7, ...), custom_call_target="tpu_custom_call" | custom-call | flops 503316480 | bytes 3125248 | tf_op jit(solution)/shard_map/pallas_call | solution.py:153
  63.8 0.1 collective-permute-start.23
  63.9 2.6 %collective-permute-start.20 = (bf16[128,512]{1,0:T(8,128)(2,1)S(1)}, bf16[128,512]{1,0:T(8,128)(2,1)S(1)}, u32[]{:S(2)}, u32[]{:S(2)}) collective-permute-start(bf16[128,512]{1,0:T(8,128)(2,1)S(1)} %get-tuple-element.23), channel_id=1, source_target_pairs={{0,2},{1,3},{2,0},{3,1},{4,6},{5,7},{6,4},{7,5},{8,10},{9,11},{10,... | collective-permute-start | bytes 393224 | tf_op jit(solution)/shard_map/ppermute | solution.py:407
  66.5 1.0 %collective-permute-start.21 = (bf16[128,512]{1,0:T(8,128)(2,1)S(1)}, bf16[128,512]{1,0:T(8,128)(2,1)S(1)}, u32[]{:S(2)}, u32[]{:S(2)}) collective-permute-start(bf16[128,512]{1,0:T(8,128)(2,1)S(1)} %get-tuple-element.24), channel_id=1, source_target_pairs={{0,4},{1,5},{2,6},{3,7},{4,0},{5,1},{6,2},{7,3},{8,12},{9,13},{10,... | collective-permute-start | bytes 393224 | tf_op jit(solution)/shard_map/ppermute | solution.py:407
  67.6 1.4 %collective-permute-start.22 = (bf16[128,512]{1,0:T(8,128)(2,1)S(1)}, bf16[128,512]{1,0:T(8,128)(2,1)S(1)}, u32[]{:S(2)}, u32[]{:S(2)}) collective-permute-start(bf16[128,512]{1,0:T(8,128)(2,1)S(1)} %get-tuple-element.25), channel_id=1, source_target_pairs={{0,6},{1,7},{2,4},{3,5},{4,2},{5,3},{6,0},{7,1},{8,14},{9,15},{10,... | collective-permute-start | bytes 393224 | tf_op jit(solution)/shard_map/ppermute | solution.py:407
  69.0 0.9 %collective-permute-start.24 = (bf16[96,512]{1,0:T(8,128)(2,1)S(1)}, bf16[96,512]{1,0:T(8,128)(2,1)S(1)}, u32[]{:S(2)}, u32[]{:S(2)}) collective-permute-start(bf16[96,512]{1,0:T(8,128)(2,1)S(1)} %add_convert_fusion.1), channel_id=1, source_target_pairs={{0,8},{8,0},{16,24},{24,16},{1,9},{9,1},{17,25},{25,17},{2,10},{10... | collective-permute-start | bytes 294920 | tf_op jit(solution)/shard_map/ppermute | solution.py:413
  69.9 1.3 %collective-permute-start.25 = (bf16[96,512]{1,0:T(8,128)(2,1)S(1)}, bf16[96,512]{1,0:T(8,128)(2,1)S(1)}, u32[]{:S(2)}, u32[]{:S(2)}) collective-permute-start(bf16[96,512]{1,0:T(8,128)(2,1)S(1)} %add_convert_fusion.1), channel_id=1, source_target_pairs={{0,16},{8,24},{16,0},{24,8},{1,17},{9,25},{17,1},{25,9},{2,18},{10... | collective-permute-start | bytes 294920 | tf_op jit(solution)/shard_map/ppermute | solution.py:413
  71.1 1.6 %collective-permute-done.20 = bf16[128,512]{1,0:T(8,128)(2,1)S(1)} collective-permute-done((bf16[128,512]{1,0:T(8,128)(2,1)S(1)}, bf16[128,512]{1,0:T(8,128)(2,1)S(1)}, u32[]{:S(2)}, u32[]{:S(2)}) %collective-permute-start.20) | collective-permute-done | bytes 131104 | tf_op jit(solution)/shard_map/ppermute | solution.py:407
  72.8 1.4 %collective-permute-start.26 = (bf16[96,512]{1,0:T(8,128)(2,1)S(1)}, bf16[96,512]{1,0:T(8,128)(2,1)S(1)}, u32[]{:S(2)}, u32[]{:S(2)}) collective-permute-start(bf16[96,512]{1,0:T(8,128)(2,1)S(1)} %add_convert_fusion.1), channel_id=1, source_target_pairs={{0,24},{8,16},{16,8},{24,0},{1,25},{9,17},{17,9},{25,1},{2,26},{10... | collective-permute-start | bytes 294920 | tf_op jit(solution)/shard_map/ppermute | solution.py:413
  74.2 5.3 %collective-permute-done.21 = bf16[128,512]{1,0:T(8,128)(2,1)S(1)} collective-permute-done((bf16[128,512]{1,0:T(8,128)(2,1)S(1)}, bf16[128,512]{1,0:T(8,128)(2,1)S(1)}, u32[]{:S(2)}, u32[]{:S(2)}) %collective-permute-start.21) | collective-permute-done | bytes 131104 | tf_op jit(solution)/shard_map/ppermute | solution.py:407
  79.5 0.7 fusion
  80.2 0.7 add_multiply_fusion
  (38 shorter events, 0.2 us)
Async XLA Ops:
  0.6 39.7 %copy-start = (bf16[7,32,512]{2,1,0:T(8,128)(2,1)S(1)}, bf16[7,32,512]{2,1,0:T(8,128)(2,1)}, u32[]{:S(2)}) copy-start(bf16[7,32,512]{2,1,0:T(8,128)(2,1)} %refs_0_.1) | copy-start | bytes 688132
  0.7 1.0 %copy-start.1 = (bf16[64,2304]{1,0:T(8,128)(2,1)S(1)}, bf16[64,2304]{1,0:T(8,128)(2,1)}, u32[]{:S(2)}) copy-start(bf16[64,2304]{1,0:T(8,128)(2,1)} %weight.1) | copy-start | bytes 884740
  1.7 0.8 %copy-start.3 = (bf16[1,128,256]{2,1,0:T(8,128)(2,1)S(1)}, bf16[1,128,256]{2,1,0:T(8,128)(2,1)}, u32[]{:S(2)}) copy-start(bf16[1,128,256]{2,1,0:T(8,128)(2,1)} %param.10) | copy-start | bytes 196612
  2.6 0.7 copy-start.4
  3.3 0.7 copy-start.5
  3.9 0.7 copy-start.8
  4.6 39.9 %copy-start.9 = (bf16[1,128,512]{2,1,0:T(8,128)(2,1)S(1)}, bf16[1,128,512]{2,1,0:T(8,128)(2,1)}, u32[]{:S(2)}) copy-start(bf16[1,128,512]{2,1,0:T(8,128)(2,1)} %param.19) | copy-start | bytes 393220
  5.7 9.9 %collective-permute-start.2 = (bf16[288,256]{1,0:T(8,128)(2,1)S(1)}, bf16[288,256]{1,0:T(8,128)(2,1)S(1)}, u32[]{:S(2)}, u32[]{:S(2)}) collective-permute-start(bf16[288,256]{1,0:T(8,128)(2,1)S(1)} %get-tuple-element.18), channel_id=1, source_target_pairs={{0,6},{1,7},{2,4},{3,5},{4,2},{5,3},{6,0},{7,1},{8,14},{9,15},{10,... | collective-permute-start | bytes 442376 | tf_op jit(solution)/shard_map/ppermute | solution.py:407
  10.9 8.1 %collective-permute-start = (bf16[288,256]{1,0:T(8,128)(2,1)S(1)}, bf16[288,256]{1,0:T(8,128)(2,1)S(1)}, u32[]{:S(2)}, u32[]{:S(2)}) collective-permute-start(bf16[288,256]{1,0:T(8,128)(2,1)S(1)} %get-tuple-element.16), channel_id=1, source_target_pairs={{0,2},{1,3},{2,0},{3,1},{4,6},{5,7},{6,4},{7,5},{8,10},{9,11},{10,... | collective-permute-start | bytes 442376 | tf_op jit(solution)/shard_map/ppermute | solution.py:407
  10.9 12.5 %collective-permute-start.1 = (bf16[288,256]{1,0:T(8,128)(2,1)S(1)}, bf16[288,256]{1,0:T(8,128)(2,1)S(1)}, u32[]{:S(2)}, u32[]{:S(2)}) collective-permute-start(bf16[288,256]{1,0:T(8,128)(2,1)S(1)} %get-tuple-element.17), channel_id=1, source_target_pairs={{0,4},{1,5},{2,6},{3,7},{4,0},{5,1},{6,2},{7,3},{8,12},{9,13},{10,... | collective-permute-start | bytes 442376 | tf_op jit(solution)/shard_map/ppermute | solution.py:407
  23.4 27.6 %copy-start.2 = (bf16[96,512]{1,0:T(8,128)(2,1)S(1)}, bf16[96,512]{1,0:T(8,128)(2,1)}, u32[]{:S(2)}) copy-start(bf16[96,512]{1,0:T(8,128)(2,1)} %own.1) | copy-start | bytes 294916
  23.4 27.7 %copy-start.6 = (f32[512]{0:T(512)S(1)}, f32[512]{0:T(512)}, u32[]{:S(2)}) copy-start(f32[512]{0:T(512)} %param.16) | copy-start | bytes 6148
  23.4 27.7 %copy-start.7 = (s32[1,8]{1,0:T(1,128)S(1)}, s32[1,8]{1,0:T(1,128)}, u32[]{:S(2)}) copy-start(s32[1,8]{1,0:T(1,128)} %counts.3) | copy-start | bytes 100
  23.5 23.6 %collective-permute-start.3 = (bf16[4,288,256]{2,1,0:T(8,128)(2,1)S(1)}, bf16[4,288,256]{2,1,0:T(8,128)(2,1)S(1)}, u32[]{:S(2)}, u32[]{:S(2)}) collective-permute-start(bf16[4,288,256]{2,1,0:T(8,128)(2,1)S(1)} %pad_maximum_fusion.mine.refs_10_.packed), channel_id=1, source_target_pairs={{0,1},{1,0},{2,3},{3,2},{4,5},{5,4},{6,7},{7,6},{8,9},{9,8},{10,11... | collective-permute-start | bytes 1769480 | tf_op jit(solution)/shard_map/ppermute | solution.py:410
  24.4 5.5 %collective-permute-start.5 = (bf16[7,32,128]{2,1,0:T(8,128)(2,1)S(1)}, bf16[7,32,128]{2,1,0:T(8,128)(2,1)S(1)}, u32[]{:S(2)}, u32[]{:S(2)}) collective-permute-start(bf16[7,32,128]{2,1,0:T(8,128)(2,1)S(1)} %constant_dynamic-slice_fusion), channel_id=1, source_target_pairs={{0,2},{1,3},{2,0},{3,1},{4,6},{5,7},{6,4},{7,5},{8,10},{9,11},{10,... | collective-permute-start | bytes 172040 | tf_op jit(solution)/shard_map/ppermute | solution.py:407
  24.4 6.7 %collective-permute-start.6 = (bf16[7,32,128]{2,1,0:T(8,128)(2,1)S(1)}, bf16[7,32,128]{2,1,0:T(8,128)(2,1)S(1)}, u32[]{:S(2)}, u32[]{:S(2)}) collective-permute-start(bf16[7,32,128]{2,1,0:T(8,128)(2,1)S(1)} %constant_dynamic-slice_fusion), channel_id=1, source_target_pairs={{0,4},{1,5},{2,6},{3,7},{4,0},{5,1},{6,2},{7,3},{8,12},{9,13},{10,... | collective-permute-start | bytes 172040 | tf_op jit(solution)/shard_map/ppermute | solution.py:407
  27.4 6.0 %collective-permute-start.7 = (bf16[7,32,128]{2,1,0:T(8,128)(2,1)S(1)}, bf16[7,32,128]{2,1,0:T(8,128)(2,1)S(1)}, u32[]{:S(2)}, u32[]{:S(2)}) collective-permute-start(bf16[7,32,128]{2,1,0:T(8,128)(2,1)S(1)} %constant_dynamic-slice_fusion), channel_id=1, source_target_pairs={{0,6},{1,7},{2,4},{3,5},{4,2},{5,3},{6,0},{7,1},{8,14},{9,15},{10,... | collective-permute-start | bytes 172040 | tf_op jit(solution)/shard_map/ppermute | solution.py:407
  33.4 7.0 %collective-permute-start.9 = (bf16[3,7,32,128]{3,2,1,0:T(8,128)(2,1)S(1)}, bf16[3,7,32,128]{3,2,1,0:T(8,128)(2,1)S(1)}, u32[]{:S(2)}, u32[]{:S(2)}) collective-permute-start(bf16[3,7,32,128]{3,2,1,0:T(8,128)(2,1)S(1)} %pad_maximum_fusion.2.refs_2_), channel_id=1, source_target_pairs={{0,8},{8,0},{16,24},{24,16},{1,9},{9,1},{17,25},{25,17},{2,10},{10... | collective-permute-start | bytes 516104 | tf_op jit(solution)/shard_map/ppermute | solution.py:413
  34.9 9.0 %collective-permute-start.10 = (bf16[3,7,32,128]{3,2,1,0:T(8,128)(2,1)S(1)}, bf16[3,7,32,128]{3,2,1,0:T(8,128)(2,1)S(1)}, u32[]{:S(2)}, u32[]{:S(2)}) collective-permute-start(bf16[3,7,32,128]{3,2,1,0:T(8,128)(2,1)S(1)} %pad_maximum_fusion.2.refs_2_), channel_id=1, source_target_pairs={{0,16},{8,24},{16,0},{24,8},{1,17},{9,25},{17,1},{25,9},{2,18},{10... | collective-permute-start | bytes 516104 | tf_op jit(solution)/shard_map/ppermute | solution.py:413
  36.4 7.5 %collective-permute-start.11 = (bf16[3,7,32,128]{3,2,1,0:T(8,128)(2,1)S(1)}, bf16[3,7,32,128]{3,2,1,0:T(8,128)(2,1)S(1)}, u32[]{:S(2)}, u32[]{:S(2)}) collective-permute-start(bf16[3,7,32,128]{3,2,1,0:T(8,128)(2,1)S(1)} %pad_maximum_fusion.2.refs_2_), channel_id=1, source_target_pairs={{0,24},{8,16},{16,8},{24,0},{1,25},{9,17},{17,9},{25,1},{2,26},{10... | collective-permute-start | bytes 516104 | tf_op jit(solution)/shard_map/ppermute | solution.py:413
  36.9 7.5 %collective-permute-start.8 = (bf16[3,7,32,128]{3,2,1,0:T(8,128)(2,1)S(1)}, bf16[3,7,32,128]{3,2,1,0:T(8,128)(2,1)S(1)}, u32[]{:S(2)}, u32[]{:S(2)}) collective-permute-start(bf16[3,7,32,128]{3,2,1,0:T(8,128)(2,1)S(1)} %pad_maximum_fusion.2.refs_2_), channel_id=1, source_target_pairs={{0,1},{1,0},{2,3},{3,2},{4,5},{5,4},{6,7},{7,6},{8,9},{9,8},{10,11... | collective-permute-start | bytes 516104 | tf_op jit(solution)/shard_map/ppermute | solution.py:410
  40.4 4.1 %collective-permute-start.4 = (bf16[7,32,512]{2,1,0:T(8,128)(2,1)S(1)}, bf16[7,32,512]{2,1,0:T(8,128)(2,1)S(1)}, u32[]{:S(2)}, u32[]{:S(2)}) collective-permute-start(bf16[7,32,512]{2,1,0:T(8,128)(2,1)S(1)} %copy-done), channel_id=1, source_target_pairs={{0,1},{1,0},{2,3},{3,2},{4,5},{5,4},{6,7},{7,6},{8,9},{9,8},{10,11... | collective-permute-start | bytes 688136 | tf_op jit(solution)/shard_map/ppermute | solution.py:410
  43.9 1.4 %collective-permute-start.12 = (bf16[3,7,32,128]{3,2,1,0:T(8,128)(2,1)S(1)}, bf16[3,7,32,128]{3,2,1,0:T(8,128)(2,1)S(1)}, u32[]{:S(2)}, u32[]{:S(2)}) collective-permute-start(bf16[3,7,32,128]{3,2,1,0:T(8,128)(2,1)S(1)} %collective-permute-done.9.refs_4_), channel_id=1, source_target_pairs={{0,1},{1,0},{2,3},{3,2},{4,5},{5,4},{6,7},{7,6},{8,9},{9,8},{10,11... | collective-permute-start | bytes 516104 | tf_op jit(solution)/shard_map/ppermute | solution.py:410
  43.9 7.1 %collective-permute-start.13 = (bf16[3,7,32,128]{3,2,1,0:T(8,128)(2,1)S(1)}, bf16[3,7,32,128]{3,2,1,0:T(8,128)(2,1)S(1)}, u32[]{:S(2)}, u32[]{:S(2)}) collective-permute-start(bf16[3,7,32,128]{3,2,1,0:T(8,128)(2,1)S(1)} %collective-permute-done.10.refs_5_), channel_id=1, source_target_pairs={{0,1},{1,0},{2,3},{3,2},{4,5},{5,4},{6,7},{7,6},{8,9},{9,8},{10,11... | collective-permute-start | bytes 516104 | tf_op jit(solution)/shard_map/ppermute | solution.py:410
  44.4 6.7 %collective-permute-start.14 = (bf16[3,7,32,128]{3,2,1,0:T(8,128)(2,1)S(1)}, bf16[3,7,32,128]{3,2,1,0:T(8,128)(2,1)S(1)}, u32[]{:S(2)}, u32[]{:S(2)}) collective-permute-start(bf16[3,7,32,128]{3,2,1,0:T(8,128)(2,1)S(1)} %collective-permute-done.11.refs_6_), channel_id=1, source_target_pairs={{0,1},{1,0},{2,3},{3,2},{4,5},{5,4},{6,7},{7,6},{8,9},{9,8},{10,11... | collective-permute-start | bytes 516104 | tf_op jit(solution)/shard_map/ppermute | solution.py:410
  44.5 10.1 %collective-permute-start.16 = (bf16[128,512]{1,0:T(8,128)(2,1)S(1)}, bf16[128,512]{1,0:T(8,128)(2,1)S(1)}, u32[]{:S(2)}, u32[]{:S(2)}) collective-permute-start(bf16[128,512]{1,0:T(8,128)(2,1)S(1)} %bitcast.30), channel_id=1, source_target_pairs={{0,2},{1,3},{2,0},{3,1},{4,6},{5,7},{6,4},{7,5},{8,10},{9,11},{10,... | collective-permute-start | bytes 393224 | tf_op jit(solution)/shard_map/ppermute | solution.py:407
  45.3 12.9 %collective-permute-start.17 = (bf16[128,512]{1,0:T(8,128)(2,1)S(1)}, bf16[128,512]{1,0:T(8,128)(2,1)S(1)}, u32[]{:S(2)}, u32[]{:S(2)}) collective-permute-start(bf16[128,512]{1,0:T(8,128)(2,1)S(1)} %bitcast.31), channel_id=1, source_target_pairs={{0,4},{1,5},{2,6},{3,7},{4,0},{5,1},{6,2},{7,3},{8,12},{9,13},{10,... | collective-permute-start | bytes 393224 | tf_op jit(solution)/shard_map/ppermute | solution.py:407
  47.1 11.1 %collective-permute-start.18 = (bf16[128,512]{1,0:T(8,128)(2,1)S(1)}, bf16[128,512]{1,0:T(8,128)(2,1)S(1)}, u32[]{:S(2)}, u32[]{:S(2)}) collective-permute-start(bf16[128,512]{1,0:T(8,128)(2,1)S(1)} %bitcast.32), channel_id=1, source_target_pairs={{0,6},{1,7},{2,4},{3,5},{4,2},{5,3},{6,0},{7,1},{8,14},{9,15},{10,... | collective-permute-start | bytes 393224 | tf_op jit(solution)/shard_map/ppermute | solution.py:407
  51.0 7.3 %collective-permute-start.19 = (bf16[96,512]{1,0:T(8,128)(2,1)S(1)}, bf16[96,512]{1,0:T(8,128)(2,1)S(1)}, u32[]{:S(2)}, u32[]{:S(2)}) collective-permute-start(bf16[96,512]{1,0:T(8,128)(2,1)S(1)} %copy-done.2), channel_id=1, source_target_pairs={{0,1},{1,0},{2,3},{3,2},{4,5},{5,4},{6,7},{7,6},{8,9},{9,8},{10,11... | collective-permute-start | bytes 294920 | tf_op jit(solution)/shard_map/ppermute | solution.py:410
  54.1 4.2 %collective-permute-start.15 = (bf16[8,384]{1,0:T(8,128)(2,1)S(1)}, bf16[8,384]{1,0:T(8,128)(2,1)S(1)}, u32[]{:S(2)}, u32[]{:S(2)}) collective-permute-start(bf16[8,384]{1,0:T(8,128)(2,1)S(1)} %get-tuple-element.20.mine), channel_id=1, source_target_pairs={{0,1},{1,0},{2,3},{3,2},{4,5},{5,4},{6,7},{7,6},{8,9},{9,8},{10,11... | collective-permute-start | bytes 18440 | tf_op jit(solution)/shard_map/ppermute | solution.py:410
  63.8 5.1 %collective-permute-start.23 = (bf16[96,512]{1,0:T(8,128)(2,1)S(1)}, bf16[96,512]{1,0:T(8,128)(2,1)S(1)}, u32[]{:S(2)}, u32[]{:S(2)}) collective-permute-start(bf16[96,512]{1,0:T(8,128)(2,1)S(1)} %get-tuple-element.27), channel_id=1, source_target_pairs={{0,1},{1,0},{2,3},{3,2},{4,5},{5,4},{6,7},{7,6},{8,9},{9,8},{10,11... | collective-permute-start | bytes 294920 | tf_op jit(solution)/shard_map/ppermute | solution.py:410
  63.9 8.8 %collective-permute-start.20 = (bf16[128,512]{1,0:T(8,128)(2,1)S(1)}, bf16[128,512]{1,0:T(8,128)(2,1)S(1)}, u32[]{:S(2)}, u32[]{:S(2)}) collective-permute-start(bf16[128,512]{1,0:T(8,128)(2,1)S(1)} %get-tuple-element.23), channel_id=1, source_target_pairs={{0,2},{1,3},{2,0},{3,1},{4,6},{5,7},{6,4},{7,5},{8,10},{9,11},{10,... | collective-permute-start | bytes 393224 | tf_op jit(solution)/shard_map/ppermute | solution.py:407
  66.5 12.9 %collective-permute-start.21 = (bf16[128,512]{1,0:T(8,128)(2,1)S(1)}, bf16[128,512]{1,0:T(8,128)(2,1)S(1)}, u32[]{:S(2)}, u32[]{:S(2)}) collective-permute-start(bf16[128,512]{1,0:T(8,128)(2,1)S(1)} %get-tuple-element.24), channel_id=1, source_target_pairs={{0,4},{1,5},{2,6},{3,7},{4,0},{5,1},{6,2},{7,3},{8,12},{9,13},{10,... | collective-permute-start | bytes 393224 | tf_op jit(solution)/shard_map/ppermute | solution.py:407
  67.6 11.9 %collective-permute-start.22 = (bf16[128,512]{1,0:T(8,128)(2,1)S(1)}, bf16[128,512]{1,0:T(8,128)(2,1)S(1)}, u32[]{:S(2)}, u32[]{:S(2)}) collective-permute-start(bf16[128,512]{1,0:T(8,128)(2,1)S(1)} %get-tuple-element.25), channel_id=1, source_target_pairs={{0,6},{1,7},{2,4},{3,5},{4,2},{5,3},{6,0},{7,1},{8,14},{9,15},{10,... | collective-permute-start | bytes 393224 | tf_op jit(solution)/shard_map/ppermute | solution.py:407
  69.0 11.2 %collective-permute-start.24 = (bf16[96,512]{1,0:T(8,128)(2,1)S(1)}, bf16[96,512]{1,0:T(8,128)(2,1)S(1)}, u32[]{:S(2)}, u32[]{:S(2)}) collective-permute-start(bf16[96,512]{1,0:T(8,128)(2,1)S(1)} %add_convert_fusion.1), channel_id=1, source_target_pairs={{0,8},{8,0},{16,24},{24,16},{1,9},{9,1},{17,25},{25,17},{2,10},{10... | collective-permute-start | bytes 294920 | tf_op jit(solution)/shard_map/ppermute | solution.py:413
  69.9 10.3 %collective-permute-start.25 = (bf16[96,512]{1,0:T(8,128)(2,1)S(1)}, bf16[96,512]{1,0:T(8,128)(2,1)S(1)}, u32[]{:S(2)}, u32[]{:S(2)}) collective-permute-start(bf16[96,512]{1,0:T(8,128)(2,1)S(1)} %add_convert_fusion.1), channel_id=1, source_target_pairs={{0,16},{8,24},{16,0},{24,8},{1,17},{9,25},{17,1},{25,9},{2,18},{10... | collective-permute-start | bytes 294920 | tf_op jit(solution)/shard_map/ppermute | solution.py:413
  72.8 7.5 %collective-permute-start.26 = (bf16[96,512]{1,0:T(8,128)(2,1)S(1)}, bf16[96,512]{1,0:T(8,128)(2,1)S(1)}, u32[]{:S(2)}, u32[]{:S(2)}) collective-permute-start(bf16[96,512]{1,0:T(8,128)(2,1)S(1)} %add_convert_fusion.1), channel_id=1, source_target_pairs={{0,24},{8,16},{16,8},{24,0},{1,25},{9,17},{17,9},{25,1},{2,26},{10... | collective-permute-start | bytes 294920 | tf_op jit(solution)/shard_map/ppermute | solution.py:413

commit v3 on v2

--- a/solution.py
+++ b/solution.py
@@ -135,11 +135,17 @@
 
 NEG = -1e30
 F32 = jnp.float32
+PACK_LIMIT = 24000000
 BF16 = jnp.bfloat16
 ROWS_CONTRACT = (((0,), (0,)), ((), ()))
 LANES_CONTRACT = (((1,), (1,)), ((), ()))
 
 
+def spot():
+    position = lax.axis_index("space")
+    return position // 2, position % 2, lax.axis_index("dp")
+
+
 def vmem():
     return pl.BlockSpec(memory_space=pltpu.VMEM)
 
@@ -148,61 +154,86 @@
     return pl.BlockSpec(memory_space=pltpu.SMEM)
 
 
-def call(kernel, scalars, arrays, outs, scratch, flops):
+def call(kernel, scalars, arrays, outs, scratch, flops, space=pltpu.VMEM, limit=24 * 2**20):
     size = sum(a.size * a.dtype.itemsize for a in list(arrays) + list(outs))
     return pl.pallas_call(
         kernel,
         out_shape=tuple(outs),
-        in_specs=[smem()] * len(scalars) + [vmem()] * len(arrays),
+        in_specs=[smem()] * len(scalars) + [pl.BlockSpec(memory_space=space)] * len(arrays),
         out_specs=tuple(vmem() for _ in outs),
         scratch_shapes=scratch,
-        compiler_params=pltpu.CompilerParams(vmem_limit_bytes=24 * 1024 * 1024),
+        compiler_params=pltpu.CompilerParams(vmem_limit_bytes=limit),
         cost_estimate=pl.CostEstimate(flops=flops, bytes_accessed=size, transcendentals=0),
-    )(*scalars, *arrays)
-
-
-def pack_kernel(groups, width, scalars, feats, near, wanted, chosen, weight, *refs):
-    packs, info = refs[:groups], refs[groups]
-    z = scalars[0]
-    rows, cin = feats.shape
+    )(*scalars, *([pltpu.with_memory_space_constraint(x, space) for x in arrays] if space == pltpu.HBM else arrays))
+
+
+def pack_kernel(groups, width, rows, feats_in, near_in, wanted_in, chosen_in, weight_in, conv_in, *refs):
+    voxels, own, beside = refs[0:3]
+    quarters = refs[3 : groups + 1]
+    near, wanted, chosen, weight, conv, pieces, info, sems = refs[groups + 1 :]
+    z, _, d = spot()
+    copies = [
+        pltpu.make_async_copy(source, target, sems.at[i])
+        for i, (source, target) in enumerate(
+            (
+                (weight_in, weight),
+                (conv_in, conv),
+                (feats_in, voxels.at[pl.ds(0, rows)]),
+                (near_in, near),
+                (wanted_in, wanted),
+                (chosen_in, chosen),
+            )
+        )
+    ]
+    for copy in copies:
+        copy.start()
+    info[...] = jnp.zeros_like(info)
+    copies[0].wait()
     depth = weight.shape[0]
     att = weight.shape[1] // 3
-    taps = near.shape[0]
-    tail = 3 * width - 2 * cin
-    strip = depth * tail // cin
-    info[...] = jnp.zeros_like(info)
+    taps, cdepth, out_width = conv.shape
+    cut = quarters[0].shape[1]
+    strip = depth * cut // out_width
+    tail = 3 * width - out_width
+    blank = jnp.zeros((depth, cut - tail), BF16)
+    for group in range(groups):
+        parts = [weight[:, p * att + group * width : p * att + (group + 1) * width] for p in range(3)]
+        piece = jnp.concatenate(parts + [blank], axis=1)
+        pieces[z ^ group, 0:depth, :] = piece[:, 0:out_width]
+        for i in range(depth // strip):
+            pieces[z ^ group, depth : depth + strip, i * cut : (i + 1) * cut] = piece[
+                i * strip : (i + 1) * strip, out_width:
+            ]
+    lanes = pl.ds(pl.multiple_of(d * cut, cut), cut)
+    copies[1].wait()
     for k in range(taps):
+        band = slice(k * cdepth, (k + 1) * cdepth)
+        own[band, :] = conv[k]
+        beside[band, :] = conv[k]
+        mine = conv[k, :, lanes]
+        for quarter in quarters:
+            quarter[band, :] = mine
+    own[taps * cdepth :, :] = pieces[0]
+    beside[taps * cdepth :, :] = pieces[1]
+    for i, quarter in enumerate(quarters):
+        quarter[taps * cdepth :, :] = pieces[2 + i, :, lanes]
+    for copy in copies[2:]:
+        copy.wait()
+    for k in range(near.shape[0]):
         high = near[k] // 32
         info[k : k + 1, 0:rows] = high.astype(F32)
         info[k : k + 1, rows : 2 * rows] = (near[k] - high * 32).astype(F32)
+    count = near.shape[0]
     cap = wanted.shape[1]
     for p in range(wanted.shape[0]):
-        info[taps : taps + 1, p * cap : (p + 1) * cap] = wanted[p : p + 1, :].astype(F32)
+        info[count : count + 1, p * cap : (p + 1) * cap] = wanted[p : p + 1, :].astype(F32)
     for b in range(chosen.shape[0]):
-        info[taps + 1 : taps + 2, b * SEL : (b + 1) * SEL] = chosen[b : b + 1, :].astype(F32)
-    start = rows + 2 * depth + strip
-    for pack in packs:
-        pack[0:rows, :] = feats[...]
-        pack[start : start + info.shape[0], :] = info[...].astype(BF16)
-    for group in range(groups):
-        piece = jnp.concatenate(
-            [weight[:, part * att + group * width : part * att + (group + 1) * width] for part in range(3)],
-            axis=1,
-        )
-        for offset, pack in enumerate(packs):
-
-            @pl.when((z ^ group) == offset)
-            def _(pack=pack, piece=piece):
-                pack[rows : rows + depth, :] = piece[:, 0:cin]
-                pack[rows + depth : rows + 2 * depth, :] = piece[:, cin : 2 * cin]
-                for i in range(cin // tail):
-                    pack[rows + 2 * depth : rows + 2 * depth + strip, i * tail : (i + 1) * tail] = piece[
-                        i * strip : (i + 1) * strip, 2 * cin :
-                    ]
-
-
-def taps_kernel(groups, rows, cap, info, scalars, mine, other, out, every, table):
-    z, c = scalars[0], scalars[1]
+        info[count + 1 : count + 2, b * SEL : (b + 1) * SEL] = chosen[b : b + 1, :].astype(F32)
+    voxels[rows:, :] = info[...].astype(BF16)
+
+
+def taps_kernel(groups, rows, cap, info, mine, other, out, every, table):
+    z, c, _ = spot()
     slots = 2 * groups * cap
     for s in range(groups):
         every[s * rows : (s + 1) * rows, :] = mine[s, 0:rows, :]
@@ -228,43 +259,46 @@
             out[k + 1, s * rows : (s + 1) * rows, :] = row.astype(BF16)
 
 
-def conv_kernel(groups, parts, rows, scalars, counts, taps, gain, *refs):
-    z, c, d = scalars[0], scalars[1], scalars[2]
+def conv_kernel(groups, parts, rows, counts, taps, gain, *refs):
+    z, c, d = spot()
     live = [counts[0, 2 * (z ^ s) + c] for s in range(groups)]
-    own, own_other, near, near_other = refs[0:4]
-    far = refs[4 : 4 + parts - 1]
-    far_other = refs[4 + parts - 1 : 4 + 2 * (parts - 1)]
-    mine, other = refs[4 + 2 * (parts - 1) : 6 + 2 * (parts - 1)]
-    hidden_out, projected_out, summary_out, weight, proj, hidden, normed = refs[6 + 2 * (parts - 1) :]
-    depth = own.shape[1]
-    cut = near.shape[-1]
+    own, beside, near, far, own_other, beside_other, near_other, far_other = refs[0:8]
+    hidden_out, projected_out, summary_out, weight, proj, hidden, normed = refs[8:]
+    count_taps, _, out_width = weight.shape
+    depth = weight.shape[1] // (2 * groups)
     pdepth = proj.shape[0] // (2 * groups)
-    cin = mine.shape[2]
+    cut = near.shape[2]
+    strip = pdepth * cut // out_width
     width = projected_out.shape[1] // 3
-    tail = 3 * width - 2 * cin
-    strip = pdepth * tail // cin
+    middle = count_taps * depth
 
     def at(row, size):
         return pl.ds(pl.multiple_of(row, size), size)
 
-    for core, whole, piece, others in ((c, own, near, far), (1 - c, own_other, near_other, far_other)):
-        weight[:, at((2 * z + core) * depth, depth), :] = whole[...]
-        for k in range(1, groups):
-            band = at((2 * (z ^ k) + core) * depth, depth)
-            weight[:, band, at(d * cut, cut)] = piece[k - 1]
+    def whole(piece, shard):
+        for k in range(count_taps):
+            weight[k, at(shard * depth, depth), :] = piece[k * depth : (k + 1) * depth, :]
+        proj[at(shard * pdepth, pdepth), 0:out_width] = piece[middle : middle + pdepth, :]
+        for i in range(parts):
+            proj[at(shard * pdepth + i * strip, strip), out_width : out_width + cut] = piece[
+                middle + pdepth :, i * cut : (i + 1) * cut
+            ]
+
+    def quarter(piece, shard, i):
+        lanes = at(i * cut, cut)
+        for k in range(count_taps):
+            weight[k, at(shard * depth, depth), lanes] = piece[k * depth : (k + 1) * depth, :]
+        proj[at(shard * pdepth, pdepth), lanes] = piece[middle : middle + pdepth, :]
+        proj[at(shard * pdepth + i * strip, strip), out_width : out_width + cut] = piece[middle + pdepth :, :]
+
+    for core, mine in ((c, (own, beside, near, far)), (1 - c, (own_other, beside_other, near_other, far_other))):
+        whole(mine[0], 2 * z + core)
+        whole(mine[1], 2 * (z ^ 1) + core)
+        for k in range(2, groups):
+            shard = 2 * (z ^ k) + core
+            quarter(mine[2].at[k - 2], shard, d)
             for m in range(1, parts):
-                weight[:, band, at((d ^ m) * cut, cut)] = others[m - 1][k - 1]
-    for core, pack in ((c, mine), (1 - c, other)):
-        for k in range(groups):
-            first = (2 * (z ^ k) + core) * pdepth
-            band = at(first, pdepth)
-            proj[band, 0:cin] = pack[k, rows : rows + pdepth, :]
-            proj[band, cin : 2 * cin] = pack[k, rows + pdepth : rows + 2 * pdepth, :]
-            for i in range(cin // tail):
-                proj[at(first + i * strip, strip), 2 * cin : 2 * cin + tail] = pack[
-                    k, rows + 2 * pdepth : rows + 2 * pdepth + strip, i * tail : (i + 1) * tail
-                ]
-    count_taps = taps.shape[0]
+                quarter(mine[3].at[m - 1, k - 2], shard, d ^ m)
     total = jnp.dot(taps[0], weight[0], preferred_element_type=F32)
     for k in range(1, count_taps):
         total = total + jnp.dot(taps[k], weight[k], preferred_element_type=F32)
@@ -296,17 +330,14 @@
     summary_out[...] = (sums / divisor).astype(BF16)
 
 
-def attend_kernel(groups, heads, rows, info, scalars, counts, projected, mine, other, packed, cotangent, own, own_other, hidden,
-                  *refs):
-    z, c = scalars[0], scalars[1]
-    base_out, grad_out, send_out = refs[0:3]
-    shares = refs[3 : 3 + groups - 1]
-    attended, outw, grad = refs[3 + groups - 1 :]
+def attend_kernel(groups, heads, rows, shards, info, counts, projected, mine, other, packed, attended,
+                  keep, near_s, far_s, value_s, far_value_s):
+    z, c, _ = spot()
     width = heads * HEAD_DIM
-    half = own.shape[0]
-    outw[pl.ds(pl.multiple_of(c * half, half), half), :] = own[...]
-    outw[pl.ds(pl.multiple_of((1 - c) * half, half), half), :] = own_other[...]
-    short = jnp.concatenate([mine[...].astype(F32), other[...].astype(F32)], axis=0).astype(BF16)
+    short = jnp.concatenate([mine[...].astype(F32), other[...].astype(F32)], axis=0)
+    slots = short.shape[0]
+    keep[...] = jnp.zeros_like(keep)
+    keep[0:slots, :] = short.astype(BF16)
     scale = HEAD_DIM ** (-0.5)
     across = lax.broadcasted_iota(jnp.int32, (rows, rows), 1)
     down = lax.broadcasted_iota(jnp.int32, (rows, rows), 0)
@@ -315,15 +346,14 @@
     local_blocks = rows // BLK
     picks = (local_blocks * SEL, 128)
     diagonal = lax.broadcasted_iota(jnp.int32, picks, 0) == lax.broadcasted_iota(jnp.int32, picks, 1)
-    slot = lax.broadcasted_iota(jnp.int32, (1, short.shape[0]), 1)
+    slot = lax.broadcasted_iota(jnp.int32, (1, keep.shape[0]), 1)
     shard = slot // local_blocks
     core = jnp.where(shard < groups, c, 1 - c)
     named = (2 * ((shard % groups) ^ z) + core) * local_blocks + slot % local_blocks
-    for s in range(groups):
-        count = counts[0, 2 * (z ^ s) + c]
+    named = jnp.where(slot < slots, named, -1)
+    for n, s in enumerate(shards):
         band = slice(s * rows, (s + 1) * rows)
-        open_keys = same & (across < count)
-        live = place < count
+        open_keys = same & (across < counts[0, 2 * (z ^ s) + c])
         entries = packed[s, info : info + 1, 0:128].astype(F32)
         entries = jnp.sum(jnp.where(diagonal, entries, 0.0), axis=1, keepdims=True)
         hits = jnp.where(entries.astype(jnp.int32) == named, 0.0, NEG)
@@ -340,37 +370,91 @@
             lane = slice(h * HEAD_DIM, (h + 1) * HEAD_DIM)
             query = projected[band, lane]
             key = projected[band, width + h * HEAD_DIM : width + (h + 1) * HEAD_DIM]
+            near = lax.dot_general(query, key, LANES_CONTRACT, preferred_element_type=F32) * scale
+            near_s[n * heads + h] = jnp.where(open_keys, near, NEG)
+            far = lax.dot_general(query, keep[:, lane], LANES_CONTRACT, preferred_element_type=F32)
+            far_s[n * heads + h] = far * scale + far_bias
+    near = near_s[...]
+    far = far_s[...]
+    highest = jnp.max(jnp.maximum(near, far), axis=-1, keepdims=True)
+    near = jnp.exp(near - highest)
+    far = jnp.exp(far - highest)
+    share = 1.0 / jnp.sum(near + far, axis=-1, keepdims=True)
+    value_s[...] = (near * share).astype(BF16)
+    far_value_s[...] = (far * share).astype(BF16)
+    for n, s in enumerate(shards):
+        band = slice(s * rows, (s + 1) * rows)
+        live = place < counts[0, 2 * (z ^ s) + c]
+        for h in range(heads):
             value = projected[band, 2 * width + h * HEAD_DIM : 2 * width + (h + 1) * HEAD_DIM]
-            near = lax.dot_general(query, key, LANES_CONTRACT, preferred_element_type=F32) * scale
-            near = jnp.where(open_keys, near, NEG)
-            far = lax.dot_general(query, short[:, lane], LANES_CONTRACT, preferred_element_type=F32)
-            far = far * scale + far_bias
-            highest = jnp.maximum(
-                jnp.max(near, axis=-1, keepdims=True), jnp.max(far, axis=-1, keepdims=True)
+            far_value = keep[:, width + h * HEAD_DIM : width + (h + 1) * HEAD_DIM]
+            mixed = jnp.dot(value_s[n * heads + h], value, preferred_element_type=F32) + jnp.dot(
+                far_value_s[n * heads + h], far_value, preferred_element_type=F32
             )
-            near = jnp.exp(near - highest)
-            far = jnp.exp(far - highest)
-            total = jnp.sum(near, axis=-1, keepdims=True) + jnp.sum(far, axis=-1, keepdims=True)
-            near = (near / total).astype(BF16)
-            far = (far / total).astype(BF16)
-            mixed = jnp.dot(near, value, preferred_element_type=F32) + jnp.dot(
-                far, short[:, width + h * HEAD_DIM : width + (h + 1) * HEAD_DIM], preferred_element_type=F32
-            )
-            attended[band, lane] = jnp.where(live, mixed, 0.0).astype(BF16)
-    for s in range(groups):
-        share = jnp.dot(attended[s * rows : (s + 1) * rows, :], outw[...], preferred_element_type=F32)
-        if s == 0:
+            attended[n * rows : (n + 1) * rows, h * HEAD_DIM : (h + 1) * HEAD_DIM] = jnp.where(
+                live, mixed, 0.0
+            ).astype(BF16)
+
+
+def outer_weights(c, own, own_other, outw):
+    half = own.shape[0]
+    outw[pl.ds(pl.multiple_of(c * half, half), half), :] = own[...]
+    outw[pl.ds(pl.multiple_of((1 - c) * half, half), half), :] = own_other[...]
+
+
+def first_kernel(groups, heads, rows, info, counts, projected, mine, other, packed, own, own_other, *refs):
+    shards = range(groups // 2, groups)
+    shares, attended = refs[: len(shards)], refs[len(shards)]
+    outw, scratch = refs[len(shards) + 1], refs[len(shards) + 2 :]
+    outer_weights(spot()[1], own, own_other, outw)
+    attend_kernel(groups, heads, rows, shards, info, counts, projected, mine, other, packed, attended,
+                  *scratch)
+    for n in range(len(shards)):
+        share = jnp.dot(attended[n * rows : (n + 1) * rows, :], outw[...], preferred_element_type=F32)
+        shares[n][...] = share.astype(BF16)
+
+
+def second_kernel(groups, heads, rows, info, counts, projected, mine, other, packed, own, own_other,
+                  early, hidden, *refs):
+    shards = range(groups // 2)
+    cotangent, refs = refs[:groups], refs[groups:]
+    base_out, grad_out, send_out = refs[0:3]
+    shares = refs[3 : 2 + len(shards)]
+    outw, attended, grad = refs[2 + len(shards) : 5 + len(shards)]
+    c = spot()[1]
+    half = own.shape[0]
+    outer_weights(c, own, own_other, outw)
+    attend_kernel(groups, heads, rows, shards, info, counts, projected, mine, other, packed, attended,
+                  *refs[5 + len(shards) :])
+    for n in range(len(shards)):
+        share = jnp.dot(attended[n * rows : (n + 1) * rows, :], outw[...], preferred_element_type=F32)
+        if n == 0:
             base_out[...] = hidden[...] + share
         else:
-            shares[s - 1][...] = share.astype(BF16)
-    total = lax.dot_general(attended[0:rows, :], cotangent[0], ROWS_CONTRACT, preferred_element_type=F32)
-    for s in range(1, groups):
-        total = total + lax.dot_general(
-            attended[s * rows : (s + 1) * rows, :], cotangent[s], ROWS_CONTRACT, preferred_element_type=F32
+            shares[n - 1][...] = share.astype(BF16)
+    total = None
+    for s in range(groups):
+        source, n = (attended, s) if s < groups // 2 else (early, s - groups // 2)
+        term = lax.dot_general(
+            source[n * rows : (n + 1) * rows, :], cotangent[s][...], ROWS_CONTRACT, preferred_element_type=F32
         )
+        total = term if total is None else total + term
     grad[...] = total
     grad_out[...] = grad[pl.ds(pl.multiple_of(c * half, half), half), :]
     send_out[...] = grad[pl.ds(pl.multiple_of((1 - c) * half, half), half), :].astype(BF16)
+
+
+def finish_kernel(count, factor, base, grad, *refs):
+    shares, terms = refs[:count], refs[count:-2]
+    layer_out, grad_out = refs[-2:]
+    layer = base[...]
+    for share in shares:
+        layer = layer + share[...].astype(F32)
+    layer_out[...] = layer.astype(BF16)
+    sums = [grad[...].astype(F32)] + [term[...].astype(F32) for term in terms]
+    while len(sums) > 1:
+        sums = [sums[i] + sums[i + 1] for i in range(0, len(sums), 2)]
+    grad_out[...] = sums[0] * factor
 
 
 def paired_shards(
@@ -388,13 +472,10 @@
     space = lax.axis_size("space")
     parts = lax.axis_size("dp")
     groups = space // 2
-    position = lax.axis_index("space")
-    d = lax.axis_index("dp")
-    z, c = position // 2, position % 2
     rows, cin = voxel_feats.shape[1:]
     taps = neighbours.shape[2]
     cap = wanted_rows.shape[3]
-    _, out_width = conv_weight.shape[1:]
+    depth, out_width = conv_weight.shape[1:]
     pdepth = input_weight.shape[0]
     att = input_weight.shape[1] // 3
     width = att // groups
@@ -412,36 +493,55 @@
     def over_dp(x, m):
         return lax.ppermute(x, "dp", [(i, i ^ m) for i in range(parts)])
 
-    where = jnp.stack([z, c, d]).astype(jnp.int32)
-    quarter = lax.dynamic_slice_in_dim(conv_weight, d * cut, cut, axis=2)
-    near = jnp.stack([over_z(quarter, k) for k in range(1, groups)])
-
     slots = space * cap
-    info = rows + 2 * pdepth + pdepth * (3 * width - 2 * cin) // cin
-    info_rows = -(-(taps + 2) // 16) * 16
-    packs = call(
-        functools.partial(pack_kernel, groups, width),
-        [where],
-        [voxel_feats[0], neighbours.transpose(2, 0, 1), wanted_rows[0, 0], block_choice[0], input_weight],
-        [jax.ShapeDtypeStruct((info + info_rows, cin), BF16)] * groups,
-        [pltpu.VMEM((info_rows, cin), F32)],
+    info_rows = -(-(taps + 2) // 8) * 8
+    strip = pdepth // parts
+    depth_all = (taps + 1) * depth + pdepth + strip
+    voxels, own, beside, *quarters = call(
+        functools.partial(pack_kernel, groups, width, rows),
+        [],
+        [
+            voxel_feats[0],
+            neighbours.transpose(2, 0, 1),
+            wanted_rows[0, 0],
+            block_choice[0],
+            input_weight,
+            conv_weight,
+        ],
+        [jax.ShapeDtypeStruct((rows + info_rows, cin), BF16)]
+        + [jax.ShapeDtypeStruct((depth_all, out_width), BF16)] * 2
+        + [jax.ShapeDtypeStruct((depth_all, cut), BF16)] * (groups - 2),
+        [
+            pltpu.VMEM((taps, 1, rows), jnp.int32),
+            pltpu.VMEM(wanted_rows.shape[2:], jnp.int32),
+            pltpu.VMEM(block_choice.shape[1:], jnp.int32),
+            pltpu.VMEM(input_weight.shape, BF16),
+            pltpu.VMEM(conv_weight.shape, BF16),
+            pltpu.VMEM((groups, pdepth + strip, out_width), BF16),
+            pltpu.VMEM((info_rows, cin), F32),
+            pltpu.SemaphoreType.DMA((6,)),
+        ],
         1000,
-    )
-    mine = jnp.stack([packs[0]] + [over_z(packs[k], k) for k in range(1, groups)])
-
-    own_other = over_core(conv_weight)
+        pltpu.HBM,
+        PACK_LIMIT,
+    )
+    beside = over_z(beside, 1)
+    near = jnp.stack([over_z(quarters[k - 2], k) for k in range(2, groups)])
+    mine = jnp.stack([voxels] + [over_z(voxels, k) for k in range(1, groups)])
+    far = jnp.stack([over_dp(near, m) for m in range(1, parts)])
+    own_other = over_core(own)
     out_other = over_core(output_weight)
-    far = [over_dp(near, m) for m in range(1, parts)]
+    beside_other = over_core(beside)
     near_other = over_core(near)
     other = over_core(mine)
-    cots = jnp.stack([cotangent[0]] + [over_z(cotangent[0], k) for k in range(1, groups)])
-    far_other = [over_core(x) for x in far]
+    far_other = over_core(far)
+    cots = [cotangent[0]] + [over_z(cotangent[0], k) for k in range(1, groups)]
 
     tokens = groups * rows
     table_rows = -(-(rows + slots + 1) // 128) * 128
     (gathered,) = call(
-        functools.partial(taps_kernel, groups, rows, cap, info),
-        [where],
+        functools.partial(taps_kernel, groups, rows, cap, rows),
+        [],
         [mine, other],
         [jax.ShapeDtypeStruct((taps + 1, tokens, cin), BF16)],
         [pltpu.VMEM((2 * tokens, cin), BF16), pltpu.VMEM((table_rows, cin), BF16)],
@@ -449,8 +549,19 @@
     )
     hidden, projected, summary = call(
         functools.partial(conv_kernel, groups, parts, rows),
-        [where, live_counts],
-        [gathered, norm_gain[None, :], conv_weight, own_other, near, near_other, *far, *far_other, mine, other],
+        [live_counts],
+        [
+            gathered,
+            norm_gain[None, :],
+            own,
+            beside,
+            near,
+            far,
+            own_other,
+            beside_other,
+            near_other,
+            far_other,
+        ],
         [
             jax.ShapeDtypeStruct((rows, out_width), F32),
             jax.ShapeDtypeStruct((tokens, 3 * width), BF16),
@@ -466,52 +577,83 @@
     )
     summary_other = over_core(summary)
 
-    outs = call(
-        functools.partial(attend_kernel, groups, heads, rows, info + taps + 1),
-        [where, live_counts],
-        [projected, summary, summary_other, mine, cots, output_weight, out_other, hidden],
+    near_shards = groups // 2
+    far_shards = groups - near_shards
+    share = jax.ShapeDtypeStruct((rows, out_width), BF16)
+    padded = -(-space * local_blocks // 128) * 128
+    outer = pltpu.VMEM((2 * half, out_width), BF16)
+
+    def softmax_space(shards):
+        return [
+            pltpu.VMEM((padded, 2 * width), BF16),
+            pltpu.VMEM((shards * heads, rows, rows), F32),
+            pltpu.VMEM((shards * heads, rows, padded), F32),
+            pltpu.VMEM((shards * heads, rows, rows), BF16),
+            pltpu.VMEM((shards * heads, rows, padded), BF16),
+        ]
+
+    common = [projected, summary, summary_other, mine, output_weight, out_other]
+    *shares, early = call(
+        functools.partial(first_kernel, groups, heads, rows, rows + taps + 1),
+        [live_counts],
+        common,
+        [share] * far_shards + [jax.ShapeDtypeStruct((far_shards * rows, width), BF16)],
+        [outer] + softmax_space(far_shards),
+        4 * tokens * width * (rows + out_width),
+    )
+    received = [over_z(shares[k - near_shards], k) for k in range(near_shards, groups)]
+    base, grad, send, *shares = call(
+        functools.partial(second_kernel, groups, heads, rows, rows + taps + 1),
+        [live_counts],
+        common + [early, hidden, *cots],
         [
             jax.ShapeDtypeStruct((rows, out_width), F32),
             jax.ShapeDtypeStruct((half, out_width), F32),
             jax.ShapeDtypeStruct((half, out_width), BF16),
         ]
-        + [jax.ShapeDtypeStruct((rows, out_width), BF16)] * (groups - 1),
+        + [share] * (near_shards - 1),
         [
-            pltpu.VMEM((tokens, width), BF16),
-            pltpu.VMEM((2 * half, out_width), BF16),
+            outer,
+            pltpu.VMEM((near_shards * rows, width), BF16),
             pltpu.VMEM((2 * half, out_width), F32),
-        ],
-        8 * tokens * width * (rows + out_width),
-    )
-    base, grad, send = outs[0:3]
-    received = [over_z(outs[2 + k], k) for k in range(1, groups)]
+        ]
+        + softmax_space(near_shards),
+        6 * tokens * width * (rows + out_width),
+    )
+    received += [over_z(shares[k - 1], k) for k in range(1, near_shards)]
     grad = (grad + over_core(send).astype(F32)).astype(BF16)
-    terms = [grad.astype(F32)] + [over_dp(grad, m).astype(F32) for m in range(1, parts)]
-    while len(terms) > 1:
-        terms = [terms[i] + terms[i + 1] for i in range(0, len(terms), 2)]
+    terms = [over_dp(grad, m) for m in range(1, parts)]
     factor = (parts * space * rows) ** (-0.5)
-    layer = base
-    for x in received:
-        layer = layer + x.astype(F32)
-    return (layer.astype(BF16)[None], terms[0] * factor)
+    layer, total = call(
+        functools.partial(finish_kernel, len(received), factor),
+        [],
+        [base, grad, *received, *terms],
+        [share, jax.ShapeDtypeStruct((half, out_width), F32)],
+        [],
+        1000,
+    )
+    return (layer[None], total)
 
 
 def section(mesh, *args):
     space, parts = mesh.shape["space"], mesh.shape["dp"]
     groups = space // 2
     powers = space % 2 == 0 and groups & (groups - 1) == 0 and parts & (parts - 1) == 0
-    cin = args[0].shape[2]
-    width = args[7].shape[1] // 3 // max(groups, 1)
-    tail = 3 * width - 2 * cin
+    rows, cin = args[0].shape[1:]
+    depth, out_width = args[5].shape[1:]
+    pdepth = args[7].shape[0]
+    width = args[7].shape[1] // 3 // groups if groups else 0
+    cut = out_width // parts
     fits = (
         powers
-        and HEADS % max(groups, 1) == 0
-        and args[5].shape[2] % (128 * parts) == 0
-        and 0 < tail <= 128
-        and cin % tail == 0
-        and (args[7].shape[0] * tail) % (16 * cin) == 0
-        and args[0].shape[1] * 2 == cin
-        and space * args[2].shape[3] <= cin
+        and groups >= 4
+        and HEADS % groups == 0
+        and out_width % (128 * parts) == 0
+        and 0 < 3 * width - out_width <= cut
+        and pdepth % (16 * parts) == 0
+        and depth % 32 == 0
+        and rows * 2 == cin
+        and space * args[2].shape[3] <= rows
     )
     if not fits:
         return general_shards(*args)

time: 81.2 us -> 65.1 us (0.80)
  waiting for transfers between devices: 34 us -> 22.7 us
  local copies, waits for them, and re-layouts: 4.74 us -> 0.02 us
  starting transfers between devices: 28 us -> 30.8 us
  other arithmetic: 1.73 us -> 0.13 us
  Pallas kernels: 11.6 us -> 10.5 us
    ppermute x12, waiting for transfers between devices: 26.9 us -> 18.1 us  [over_z(): lax.ppermute(x, 'space', [(i, (i // 2 ^ k) * 2 + i % 2) for i in range(sp...]
    unnamed x20 -> x8, local copies, waits for them, and re-layouts: 3.91 us -> 0.02 us
    ppermute x6, waiting for transfers between devices: 6.98 us -> 3.26 us  [over_dp(): return lax.ppermute(x, 'dp', [(i, i ^ m) for i in range(parts)])]
    ppermute x6, starting transfers between devices: 7.1 us -> 8.43 us  [over_dp(): return lax.ppermute(x, 'dp', [(i, i ^ m) for i in range(parts)])]
    ppermute x9 -> x8, waiting for transfers between devices: 0.1 us -> 1.37 us  [over_core(): return lax.ppermute(x, 'space', [(i, i ^ 1) for i in range(space)])]
    pallas_call x4 -> x6, Pallas kernels: 11.6 us -> 10.5 us  [call(): pl.pallas_call(kernel, out_shape=tuple(outs), in_specs=[smem()] * len(sca...]
    ppermute x12, starting transfers between devices: 19.6 us -> 20.6 us  [over_z(): lax.ppermute(x, 'space', [(i, (i // 2 ^ k) * 2 + i % 2) for i in range(sp...]
    dynamic_slice x1 -> x0, local copies, waits for them, and re-layouts: 0.83 us -> none  [paired_shards(): quarter = lax.dynamic_slice_in_dim(conv_weight, d * cut, cut, axis=2)]
  transfers between devices with their start and end apart: 27 -> 26, of which waited for: 12 -> 11; matrix products, arithmetic and copies ran while one was open for 2% -> 0% of each run, Pallas kernels for 6% -> 10%
where the time goes in v3:
time: 65.1 us; the launch traced here: 64.9 us
  starting transfers between devices  30.8 us (47%)
  waiting for transfers between devices  22.7 us (35%)
  Pallas kernels  10.5 us (16%)
  between operations  0.8 us (1%)
    ppermute x12, starting transfers between devices, over_z(): lax.ppermute(x, 'space', [(i, (i // 2 ^ k) * 2 + i % 2) for i in range(sp...  20.6 us
    ppermute x12, waiting for transfers between devices, over_z(): lax.ppermute(x, 'space', [(i, (i // 2 ^ k) * 2 + i % 2) for i in range(sp...  18.1 us
    pallas_call x6, Pallas kernels, call(): pl.pallas_call(kernel, out_shape=tuple(outs), in_specs=[smem()] * len(sca...  10.5 us
    ppermute x6, starting transfers between devices, over_dp(): return lax.ppermute(x, 'dp', [(i, i ^ m) for i in range(parts)])  8.43 us
    ppermute x6, waiting for transfers between devices, over_dp(): return lax.ppermute(x, 'dp', [(i, i ^ m) for i in range(parts)])  3.26 us
    ppermute x8, starting transfers between devices, over_core(): return lax.ppermute(x, 'space', [(i, i ^ 1) for i in range(space)])  1.76 us
    ppermute x8, waiting for transfers between devices, over_core(): return lax.ppermute(x, 'space', [(i, i ^ 1) for i in range(space)])  1.37 us
  transfers between devices with their start and end apart: 26, of which 11 were waited for; matrix products, arithmetic and copies ran while one was open for 0% of the time, Pallas kernels for 10%

profile of v3, /device:TPU:0, one launch (start us, length us, event | category | flops | bytes accessed | tf_op | source)
XLA Modules:
  0.0 64.9 jit_solution(13246020474172339139)
XLA Ops:
  0.6 1.3 %shard_map.113 = (bf16[136,256]{1,0:T(8,128)(2,1)S(1)}, bf16[304,512]{1,0:T(8,128)(2,1)S(1)}, bf16[304,512]{1,0:T(8,128)(2,1)S(1)}, bf16[304,128]{1,0:T(8,128)(2,1)S(1)}, bf16[304,128]{1,0:T(8,128)(2,1)S(1)}) custom-call(bf16[128,256]{1,0:T(8,128)(2,1)} %bitcast.30, s32[6,1,128]{2,1,0:T(1,128)} %bitcast.32, s32[8,8]{1,0:T(8,128)} %bitcast.31, ...), custom_call_target="tpu_custom_call" | custom-call | flops 1000 | bytes 1441056 | tf_op jit(solution)/shard_map/pallas_call | solution.py:159
  2.0 5.1 %collective-permute-start.6 = (bf16[304,128]{1,0:T(8,128)(2,1)S(1)}, bf16[304,128]{1,0:T(8,128)(2,1)S(1)}, u32[]{:S(2)}, u32[]{:S(2)}) collective-permute-start(bf16[304,128]{1,0:T(8,128)(2,1)S(1)} %get-tuple-element.23), channel_id=1, source_target_pairs={{0,6},{1,7},{2,4},{3,5},{4,2},{5,3},{6,0},{7,1},{8,14},{9,15},{10,... | collective-permute-start | bytes 233480 | tf_op jit(solution)/shard_map/ppermute | solution.py:488
  7.1 0.0 collective-permute-start.5
  7.1 2.8 %collective-permute-done.6 = bf16[304,128]{1,0:T(8,128)(2,1)S(1)} collective-permute-done((bf16[304,128]{1,0:T(8,128)(2,1)S(1)}, bf16[304,128]{1,0:T(8,128)(2,1)S(1)}, u32[]{:S(2)}, u32[]{:S(2)}) %collective-permute-start.6) | collective-permute-done | bytes 77856 | tf_op jit(solution)/shard_map/ppermute | solution.py:488
  9.9 3.7 %collective-permute-done.5 = bf16[304,128]{1,0:T(8,128)(2,1)S(1)} collective-permute-done((bf16[304,128]{1,0:T(8,128)(2,1)S(1)}, bf16[304,128]{1,0:T(8,128)(2,1)S(1)}, u32[]{:S(2)}, u32[]{:S(2)}) %collective-permute-start.5) | collective-permute-done | bytes 77856 | tf_op jit(solution)/shard_map/ppermute | solution.py:488
  13.7 1.6 %collective-permute-start.7 = (bf16[2,304,128]{2,1,0:T(8,128)(2,1)S(1)}, bf16[2,304,128]{2,1,0:T(8,128)(2,1)S(1)}, u32[]{:S(2)}, u32[]{:S(2)}) collective-permute-start(bf16[2,304,128]{2,1,0:T(8,128)(2,1)S(1)} %pad_maximum_fusion.2.refs_2_), channel_id=1, source_target_pairs={{0,8},{8,0},{16,24},{24,16},{1,9},{9,1},{17,25},{25,17},{2,10},{10... | collective-permute-start | bytes 466952 | tf_op jit(solution)/shard_map/ppermute | solution.py:494
  15.2 1.5 %collective-permute-start.8 = (bf16[2,304,128]{2,1,0:T(8,128)(2,1)S(1)}, bf16[2,304,128]{2,1,0:T(8,128)(2,1)S(1)}, u32[]{:S(2)}, u32[]{:S(2)}) collective-permute-start(bf16[2,304,128]{2,1,0:T(8,128)(2,1)S(1)} %pad_maximum_fusion.2.refs_2_), channel_id=1, source_target_pairs={{0,16},{8,24},{16,0},{24,8},{1,17},{9,25},{17,1},{25,9},{2,18},{10... | collective-permute-start | bytes 466952 | tf_op jit(solution)/shard_map/ppermute | solution.py:494
  16.7 0.5 collective-permute-start.9
  17.2 0.0 collective-permute-start.4
  17.2 2.0 %collective-permute-start = (bf16[136,256]{1,0:T(8,128)(2,1)S(1)}, bf16[136,256]{1,0:T(8,128)(2,1)S(1)}, u32[]{:S(2)}, u32[]{:S(2)}) collective-permute-start(bf16[136,256]{1,0:T(8,128)(2,1)S(1)} %get-tuple-element.19), channel_id=1, source_target_pairs={{0,2},{1,3},{2,0},{3,1},{4,6},{5,7},{6,4},{7,5},{8,10},{9,11},{10,... | collective-permute-start | bytes 208904 | tf_op jit(solution)/shard_map/ppermute | solution.py:488
  19.2 0.6 collective-permute-done.7
  19.8 1.3 %collective-permute-start.1 = (bf16[136,256]{1,0:T(8,128)(2,1)S(1)}, bf16[136,256]{1,0:T(8,128)(2,1)S(1)}, u32[]{:S(2)}, u32[]{:S(2)}) collective-permute-start(bf16[136,256]{1,0:T(8,128)(2,1)S(1)} %get-tuple-element.19), channel_id=1, source_target_pairs={{0,4},{1,5},{2,6},{3,7},{4,0},{5,1},{6,2},{7,3},{8,12},{9,13},{10,... | collective-permute-start | bytes 208904 | tf_op jit(solution)/shard_map/ppermute | solution.py:488
  21.1 2.7 %collective-permute-done.8 = bf16[2,304,128]{2,1,0:T(8,128)(2,1)S(1)} collective-permute-done((bf16[2,304,128]{2,1,0:T(8,128)(2,1)S(1)}, bf16[2,304,128]{2,1,0:T(8,128)(2,1)S(1)}, u32[]{:S(2)}, u32[]{:S(2)}) %collective-permute-start.8) | collective-permute-done | bytes 155680 | tf_op jit(solution)/shard_map/ppermute | solution.py:494
  23.8 2.6 %collective-permute-start.2 = (bf16[136,256]{1,0:T(8,128)(2,1)S(1)}, bf16[136,256]{1,0:T(8,128)(2,1)S(1)}, u32[]{:S(2)}, u32[]{:S(2)}) collective-permute-start(bf16[136,256]{1,0:T(8,128)(2,1)S(1)} %get-tuple-element.19), channel_id=1, source_target_pairs={{0,6},{1,7},{2,4},{3,5},{4,2},{5,3},{6,0},{7,1},{8,14},{9,15},{10,... | collective-permute-start | bytes 208904 | tf_op jit(solution)/shard_map/ppermute | solution.py:488
  26.4 0.1 pad_maximum_fusion.refs_3_
  26.5 0.1 collective-permute-start.13
  26.6 2.2 %collective-permute-done = bf16[136,256]{1,0:T(8,128)(2,1)S(1)} collective-permute-done((bf16[136,256]{1,0:T(8,128)(2,1)S(1)}, bf16[136,256]{1,0:T(8,128)(2,1)S(1)}, u32[]{:S(2)}, u32[]{:S(2)}) %collective-permute-start) | collective-permute-done | bytes 69664 | tf_op jit(solution)/shard_map/ppermute | solution.py:488
  28.7 0.0 collective-permute-done.1
  28.7 1.3 %collective-permute-done.2 = bf16[136,256]{1,0:T(8,128)(2,1)S(1)} collective-permute-done((bf16[136,256]{1,0:T(8,128)(2,1)S(1)}, bf16[136,256]{1,0:T(8,128)(2,1)S(1)}, u32[]{:S(2)}, u32[]{:S(2)}) %collective-permute-start.2) | collective-permute-done | bytes 69664 | tf_op jit(solution)/shard_map/ppermute | solution.py:488
  30.1 0.1 collective-permute-start.3
  30.2 0.5 collective-permute-start.10
  30.7 0.0 collective-permute-done.4.refs_1_
  30.7 0.1 collective-permute-start.11
  30.7 0.4 collective-permute-start.12
  31.2 0.5 collective-permute-done.3.other
  31.7 0.0 collective-permute-start.16
  31.7 1.5 %shard_map.114.taps = bf16[7,512,256]{2,1,0:T(8,128)(2,1)S(1)} custom-call(bf16[4,136,256]{2,1,0:T(8,128)(2,1)S(1)} %pad_maximum_fusion.1.mine.packed, bf16[4,136,256]{2,1,0:T(8,128)(2,1)S(1)} %collective-permute-done.3.other), custom_call_target="tpu_custom_call" | custom-call | flops 402653184 | bytes 2392064 | tf_op jit(solution)/shard_map/pallas_call | solution.py:159
  33.3 0.0 collective-permute-done.12.refs_6_
  33.3 3.1 %collective-permute-start.17 = (bf16[128,512]{1,0:T(8,128)(2,1)S(1)}, bf16[128,512]{1,0:T(8,128)(2,1)S(1)}, u32[]{:S(2)}, u32[]{:S(2)}) collective-permute-start(bf16[128,512]{1,0:T(8,128)(2,1)S(1)} %bitcast.17), channel_id=1, source_target_pairs={{0,4},{1,5},{2,6},{3,7},{4,0},{5,1},{6,2},{7,3},{8,12},{9,13},{10,... | collective-permute-start | bytes 393224 | tf_op jit(solution)/shard_map/ppermute | solution.py:488
  36.4 0.0 collective-permute-done.10.refs_4_
  36.4 1.3 %collective-permute-start.18 = (bf16[128,512]{1,0:T(8,128)(2,1)S(1)}, bf16[128,512]{1,0:T(8,128)(2,1)S(1)}, u32[]{:S(2)}, u32[]{:S(2)}) collective-permute-start(bf16[128,512]{1,0:T(8,128)(2,1)S(1)} %bitcast.18), channel_id=1, source_target_pairs={{0,6},{1,7},{2,4},{3,5},{4,2},{5,3},{6,0},{7,1},{8,14},{9,15},{10,... | collective-permute-start | bytes 393224 | tf_op jit(solution)/shard_map/ppermute | solution.py:488
  37.7 0.0 collective-permute-start.15
  37.8 2.9 %shard_map.115 = (f32[128,512]{1,0:T(8,128)S(1)}, bf16[512,576]{1,0:T(8,128)(2,1)S(1)}, bf16[8,384]{1,0:T(8,128)(2,1)S(1)}) custom-call(s32[1,8]{1,0:T(1,128)S(1)} %copy-done.2, bf16[7,512,256]{2,1,0:T(8,128)(2,1)S(1)} %shard_map.114.taps, f32[1,512]{1,0:T(1,128)S(1)} %bitcast.21, bf16[304,512]{1,0:T(8,128)(2,1)S(1)} %get-tuple-element.20.refs_0_, ...), custom_call_target="tpu_custom_call" | custom-call | flops 1241513984 | bytes 5185536 | tf_op jit(solution)/shard_map/pallas_call | solution.py:159
  40.7 0.5 collective-permute-start.14
  41.2 0.8 %collective-permute-done.14.other = bf16[8,384]{1,0:T(8,128)(2,1)S(1)} collective-permute-done((bf16[8,384]{1,0:T(8,128)(2,1)S(1)}, bf16[8,384]{1,0:T(8,128)(2,1)S(1)}, u32[]{:S(2)}, u32[]{:S(2)}) %collective-permute-start.14) | collective-permute-done | bytes 6176 | tf_op jit(solution)/shard_map/ppermute | solution.py:491
  42.1 1.8 %shard_map.116 = (bf16[128,512]{1,0:T(8,128)(2,1)S(1)}, bf16[128,512]{1,0:T(8,128)(2,1)S(1)}, bf16[256,192]{1,0:T(8,128)(2,1)S(1)}) custom-call(s32[1,8]{1,0:T(1,128)S(1)} %copy-done.2, bf16[512,576]{1,0:T(8,128)(2,1)S(1)} %get-tuple-element.24.projected, bf16[8,384]{1,0:T(8,128)(2,1)S(1)} %get-tuple-element.25.mine, ...), custom_call_target="tpu_custom_call" | custom-call | flops 251658240 | bytes 1437696 | tf_op jit(solution)/shard_map/pallas_call | solution.py:159
  43.9 2.5 %collective-permute-done.17.refs_2_ = bf16[128,512]{1,0:T(8,128)(2,1)S(1)} collective-permute-done((bf16[128,512]{1,0:T(8,128)(2,1)S(1)}, bf16[128,512]{1,0:T(8,128)(2,1)S(1)}, u32[]{:S(2)}, u32[]{:S(2)}) %collective-permute-start.17) | collective-permute-done | bytes 131104 | tf_op jit(solution)/shard_map/ppermute | solution.py:488
  46.4 2.1 %shard_map.117 = (f32[128,512]{1,0:T(8,128)S(1)}, f32[96,512]{1,0:T(8,128)S(1)}, bf16[96,512]{1,0:T(8,128)(2,1)S(1)}, bf16[128,512]{1,0:T(8,128)(2,1)S(1)}) custom-call(s32[1,8]{1,0:T(1,128)S(1)} %copy-done.2, bf16[512,576]{1,0:T(8,128)(2,1)S(1)} %get-tuple-element.24.projected, bf16[8,384]{1,0:T(8,128)(2,1)S(1)} %get-tuple-element.25.mine, ...), custom_call_target="tpu_custom_call" | custom-call | flops 377487360 | bytes 2650112 | tf_op jit(solution)/shard_map/pallas_call | solution.py:159
  48.5 0.1 collective-permute-start.19
  48.6 2.6 %collective-permute-start.22 = (bf16[128,512]{1,0:T(8,128)(2,1)S(1)}, bf16[128,512]{1,0:T(8,128)(2,1)S(1)}, u32[]{:S(2)}, u32[]{:S(2)}) collective-permute-start(bf16[128,512]{1,0:T(8,128)(2,1)S(1)} %get-tuple-element.33), channel_id=1, source_target_pairs={{0,2},{1,3},{2,0},{3,1},{4,6},{5,7},{6,4},{7,5},{8,10},{9,11},{10,... | collective-permute-start | bytes 393224 | tf_op jit(solution)/shard_map/ppermute | solution.py:488
  51.2 1.0 %collective-permute-start.20 = (bf16[128,512]{1,0:T(8,128)(2,1)S(1)}, bf16[128,512]{1,0:T(8,128)(2,1)S(1)}, u32[]{:S(2)}, u32[]{:S(2)}) collective-permute-start(bf16[128,512]{1,0:T(8,128)(2,1)S(1)} %get-tuple-element.31), channel_id=1, source_target_pairs={{0,4},{1,5},{2,6},{3,7},{4,0},{5,1},{6,2},{7,3},{8,12},{9,13},{10,... | collective-permute-start | bytes 393224 | tf_op jit(solution)/shard_map/ppermute | solution.py:488
  52.2 1.5 %collective-permute-start.21 = (bf16[128,512]{1,0:T(8,128)(2,1)S(1)}, bf16[128,512]{1,0:T(8,128)(2,1)S(1)}, u32[]{:S(2)}, u32[]{:S(2)}) collective-permute-start(bf16[128,512]{1,0:T(8,128)(2,1)S(1)} %get-tuple-element.32), channel_id=1, source_target_pairs={{0,6},{1,7},{2,4},{3,5},{4,2},{5,3},{6,0},{7,1},{8,14},{9,15},{10,... | collective-permute-start | bytes 393224 | tf_op jit(solution)/shard_map/ppermute | solution.py:488
  53.6 1.4 %collective-permute-start.23 = (bf16[96,512]{1,0:T(8,128)(2,1)S(1)}, bf16[96,512]{1,0:T(8,128)(2,1)S(1)}, u32[]{:S(2)}, u32[]{:S(2)}) collective-permute-start(bf16[96,512]{1,0:T(8,128)(2,1)S(1)} %add_convert_fusion.grad), channel_id=1, source_target_pairs={{0,8},{8,0},{16,24},{24,16},{1,9},{9,1},{17,25},{25,17},{2,10},{10... | collective-permute-start | bytes 294920 | tf_op jit(solution)/shard_map/ppermute | solution.py:494
  55.1 1.5 %collective-permute-start.24 = (bf16[96,512]{1,0:T(8,128)(2,1)S(1)}, bf16[96,512]{1,0:T(8,128)(2,1)S(1)}, u32[]{:S(2)}, u32[]{:S(2)}) collective-permute-start(bf16[96,512]{1,0:T(8,128)(2,1)S(1)} %add_convert_fusion.grad), channel_id=1, source_target_pairs={{0,16},{8,24},{16,0},{24,8},{1,17},{9,25},{17,1},{25,9},{2,18},{10... | collective-permute-start | bytes 294920 | tf_op jit(solution)/shard_map/ppermute | solution.py:494
  56.6 0.8 %collective-permute-done.22.refs_2_ = bf16[128,512]{1,0:T(8,128)(2,1)S(1)} collective-permute-done((bf16[128,512]{1,0:T(8,128)(2,1)S(1)}, bf16[128,512]{1,0:T(8,128)(2,1)S(1)}, u32[]{:S(2)}, u32[]{:S(2)}) %collective-permute-start.22) | collective-permute-done | bytes 131104 | tf_op jit(solution)/shard_map/ppermute | solution.py:488
  57.4 1.9 %collective-permute-start.25 = (bf16[96,512]{1,0:T(8,128)(2,1)S(1)}, bf16[96,512]{1,0:T(8,128)(2,1)S(1)}, u32[]{:S(2)}, u32[]{:S(2)}) collective-permute-start(bf16[96,512]{1,0:T(8,128)(2,1)S(1)} %add_convert_fusion.grad), channel_id=1, source_target_pairs={{0,24},{8,16},{16,8},{24,0},{1,25},{9,17},{17,9},{25,1},{2,26},{10... | collective-permute-start | bytes 294920 | tf_op jit(solution)/shard_map/ppermute | solution.py:494
  59.3 4.8 %collective-permute-done.20.refs_0_ = bf16[128,512]{1,0:T(8,128)(2,1)S(1)} collective-permute-done((bf16[128,512]{1,0:T(8,128)(2,1)S(1)}, bf16[128,512]{1,0:T(8,128)(2,1)S(1)}, u32[]{:S(2)}, u32[]{:S(2)}) %collective-permute-start.20) | collective-permute-done | bytes 131104 | tf_op jit(solution)/shard_map/ppermute | solution.py:488
  64.1 0.8 %shard_map.118 = (bf16[128,512]{1,0:T(8,128)(2,1)}, f32[96,512]{1,0:T(8,128)}) custom-call(f32[128,512]{1,0:T(8,128)S(1)} %get-tuple-element.28.base, bf16[96,512]{1,0:T(8,128)(2,1)S(1)} %add_convert_fusion.grad, bf16[128,512]{1,0:T(8,128)(2,1)S(1)} %collective-permute-done.20.refs_0_, bf16[128,512]{1,0:T(8,128)(2,1)S(1)} %collective-permute-done.21.refs_1_, ...), custom_call_target="tpu_custom_call" | custom-call | flops 1000 | bytes 1376256 | tf_op jit(solution)/shard_map/pallas_call | solution.py:159
  (22 shorter events, 0.1 us)
Async XLA Ops:
  0.6 31.1 %copy-start.1 = (bf16[1,128,512]{2,1,0:T(8,128)(2,1)S(1)}, bf16[1,128,512]{2,1,0:T(8,128)(2,1)}, u32[]{:S(2)}) copy-start(bf16[1,128,512]{2,1,0:T(8,128)(2,1)} %param.19) | copy-start | bytes 393220
  2.0 7.9 %collective-permute-start.6 = (bf16[304,128]{1,0:T(8,128)(2,1)S(1)}, bf16[304,128]{1,0:T(8,128)(2,1)S(1)}, u32[]{:S(2)}, u32[]{:S(2)}) collective-permute-start(bf16[304,128]{1,0:T(8,128)(2,1)S(1)} %get-tuple-element.23), channel_id=1, source_target_pairs={{0,6},{1,7},{2,4},{3,5},{4,2},{5,3},{6,0},{7,1},{8,14},{9,15},{10,... | collective-permute-start | bytes 233480 | tf_op jit(solution)/shard_map/ppermute | solution.py:488
  7.1 6.5 %collective-permute-start.5 = (bf16[304,128]{1,0:T(8,128)(2,1)S(1)}, bf16[304,128]{1,0:T(8,128)(2,1)S(1)}, u32[]{:S(2)}, u32[]{:S(2)}) collective-permute-start(bf16[304,128]{1,0:T(8,128)(2,1)S(1)} %get-tuple-element.22), channel_id=1, source_target_pairs={{0,4},{1,5},{2,6},{3,7},{4,0},{5,1},{6,2},{7,3},{8,12},{9,13},{10,... | collective-permute-start | bytes 233480 | tf_op jit(solution)/shard_map/ppermute | solution.py:488
  13.7 6.2 %collective-permute-start.7 = (bf16[2,304,128]{2,1,0:T(8,128)(2,1)S(1)}, bf16[2,304,128]{2,1,0:T(8,128)(2,1)S(1)}, u32[]{:S(2)}, u32[]{:S(2)}) collective-permute-start(bf16[2,304,128]{2,1,0:T(8,128)(2,1)S(1)} %pad_maximum_fusion.2.refs_2_), channel_id=1, source_target_pairs={{0,8},{8,0},{16,24},{24,16},{1,9},{9,1},{17,25},{25,17},{2,10},{10... | collective-permute-start | bytes 466952 | tf_op jit(solution)/shard_map/ppermute | solution.py:494
  15.2 8.6 %collective-permute-start.8 = (bf16[2,304,128]{2,1,0:T(8,128)(2,1)S(1)}, bf16[2,304,128]{2,1,0:T(8,128)(2,1)S(1)}, u32[]{:S(2)}, u32[]{:S(2)}) collective-permute-start(bf16[2,304,128]{2,1,0:T(8,128)(2,1)S(1)} %pad_maximum_fusion.2.refs_2_), channel_id=1, source_target_pairs={{0,16},{8,24},{16,0},{24,8},{1,17},{9,25},{17,1},{25,9},{2,18},{10... | collective-permute-start | bytes 466952 | tf_op jit(solution)/shard_map/ppermute | solution.py:494
  16.7 9.7 %collective-permute-start.9 = (bf16[2,304,128]{2,1,0:T(8,128)(2,1)S(1)}, bf16[2,304,128]{2,1,0:T(8,128)(2,1)S(1)}, u32[]{:S(2)}, u32[]{:S(2)}) collective-permute-start(bf16[2,304,128]{2,1,0:T(8,128)(2,1)S(1)} %pad_maximum_fusion.2.refs_2_), channel_id=1, source_target_pairs={{0,24},{8,16},{16,8},{24,0},{1,25},{9,17},{17,9},{25,1},{2,26},{10... | collective-permute-start | bytes 466952 | tf_op jit(solution)/shard_map/ppermute | solution.py:494
  17.2 13.4 %collective-permute-start.4 = (bf16[304,512]{1,0:T(8,128)(2,1)S(1)}, bf16[304,512]{1,0:T(8,128)(2,1)S(1)}, u32[]{:S(2)}, u32[]{:S(2)}) collective-permute-start(bf16[304,512]{1,0:T(8,128)(2,1)S(1)} %get-tuple-element.21), channel_id=1, source_target_pairs={{0,2},{1,3},{2,0},{3,1},{4,6},{5,7},{6,4},{7,5},{8,10},{9,11},{10,... | collective-permute-start | bytes 933896 | tf_op jit(solution)/shard_map/ppermute | solution.py:488
  17.2 11.5 %collective-permute-start = (bf16[136,256]{1,0:T(8,128)(2,1)S(1)}, bf16[136,256]{1,0:T(8,128)(2,1)S(1)}, u32[]{:S(2)}, u32[]{:S(2)}) collective-permute-start(bf16[136,256]{1,0:T(8,128)(2,1)S(1)} %get-tuple-element.19), channel_id=1, source_target_pairs={{0,2},{1,3},{2,0},{3,1},{4,6},{5,7},{6,4},{7,5},{8,10},{9,11},{10,... | collective-permute-start | bytes 208904 | tf_op jit(solution)/shard_map/ppermute | solution.py:488
  19.8 8.9 %collective-permute-start.1 = (bf16[136,256]{1,0:T(8,128)(2,1)S(1)}, bf16[136,256]{1,0:T(8,128)(2,1)S(1)}, u32[]{:S(2)}, u32[]{:S(2)}) collective-permute-start(bf16[136,256]{1,0:T(8,128)(2,1)S(1)} %get-tuple-element.19), channel_id=1, source_target_pairs={{0,4},{1,5},{2,6},{3,7},{4,0},{5,1},{6,2},{7,3},{8,12},{9,13},{10,... | collective-permute-start | bytes 208904 | tf_op jit(solution)/shard_map/ppermute | solution.py:488
  23.8 6.2 %collective-permute-start.2 = (bf16[136,256]{1,0:T(8,128)(2,1)S(1)}, bf16[136,256]{1,0:T(8,128)(2,1)S(1)}, u32[]{:S(2)}, u32[]{:S(2)}) collective-permute-start(bf16[136,256]{1,0:T(8,128)(2,1)S(1)} %get-tuple-element.19), channel_id=1, source_target_pairs={{0,6},{1,7},{2,4},{3,5},{4,2},{5,3},{6,0},{7,1},{8,14},{9,15},{10,... | collective-permute-start | bytes 208904 | tf_op jit(solution)/shard_map/ppermute | solution.py:488
  26.4 11.3 %copy-start = (bf16[96,512]{1,0:T(8,128)(2,1)S(1)}, bf16[96,512]{1,0:T(8,128)(2,1)}, u32[]{:S(2)}) copy-start(bf16[96,512]{1,0:T(8,128)(2,1)} %own.3) | copy-start | bytes 294916
  26.4 11.3 %copy-start.2 = (s32[1,8]{1,0:T(1,128)S(1)}, s32[1,8]{1,0:T(1,128)}, u32[]{:S(2)}) copy-start(s32[1,8]{1,0:T(1,128)} %counts.5) | copy-start | bytes 100
  26.4 11.3 %copy-start.3 = (f32[512]{0:T(512)S(1)}, f32[512]{0:T(512)}, u32[]{:S(2)}) copy-start(f32[512]{0:T(512)} %param.16) | copy-start | bytes 6148
  26.5 11.2 %collective-permute-start.13 = (bf16[3,2,304,128]{3,2,1,0:T(8,128)(2,1)S(1)}, bf16[3,2,304,128]{3,2,1,0:T(8,128)(2,1)S(1)}, u32[]{:S(2)}, u32[]{:S(2)}) collective-permute-start(bf16[3,2,304,128]{3,2,1,0:T(8,128)(2,1)S(1)} %pad_maximum_fusion.refs_3_), channel_id=1, source_target_pairs={{0,1},{1,0},{2,3},{3,2},{4,5},{5,4},{6,7},{7,6},{8,9},{9,8},{10,11... | collective-permute-start | bytes 1400840 | tf_op jit(solution)/shard_map/ppermute | solution.py:491
  30.1 1.6 %collective-permute-start.3 = (bf16[4,136,256]{2,1,0:T(8,128)(2,1)S(1)}, bf16[4,136,256]{2,1,0:T(8,128)(2,1)S(1)}, u32[]{:S(2)}, u32[]{:S(2)}) collective-permute-start(bf16[4,136,256]{2,1,0:T(8,128)(2,1)S(1)} %pad_maximum_fusion.1.mine.packed), channel_id=1, source_target_pairs={{0,1},{1,0},{2,3},{3,2},{4,5},{5,4},{6,7},{7,6},{8,9},{9,8},{10,11... | collective-permute-start | bytes 835592 | tf_op jit(solution)/shard_map/ppermute | solution.py:491
  30.2 6.2 %collective-permute-start.10 = (bf16[304,512]{1,0:T(8,128)(2,1)S(1)}, bf16[304,512]{1,0:T(8,128)(2,1)S(1)}, u32[]{:S(2)}, u32[]{:S(2)}) collective-permute-start(bf16[304,512]{1,0:T(8,128)(2,1)S(1)} %get-tuple-element.20.refs_0_), channel_id=1, source_target_pairs={{0,1},{1,0},{2,3},{3,2},{4,5},{5,4},{6,7},{7,6},{8,9},{9,8},{10,11... | collective-permute-start | bytes 933896 | tf_op jit(solution)/shard_map/ppermute | solution.py:491
  30.7 7.1 %collective-permute-start.11 = (bf16[304,512]{1,0:T(8,128)(2,1)S(1)}, bf16[304,512]{1,0:T(8,128)(2,1)S(1)}, u32[]{:S(2)}, u32[]{:S(2)}) collective-permute-start(bf16[304,512]{1,0:T(8,128)(2,1)S(1)} %collective-permute-done.4.refs_1_), channel_id=1, source_target_pairs={{0,1},{1,0},{2,3},{3,2},{4,5},{5,4},{6,7},{7,6},{8,9},{9,8},{10,11... | collective-permute-start | bytes 933896 | tf_op jit(solution)/shard_map/ppermute | solution.py:491
  30.7 2.5 %collective-permute-start.12 = (bf16[2,304,128]{2,1,0:T(8,128)(2,1)S(1)}, bf16[2,304,128]{2,1,0:T(8,128)(2,1)S(1)}, u32[]{:S(2)}, u32[]{:S(2)}) collective-permute-start(bf16[2,304,128]{2,1,0:T(8,128)(2,1)S(1)} %pad_maximum_fusion.2.refs_2_), channel_id=1, source_target_pairs={{0,1},{1,0},{2,3},{3,2},{4,5},{5,4},{6,7},{7,6},{8,9},{9,8},{10,11... | collective-permute-start | bytes 466952 | tf_op jit(solution)/shard_map/ppermute | solution.py:491
  31.7 12.2 %collective-permute-start.16 = (bf16[128,512]{1,0:T(8,128)(2,1)S(1)}, bf16[128,512]{1,0:T(8,128)(2,1)S(1)}, u32[]{:S(2)}, u32[]{:S(2)}) collective-permute-start(bf16[128,512]{1,0:T(8,128)(2,1)S(1)} %bitcast.16), channel_id=1, source_target_pairs={{0,2},{1,3},{2,0},{3,1},{4,6},{5,7},{6,4},{7,5},{8,10},{9,11},{10,... | collective-permute-start | bytes 393224 | tf_op jit(solution)/shard_map/ppermute | solution.py:488
  33.3 13.1 %collective-permute-start.17 = (bf16[128,512]{1,0:T(8,128)(2,1)S(1)}, bf16[128,512]{1,0:T(8,128)(2,1)S(1)}, u32[]{:S(2)}, u32[]{:S(2)}) collective-permute-start(bf16[128,512]{1,0:T(8,128)(2,1)S(1)} %bitcast.17), channel_id=1, source_target_pairs={{0,4},{1,5},{2,6},{3,7},{4,0},{5,1},{6,2},{7,3},{8,12},{9,13},{10,... | collective-permute-start | bytes 393224 | tf_op jit(solution)/shard_map/ppermute | solution.py:488
  36.4 10.0 %collective-permute-start.18 = (bf16[128,512]{1,0:T(8,128)(2,1)S(1)}, bf16[128,512]{1,0:T(8,128)(2,1)S(1)}, u32[]{:S(2)}, u32[]{:S(2)}) collective-permute-start(bf16[128,512]{1,0:T(8,128)(2,1)S(1)} %bitcast.18), channel_id=1, source_target_pairs={{0,6},{1,7},{2,4},{3,5},{4,2},{5,3},{6,0},{7,1},{8,14},{9,15},{10,... | collective-permute-start | bytes 393224 | tf_op jit(solution)/shard_map/ppermute | solution.py:488
  37.7 3.5 %collective-permute-start.15 = (bf16[96,512]{1,0:T(8,128)(2,1)S(1)}, bf16[96,512]{1,0:T(8,128)(2,1)S(1)}, u32[]{:S(2)}, u32[]{:S(2)}) collective-permute-start(bf16[96,512]{1,0:T(8,128)(2,1)S(1)} %copy-done), channel_id=1, source_target_pairs={{0,1},{1,0},{2,3},{3,2},{4,5},{5,4},{6,7},{7,6},{8,9},{9,8},{10,11... | collective-permute-start | bytes 294920 | tf_op jit(solution)/shard_map/ppermute | solution.py:491
  40.7 1.4 %collective-permute-start.14 = (bf16[8,384]{1,0:T(8,128)(2,1)S(1)}, bf16[8,384]{1,0:T(8,128)(2,1)S(1)}, u32[]{:S(2)}, u32[]{:S(2)}) collective-permute-start(bf16[8,384]{1,0:T(8,128)(2,1)S(1)} %get-tuple-element.25.mine), channel_id=1, source_target_pairs={{0,1},{1,0},{2,3},{3,2},{4,5},{5,4},{6,7},{7,6},{8,9},{9,8},{10,11... | collective-permute-start | bytes 18440 | tf_op jit(solution)/shard_map/ppermute | solution.py:491
  48.5 5.1 %collective-permute-start.19 = (bf16[96,512]{1,0:T(8,128)(2,1)S(1)}, bf16[96,512]{1,0:T(8,128)(2,1)S(1)}, u32[]{:S(2)}, u32[]{:S(2)}) collective-permute-start(bf16[96,512]{1,0:T(8,128)(2,1)S(1)} %get-tuple-element.30), channel_id=1, source_target_pairs={{0,1},{1,0},{2,3},{3,2},{4,5},{5,4},{6,7},{7,6},{8,9},{9,8},{10,11... | collective-permute-start | bytes 294920 | tf_op jit(solution)/shard_map/ppermute | solution.py:491
  48.6 8.8 %collective-permute-start.22 = (bf16[128,512]{1,0:T(8,128)(2,1)S(1)}, bf16[128,512]{1,0:T(8,128)(2,1)S(1)}, u32[]{:S(2)}, u32[]{:S(2)}) collective-permute-start(bf16[128,512]{1,0:T(8,128)(2,1)S(1)} %get-tuple-element.33), channel_id=1, source_target_pairs={{0,2},{1,3},{2,0},{3,1},{4,6},{5,7},{6,4},{7,5},{8,10},{9,11},{10,... | collective-permute-start | bytes 393224 | tf_op jit(solution)/shard_map/ppermute | solution.py:488
  51.2 12.9 %collective-permute-start.20 = (bf16[128,512]{1,0:T(8,128)(2,1)S(1)}, bf16[128,512]{1,0:T(8,128)(2,1)S(1)}, u32[]{:S(2)}, u32[]{:S(2)}) collective-permute-start(bf16[128,512]{1,0:T(8,128)(2,1)S(1)} %get-tuple-element.31), channel_id=1, source_target_pairs={{0,4},{1,5},{2,6},{3,7},{4,0},{5,1},{6,2},{7,3},{8,12},{9,13},{10,... | collective-permute-start | bytes 393224 | tf_op jit(solution)/shard_map/ppermute | solution.py:488
  52.2 12.0 %collective-permute-start.21 = (bf16[128,512]{1,0:T(8,128)(2,1)S(1)}, bf16[128,512]{1,0:T(8,128)(2,1)S(1)}, u32[]{:S(2)}, u32[]{:S(2)}) collective-permute-start(bf16[128,512]{1,0:T(8,128)(2,1)S(1)} %get-tuple-element.32), channel_id=1, source_target_pairs={{0,6},{1,7},{2,4},{3,5},{4,2},{5,3},{6,0},{7,1},{8,14},{9,15},{10,... | collective-permute-start | bytes 393224 | tf_op jit(solution)/shard_map/ppermute | solution.py:488
  53.6 10.5 %collective-permute-start.23 = (bf16[96,512]{1,0:T(8,128)(2,1)S(1)}, bf16[96,512]{1,0:T(8,128)(2,1)S(1)}, u32[]{:S(2)}, u32[]{:S(2)}) collective-permute-start(bf16[96,512]{1,0:T(8,128)(2,1)S(1)} %add_convert_fusion.grad), channel_id=1, source_target_pairs={{0,8},{8,0},{16,24},{24,16},{1,9},{9,1},{17,25},{25,17},{2,10},{10... | collective-permute-start | bytes 294920 | tf_op jit(solution)/shard_map/ppermute | solution.py:494
  55.1 9.0 %collective-permute-start.24 = (bf16[96,512]{1,0:T(8,128)(2,1)S(1)}, bf16[96,512]{1,0:T(8,128)(2,1)S(1)}, u32[]{:S(2)}, u32[]{:S(2)}) collective-permute-start(bf16[96,512]{1,0:T(8,128)(2,1)S(1)} %add_convert_fusion.grad), channel_id=1, source_target_pairs={{0,16},{8,24},{16,0},{24,8},{1,17},{9,25},{17,1},{25,9},{2,18},{10... | collective-permute-start | bytes 294920 | tf_op jit(solution)/shard_map/ppermute | solution.py:494
  57.4 6.8 %collective-permute-start.25 = (bf16[96,512]{1,0:T(8,128)(2,1)S(1)}, bf16[96,512]{1,0:T(8,128)(2,1)S(1)}, u32[]{:S(2)}, u32[]{:S(2)}) collective-permute-start(bf16[96,512]{1,0:T(8,128)(2,1)S(1)} %add_convert_fusion.grad), channel_id=1, source_target_pairs={{0,24},{8,16},{16,8},{24,0},{1,25},{9,17},{17,9},{25,1},{2,26},{10... | collective-permute-start | bytes 294920 | tf_op jit(solution)/shard_map/ppermute | solution.py:494

commit v4 on v3

--- a/solution.py
+++ b/solution.py
@@ -167,10 +167,11 @@
     )(*scalars, *([pltpu.with_memory_space_constraint(x, space) for x in arrays] if space == pltpu.HBM else arrays))
 
 
-def pack_kernel(groups, width, rows, feats_in, near_in, wanted_in, chosen_in, weight_in, conv_in, *refs):
+def pack_kernel(groups, width, rows, feats_in, near_in, wanted_in, chosen_in, weight_in, conv_in, cot_in,
+                *refs):
     voxels, own, beside = refs[0:3]
     quarters = refs[3 : groups + 1]
-    near, wanted, chosen, weight, conv, pieces, info, sems = refs[groups + 1 :]
+    cot, near, wanted, chosen, weight, conv, pieces, info, sems = refs[groups + 1 :]
     z, _, d = spot()
     copies = [
         pltpu.make_async_copy(source, target, sems.at[i])
@@ -182,6 +183,7 @@
                 (near_in, near),
                 (wanted_in, wanted),
                 (chosen_in, chosen),
+                (cot_in, cot),
             )
         )
     ]
@@ -417,7 +419,8 @@
 def second_kernel(groups, heads, rows, info, counts, projected, mine, other, packed, own, own_other,
                   early, hidden, *refs):
     shards = range(groups // 2)
-    cotangent, refs = refs[:groups], refs[groups:]
+    own_cot, beside_cot, crossed, passed = refs[0:4]
+    refs = refs[4:]
     base_out, grad_out, send_out = refs[0:3]
     shares = refs[3 : 2 + len(shards)]
     outw, attended, grad = refs[2 + len(shards) : 5 + len(shards)]
@@ -432,11 +435,17 @@
             base_out[...] = hidden[...] + share
         else:
             shares[n - 1][...] = share.astype(BF16)
+    z = spot()[0]
+    outside = (z == 0) | (z == groups - 1)
+    place = jnp.where(outside, 0, 1)
+    cots = [own_cot[...], beside_cot[...]]
+    for i in (place, 1 - place):
+        cots.append(jnp.where(outside, passed[i], crossed[i]))
     total = None
     for s in range(groups):
         source, n = (attended, s) if s < groups // 2 else (early, s - groups // 2)
         term = lax.dot_general(
-            source[n * rows : (n + 1) * rows, :], cotangent[s][...], ROWS_CONTRACT, preferred_element_type=F32
+            source[n * rows : (n + 1) * rows, :], cots[s], ROWS_CONTRACT, preferred_element_type=F32
         )
         total = term if total is None else total + term
     grad[...] = total
@@ -497,7 +506,7 @@
     info_rows = -(-(taps + 2) // 8) * 8
     strip = pdepth // parts
     depth_all = (taps + 1) * depth + pdepth + strip
-    voxels, own, beside, *quarters = call(
+    voxels, own, beside, *quarters, own_cot = call(
         functools.partial(pack_kernel, groups, width, rows),
         [],
         [
@@ -507,10 +516,12 @@
             block_choice[0],
             input_weight,
             conv_weight,
+            cotangent[0],
         ],
         [jax.ShapeDtypeStruct((rows + info_rows, cin), BF16)]
         + [jax.ShapeDtypeStruct((depth_all, out_width), BF16)] * 2
-        + [jax.ShapeDtypeStruct((depth_all, cut), BF16)] * (groups - 2),
+        + [jax.ShapeDtypeStruct((depth_all, cut), BF16)] * (groups - 2)
+        + [jax.ShapeDtypeStruct((rows, out_width), BF16)],
         [
             pltpu.VMEM((taps, 1, rows), jnp.int32),
             pltpu.VMEM(wanted_rows.shape[2:], jnp.int32),
@@ -519,7 +530,7 @@
             pltpu.VMEM(conv_weight.shape, BF16),
             pltpu.VMEM((groups, pdepth + strip, out_width), BF16),
             pltpu.VMEM((info_rows, cin), F32),
-            pltpu.SemaphoreType.DMA((6,)),
+            pltpu.SemaphoreType.DMA((7,)),
         ],
         1000,
         pltpu.HBM,
@@ -528,14 +539,21 @@
     beside = over_z(beside, 1)
     near = jnp.stack([over_z(quarters[k - 2], k) for k in range(2, groups)])
     mine = jnp.stack([voxels] + [over_z(voxels, k) for k in range(1, groups)])
-    far = jnp.stack([over_dp(near, m) for m in range(1, parts)])
+    far = [over_dp(near, m) for m in range(1, parts)]
+    far = jnp.stack(far)
     own_other = over_core(own)
     out_other = over_core(output_weight)
     beside_other = over_core(beside)
     near_other = over_core(near)
     other = over_core(mine)
     far_other = over_core(far)
-    cots = [cotangent[0]] + [over_z(cotangent[0], k) for k in range(1, groups)]
+    beside_cot = over_z(own_cot, 1)
+    pair = jnp.stack([own_cot, beside_cot])
+    low, high = groups // 2 - 1, groups // 2
+    inner = [(2 * a + i, 2 * b + i) for i in range(2) for a, b in ((low, high), (high, low))]
+    outer = [(2 * a + i, 2 * b + i) for i in range(2) for a, b in ((low, low - 1), (high, high + 1))]
+    crossed = lax.ppermute(pair, "space", inner)
+    cots = [own_cot, beside_cot, crossed, lax.ppermute(crossed, "space", outer)]
 
     tokens = groups * rows
     table_rows = -(-(rows + slots + 1) // 128) * 128
@@ -646,7 +664,7 @@
     cut = out_width // parts
     fits = (
         powers
-        and groups >= 4
+        and groups == 4
         and HEADS % groups == 0
         and out_width % (128 * parts) == 0
         and 0 < 3 * width - out_width <= cut

time: 65.1 us -> 66.2 us (1.017)
  starting transfers between devices: 30.8 us -> 31.8 us
    ppermute x0 -> x2, waiting for transfers between devices: none -> 5.42 us  [the longest x1 5.42 us: paired_shards(): cots = [own_cot, beside_cot, crossed, lax.ppermute(crossed, 'space', outer)]]
    ppermute x12 -> x10, waiting for transfers between devices: 18.1 us -> 15 us  [over_z(): lax.ppermute(x, 'space', [(i, (i // 2 ^ k) * 2 + i % 2) for i in range(sp...]
    ppermute x6, waiting for transfers between devices: 3.26 us -> 1.22 us  [over_dp(): return lax.ppermute(x, 'dp', [(i, i ^ m) for i in range(parts)])]
    ppermute x0 -> x2, starting transfers between devices: none -> 1.96 us  [the longest x1 1.28 us: paired_shards(): cots = [own_cot, beside_cot, crossed, lax.ppermute(crossed, 'space', outer)]]
    ppermute x12 -> x10, starting transfers between devices: 20.6 us -> 19.4 us  [over_z(): lax.ppermute(x, 'space', [(i, (i // 2 ^ k) * 2 + i % 2) for i in range(sp...]
  transfers between devices with their start and end apart: 26 -> 26, of which waited for: 11 -> 7; matrix products, arithmetic and copies ran while one was open for 0% -> 0% of each run, Pallas kernels for 10% -> 10%
where the time goes in v4:
time: 66.2 us; the launch traced here: 66 us
  starting transfers between devices  31.8 us (48%)
  waiting for transfers between devices  22.7 us (34%)
  Pallas kernels  10.5 us (16%)
  between operations  0.82 us (1%)
    ppermute x10, starting transfers between devices, over_z(): lax.ppermute(x, 'space', [(i, (i // 2 ^ k) * 2 + i % 2) for i in range(sp...  19.4 us
    ppermute x10, waiting for transfers between devices, over_z(): lax.ppermute(x, 'space', [(i, (i // 2 ^ k) * 2 + i % 2) for i in range(sp...  15 us
    pallas_call x6, Pallas kernels, call(): pl.pallas_call(kernel, out_shape=tuple(outs), in_specs=[smem()] * len(sca...  10.5 us
    ppermute x6, starting transfers between devices, over_dp(): return lax.ppermute(x, 'dp', [(i, i ^ m) for i in range(parts)])  8.96 us
    ppermute x1, waiting for transfers between devices, paired_shards(): cots = [own_cot, beside_cot, crossed, lax.ppermute(crossed, 'space', outer)]  5.42 us
    ppermute x8, starting transfers between devices, over_core(): return lax.ppermute(x, 'space', [(i, i ^ 1) for i in range(space)])  1.48 us
  transfers between devices with their start and end apart: 26, of which 7 were waited for; matrix products, arithmetic and copies ran while one was open for 0% of the time, Pallas kernels for 10%

profile of v4, /device:TPU:0, one launch (start us, length us, event | category | flops | bytes accessed | tf_op | source)
XLA Modules:
  0.0 66.0 jit_solution(5295975102353983271)
XLA Ops:
  0.6 1.3 %shard_map.113 = (bf16[136,256]{1,0:T(8,128)(2,1)S(1)}, bf16[304,512]{1,0:T(8,128)(2,1)S(1)}, bf16[304,512]{1,0:T(8,128)(2,1)S(1)}, bf16[304,128]{1,0:T(8,128)(2...) custom-call(bf16[128,256]{1,0:T(8,128)(2,1)} %bitcast.31, s32[6,1,128]{2,1,0:T(1,128)} %bitcast.33, ...), custom_call_target="tpu_custom_call" | custom-call | flops 1000 | bytes 1703200 | tf_op jit(solution)/shard_map/pallas_call | solution.py:159
  2.0 4.1 %collective-permute-start.5 = (bf16[304,128]{1,0:T(8,128)(2,1)S(1)}, bf16[304,128]{1,0:T(8,128)(2,1)S(1)}, u32[]{:S(2)}, u32[]{:S(2)}) collective-permute-start(bf16[304,128]{1,0:T(8,128)(2,1)S(1)} %get-tuple-element.23), channel_id=1, source_target_pairs={{0,4},{1,5},{2,6},{3,7},{4,0},{5,1},{6,2},{7,3},{8,12},{9,13},{10,... | collective-permute-start | bytes 233480 | tf_op jit(solution)/shard_map/ppermute | solution.py:497
  6.1 1.3 %collective-permute-start.6 = (bf16[304,128]{1,0:T(8,128)(2,1)S(1)}, bf16[304,128]{1,0:T(8,128)(2,1)S(1)}, u32[]{:S(2)}, u32[]{:S(2)}) collective-permute-start(bf16[304,128]{1,0:T(8,128)(2,1)S(1)} %get-tuple-element.24), channel_id=1, source_target_pairs={{0,6},{1,7},{2,4},{3,5},{4,2},{5,3},{6,0},{7,1},{8,14},{9,15},{10,... | collective-permute-start | bytes 233480 | tf_op jit(solution)/shard_map/ppermute | solution.py:497
  7.4 0.2 collective-permute-start
  7.7 2.8 %collective-permute-start.1 = (bf16[136,256]{1,0:T(8,128)(2,1)S(1)}, bf16[136,256]{1,0:T(8,128)(2,1)S(1)}, u32[]{:S(2)}, u32[]{:S(2)}) collective-permute-start(bf16[136,256]{1,0:T(8,128)(2,1)S(1)} %get-tuple-element.20), channel_id=1, source_target_pairs={{0,4},{1,5},{2,6},{3,7},{4,0},{5,1},{6,2},{7,3},{8,12},{9,13},{10,... | collective-permute-start | bytes 208904 | tf_op jit(solution)/shard_map/ppermute | solution.py:497
  10.5 1.3 %collective-permute-start.2 = (bf16[136,256]{1,0:T(8,128)(2,1)S(1)}, bf16[136,256]{1,0:T(8,128)(2,1)S(1)}, u32[]{:S(2)}, u32[]{:S(2)}) collective-permute-start(bf16[136,256]{1,0:T(8,128)(2,1)S(1)} %get-tuple-element.20), channel_id=1, source_target_pairs={{0,6},{1,7},{2,4},{3,5},{4,2},{5,3},{6,0},{7,1},{8,14},{9,15},{10,... | collective-permute-start | bytes 208904 | tf_op jit(solution)/shard_map/ppermute | solution.py:497
  11.8 0.0 collective-permute-done.5
  11.8 1.4 %collective-permute-done.6 = bf16[304,128]{1,0:T(8,128)(2,1)S(1)} collective-permute-done((bf16[304,128]{1,0:T(8,128)(2,1)S(1)}, bf16[304,128]{1,0:T(8,128)(2,1)S(1)}, u32[]{:S(2)}, u32[]{:S(2)}) %collective-permute-start.6) | collective-permute-done | bytes 77856 | tf_op jit(solution)/shard_map/ppermute | solution.py:497
  13.2 1.6 %collective-permute-start.7 = (bf16[2,304,128]{2,1,0:T(8,128)(2,1)S(1)}, bf16[2,304,128]{2,1,0:T(8,128)(2,1)S(1)}, u32[]{:S(2)}, u32[]{:S(2)}) collective-permute-start(bf16[2,304,128]{2,1,0:T(8,128)(2,1)S(1)} %pad_maximum_fusion.3.refs_2_), channel_id=1, source_target_pairs={{0,8},{8,0},{16,24},{24,16},{1,9},{9,1},{17,25},{25,17},{2,10},{10... | collective-permute-start | bytes 466952 | tf_op jit(solution)/shard_map/ppermute | solution.py:503
  14.8 1.5 %collective-permute-start.8 = (bf16[2,304,128]{2,1,0:T(8,128)(2,1)S(1)}, bf16[2,304,128]{2,1,0:T(8,128)(2,1)S(1)}, u32[]{:S(2)}, u32[]{:S(2)}) collective-permute-start(bf16[2,304,128]{2,1,0:T(8,128)(2,1)S(1)} %pad_maximum_fusion.3.refs_2_), channel_id=1, source_target_pairs={{0,16},{8,24},{16,0},{24,8},{1,17},{9,25},{17,1},{25,9},{2,18},{10... | collective-permute-start | bytes 466952 | tf_op jit(solution)/shard_map/ppermute | solution.py:503
  16.3 0.5 collective-permute-start.9
  16.8 1.5 %collective-permute-done.1 = bf16[136,256]{1,0:T(8,128)(2,1)S(1)} collective-permute-done((bf16[136,256]{1,0:T(8,128)(2,1)S(1)}, bf16[136,256]{1,0:T(8,128)(2,1)S(1)}, u32[]{:S(2)}, u32[]{:S(2)}) %collective-permute-start.1) | collective-permute-done | bytes 69664 | tf_op jit(solution)/shard_map/ppermute | solution.py:497
  18.3 2.8 %collective-permute-start.4 = (bf16[304,512]{1,0:T(8,128)(2,1)S(1)}, bf16[304,512]{1,0:T(8,128)(2,1)S(1)}, u32[]{:S(2)}, u32[]{:S(2)}) collective-permute-start(bf16[304,512]{1,0:T(8,128)(2,1)S(1)} %get-tuple-element.22), channel_id=1, source_target_pairs={{0,2},{1,3},{2,0},{3,1},{4,6},{5,7},{6,4},{7,5},{8,10},{9,11},{10,... | collective-permute-start | bytes 933896 | tf_op jit(solution)/shard_map/ppermute | solution.py:497
  21.0 0.1 collective-permute-start.16
  21.1 0.0 collective-permute-done.7
  21.1 0.1 collective-permute-start.3
  21.2 1.2 %collective-permute-done.9 = bf16[2,304,128]{2,1,0:T(8,128)(2,1)S(1)} collective-permute-done((bf16[2,304,128]{2,1,0:T(8,128)(2,1)S(1)}, bf16[2,304,128]{2,1,0:T(8,128)(2,1)S(1)}, u32[]{:S(2)}, u32[]{:S(2)}) %collective-permute-start.9) | collective-permute-done | bytes 155680 | tf_op jit(solution)/shard_map/ppermute | solution.py:503
  22.5 0.1 pad_maximum_fusion.refs_3_
  22.5 0.1 collective-permute-start.13
  22.6 7.5 %collective-permute-done.16.refs_1_ = bf16[128,512]{1,0:T(8,128)(2,1)S(1)} collective-permute-done((bf16[128,512]{1,0:T(8,128)(2,1)S(1)}, bf16[128,512]{1,0:T(8,128)(2,1)S(1)}, u32[]{:S(2)}, u32[]{:S(2)}) %collective-permute-start.16) | collective-permute-done | bytes 131104 | tf_op jit(solution)/shard_map/ppermute | solution.py:497
  30.1 0.7 %collective-permute-start.17 = (bf16[2,128,512]{2,1,0:T(8,128)(2,1)S(1)}, bf16[2,128,512]{2,1,0:T(8,128)(2,1)S(1)}, u32[]{:S(2)}, u32[]{:S(2)}) collective-permute-start(bf16[2,128,512]{2,1,0:T(8,128)(2,1)S(1)} %pad_maximum_fusion.2), channel_id=1, source_target_pairs={{2,4},{4,2},{3,5},{5,3},{10,12},{12,10},{11,13},{13,11},{18,20},{2... | collective-permute-start | bytes 786440 | tf_op jit(solution)/shard_map/ppermute | solution.py:555
  30.8 0.1 collective-permute-start.10
  30.9 0.0 collective-permute-done.4.refs_1_
  30.9 0.5 collective-permute-start.11
  31.4 0.1 collective-permute-start.12
  31.5 0.0 collective-permute-done.17.refs_2_
  31.5 1.3 %collective-permute-start.18 = (bf16[2,128,512]{2,1,0:T(8,128)(2,1)S(1)}, bf16[2,128,512]{2,1,0:T(8,128)(2,1)S(1)}, u32[]{:S(2)}, u32[]{:S(2)}) collective-permute-start(bf16[2,128,512]{2,1,0:T(8,128)(2,1)S(1)} %collective-permute-done.17.refs_2_), channel_id=1, source_target_pairs={{2,0},{4,6},{3,1},{5,7},{10,8},{12,14},{11,9},{13,15},{18,16},{20,... | collective-permute-start | bytes 786440 | tf_op jit(solution)/shard_map/ppermute | solution.py:556
  32.8 1.5 %shard_map.114.taps = bf16[7,512,256]{2,1,0:T(8,128)(2,1)S(1)} custom-call(bf16[4,136,256]{2,1,0:T(8,128)(2,1)S(1)} %pad_maximum_fusion.1.mine.packed, bf16[4,136,256]{2,1,0:T(8,128)(2,1)S(1)} %collective-permute-done.3.other), custom_call_target="tpu_custom_call" | custom-call | flops 402653184 | bytes 2392064 | tf_op jit(solution)/shard_map/pallas_call | solution.py:159
  34.3 0.0 collective-permute-done.12.refs_6_
  34.4 0.5 collective-permute-start.15
  34.9 0.0 collective-permute-done.13.refs_7_
  34.9 2.9 %shard_map.115 = (f32[128,512]{1,0:T(8,128)S(1)}, bf16[512,576]{1,0:T(8,128)(2,1)S(1)}, bf16[8,384]{1,0:T(8,128)(2,1)S(1)}) custom-call(s32[1,8]{1,0:T(1,128)S(1)} %copy-done.1, bf16[7,512,256]{2,1,0:T(8,128)(2,1)S(1)} %shard_map.114.taps, f32[1,512]{1,0:T(1,128)S(1)} %bitcast.21, bf16[304,512]{1,0:T(8,128)(2,1)S(1)} %get-tuple-element.21.refs_0_, ...), custom_call_target="tpu_custom_call" | custom-call | flops 1241513984 | bytes 5185536 | tf_op jit(solution)/shard_map/pallas_call | solution.py:159
  37.8 0.1 collective-permute-start.14
  38.0 0.0 collective-permute-done.15.own_other
  38.0 1.1 %collective-permute-done.14.other = bf16[8,384]{1,0:T(8,128)(2,1)S(1)} collective-permute-done((bf16[8,384]{1,0:T(8,128)(2,1)S(1)}, bf16[8,384]{1,0:T(8,128)(2,1)S(1)}, u32[]{:S(2)}, u32[]{:S(2)}) %collective-permute-start.14) | collective-permute-done | bytes 6176 | tf_op jit(solution)/shard_map/ppermute | solution.py:500
  39.0 1.8 %shard_map.116 = (bf16[128,512]{1,0:T(8,128)(2,1)S(1)}, bf16[128,512]{1,0:T(8,128)(2,1)S(1)}, bf16[256,192]{1,0:T(8,128)(2,1)S(1)}) custom-call(s32[1,8]{1,0:T(1,128)S(1)} %copy-done.1, bf16[512,576]{1,0:T(8,128)(2,1)S(1)} %get-tuple-element.25.projected, bf16[8,384]{1,0:T(8,128)(2,1)S(1)} %get-tuple-element.26.mine, ...), custom_call_target="tpu_custom_call" | custom-call | flops 251658240 | bytes 1437696 | tf_op jit(solution)/shard_map/pallas_call | solution.py:159
  40.9 5.4 %collective-permute-done.18.refs_3_ = bf16[2,128,512]{2,1,0:T(8,128)(2,1)S(1)} collective-permute-done((bf16[2,128,512]{2,1,0:T(8,128)(2,1)S(1)}, bf16[2,128,512]{2,1,0:T(8,128)(2,1)S(1)}, u32[]{:S(2)}, u32[]{:S(2)}) %collective-permute-start.18) | collective-permute-done | bytes 262176 | tf_op jit(solution)/shard_map/ppermute | solution.py:556
  46.3 2.1 %shard_map.117 = (f32[128,512]{1,0:T(8,128)S(1)}, f32[96,512]{1,0:T(8,128)S(1)}, bf16[96,512]{1,0:T(8,128)(2,1)S(1)}, bf16[128,512]{1,0:T(8,128)(2,1)S(1)}) custom-call(s32[1,8]{1,0:T(1,128)S(1)} %copy-done.1, bf16[512,576]{1,0:T(8,128)(2,1)S(1)} %get-tuple-element.25.projected, bf16[8,384]{1,0:T(8,128)(2,1)S(1)} %get-tuple-element.26.mine, ...), custom_call_target="tpu_custom_call" | custom-call | flops 377487360 | bytes 2912256 | tf_op jit(solution)/shard_map/pallas_call | solution.py:159
  48.4 0.1 collective-permute-start.19
  48.5 3.8 %collective-permute-start.22 = (bf16[128,512]{1,0:T(8,128)(2,1)S(1)}, bf16[128,512]{1,0:T(8,128)(2,1)S(1)}, u32[]{:S(2)}, u32[]{:S(2)}) collective-permute-start(bf16[128,512]{1,0:T(8,128)(2,1)S(1)} %get-tuple-element.35), channel_id=1, source_target_pairs={{0,2},{1,3},{2,0},{3,1},{4,6},{5,7},{6,4},{7,5},{8,10},{9,11},{10,... | collective-permute-start | bytes 393224 | tf_op jit(solution)/shard_map/ppermute | solution.py:497
  52.3 1.4 %collective-permute-start.20 = (bf16[128,512]{1,0:T(8,128)(2,1)S(1)}, bf16[128,512]{1,0:T(8,128)(2,1)S(1)}, u32[]{:S(2)}, u32[]{:S(2)}) collective-permute-start(bf16[128,512]{1,0:T(8,128)(2,1)S(1)} %get-tuple-element.33), channel_id=1, source_target_pairs={{0,4},{1,5},{2,6},{3,7},{4,0},{5,1},{6,2},{7,3},{8,12},{9,13},{10,... | collective-permute-start | bytes 393224 | tf_op jit(solution)/shard_map/ppermute | solution.py:497
  53.7 1.5 %collective-permute-start.21 = (bf16[128,512]{1,0:T(8,128)(2,1)S(1)}, bf16[128,512]{1,0:T(8,128)(2,1)S(1)}, u32[]{:S(2)}, u32[]{:S(2)}) collective-permute-start(bf16[128,512]{1,0:T(8,128)(2,1)S(1)} %get-tuple-element.34), channel_id=1, source_target_pairs={{0,6},{1,7},{2,4},{3,5},{4,2},{5,3},{6,0},{7,1},{8,14},{9,15},{10,... | collective-permute-start | bytes 393224 | tf_op jit(solution)/shard_map/ppermute | solution.py:497
  55.2 0.0 collective-permute-done.19
  55.2 1.6 %collective-permute-start.23 = (bf16[96,512]{1,0:T(8,128)(2,1)S(1)}, bf16[96,512]{1,0:T(8,128)(2,1)S(1)}, u32[]{:S(2)}, u32[]{:S(2)}) collective-permute-start(bf16[96,512]{1,0:T(8,128)(2,1)S(1)} %add_convert_fusion.grad), channel_id=1, source_target_pairs={{0,8},{8,0},{16,24},{24,16},{1,9},{9,1},{17,25},{25,17},{2,10},{10... | collective-permute-start | bytes 294920 | tf_op jit(solution)/shard_map/ppermute | solution.py:503
  56.8 1.5 %collective-permute-start.24 = (bf16[96,512]{1,0:T(8,128)(2,1)S(1)}, bf16[96,512]{1,0:T(8,128)(2,1)S(1)}, u32[]{:S(2)}, u32[]{:S(2)}) collective-permute-start(bf16[96,512]{1,0:T(8,128)(2,1)S(1)} %add_convert_fusion.grad), channel_id=1, source_target_pairs={{0,16},{8,24},{16,0},{24,8},{1,17},{9,25},{17,1},{25,9},{2,18},{10... | collective-permute-start | bytes 294920 | tf_op jit(solution)/shard_map/ppermute | solution.py:503
  58.3 2.3 %collective-permute-start.25 = (bf16[96,512]{1,0:T(8,128)(2,1)S(1)}, bf16[96,512]{1,0:T(8,128)(2,1)S(1)}, u32[]{:S(2)}, u32[]{:S(2)}) collective-permute-start(bf16[96,512]{1,0:T(8,128)(2,1)S(1)} %add_convert_fusion.grad), channel_id=1, source_target_pairs={{0,24},{8,16},{16,8},{24,0},{1,25},{9,17},{17,9},{25,1},{2,26},{10... | collective-permute-start | bytes 294920 | tf_op jit(solution)/shard_map/ppermute | solution.py:503
  60.6 4.6 %collective-permute-done.20.refs_0_ = bf16[128,512]{1,0:T(8,128)(2,1)S(1)} collective-permute-done((bf16[128,512]{1,0:T(8,128)(2,1)S(1)}, bf16[128,512]{1,0:T(8,128)(2,1)S(1)}, u32[]{:S(2)}, u32[]{:S(2)}) %collective-permute-start.20) | collective-permute-done | bytes 131104 | tf_op jit(solution)/shard_map/ppermute | solution.py:497
  65.2 0.8 %shard_map.118 = (bf16[128,512]{1,0:T(8,128)(2,1)}, f32[96,512]{1,0:T(8,128)}) custom-call(f32[128,512]{1,0:T(8,128)S(1)} %get-tuple-element.30.base, bf16[96,512]{1,0:T(8,128)(2,1)S(1)} %add_convert_fusion.grad, bf16[128,512]{1,0:T(8,128)(2,1)S(1)} %collective-permute-done.20.refs_0_, bf16[128,512]{1,0:T(8,128)(2,1)S(1)} %collective-permute-done.21.refs_1_, ...), custom_call_target="tpu_custom_call" | custom-call | flops 1000 | bytes 1376256 | tf_op jit(solution)/shard_map/pallas_call | solution.py:159
  (21 shorter events, 0.1 us)
Async XLA Ops:
  2.0 9.9 %collective-permute-start.5 = (bf16[304,128]{1,0:T(8,128)(2,1)S(1)}, bf16[304,128]{1,0:T(8,128)(2,1)S(1)}, u32[]{:S(2)}, u32[]{:S(2)}) collective-permute-start(bf16[304,128]{1,0:T(8,128)(2,1)S(1)} %get-tuple-element.23), channel_id=1, source_target_pairs={{0,4},{1,5},{2,6},{3,7},{4,0},{5,1},{6,2},{7,3},{8,12},{9,13},{10,... | collective-permute-start | bytes 233480 | tf_op jit(solution)/shard_map/ppermute | solution.py:497
  6.1 7.1 %collective-permute-start.6 = (bf16[304,128]{1,0:T(8,128)(2,1)S(1)}, bf16[304,128]{1,0:T(8,128)(2,1)S(1)}, u32[]{:S(2)}, u32[]{:S(2)}) collective-permute-start(bf16[304,128]{1,0:T(8,128)(2,1)S(1)} %get-tuple-element.24), channel_id=1, source_target_pairs={{0,6},{1,7},{2,4},{3,5},{4,2},{5,3},{6,0},{7,1},{8,14},{9,15},{10,... | collective-permute-start | bytes 233480 | tf_op jit(solution)/shard_map/ppermute | solution.py:497
  7.4 8.9 %collective-permute-start = (bf16[136,256]{1,0:T(8,128)(2,1)S(1)}, bf16[136,256]{1,0:T(8,128)(2,1)S(1)}, u32[]{:S(2)}, u32[]{:S(2)}) collective-permute-start(bf16[136,256]{1,0:T(8,128)(2,1)S(1)} %get-tuple-element.20), channel_id=1, source_target_pairs={{0,2},{1,3},{2,0},{3,1},{4,6},{5,7},{6,4},{7,5},{8,10},{9,11},{10,... | collective-permute-start | bytes 208904 | tf_op jit(solution)/shard_map/ppermute | solution.py:497
  7.7 10.6 %collective-permute-start.1 = (bf16[136,256]{1,0:T(8,128)(2,1)S(1)}, bf16[136,256]{1,0:T(8,128)(2,1)S(1)}, u32[]{:S(2)}, u32[]{:S(2)}) collective-permute-start(bf16[136,256]{1,0:T(8,128)(2,1)S(1)} %get-tuple-element.20), channel_id=1, source_target_pairs={{0,4},{1,5},{2,6},{3,7},{4,0},{5,1},{6,2},{7,3},{8,12},{9,13},{10,... | collective-permute-start | bytes 208904 | tf_op jit(solution)/shard_map/ppermute | solution.py:497
  10.5 10.5 %collective-permute-start.2 = (bf16[136,256]{1,0:T(8,128)(2,1)S(1)}, bf16[136,256]{1,0:T(8,128)(2,1)S(1)}, u32[]{:S(2)}, u32[]{:S(2)}) collective-permute-start(bf16[136,256]{1,0:T(8,128)(2,1)S(1)} %get-tuple-element.20), channel_id=1, source_target_pairs={{0,6},{1,7},{2,4},{3,5},{4,2},{5,3},{6,0},{7,1},{8,14},{9,15},{10,... | collective-permute-start | bytes 208904 | tf_op jit(solution)/shard_map/ppermute | solution.py:497
  13.2 7.9 %collective-permute-start.7 = (bf16[2,304,128]{2,1,0:T(8,128)(2,1)S(1)}, bf16[2,304,128]{2,1,0:T(8,128)(2,1)S(1)}, u32[]{:S(2)}, u32[]{:S(2)}) collective-permute-start(bf16[2,304,128]{2,1,0:T(8,128)(2,1)S(1)} %pad_maximum_fusion.3.refs_2_), channel_id=1, source_target_pairs={{0,8},{8,0},{16,24},{24,16},{1,9},{9,1},{17,25},{25,17},{2,10},{10... | collective-permute-start | bytes 466952 | tf_op jit(solution)/shard_map/ppermute | solution.py:503
  14.8 6.4 %collective-permute-start.8 = (bf16[2,304,128]{2,1,0:T(8,128)(2,1)S(1)}, bf16[2,304,128]{2,1,0:T(8,128)(2,1)S(1)}, u32[]{:S(2)}, u32[]{:S(2)}) collective-permute-start(bf16[2,304,128]{2,1,0:T(8,128)(2,1)S(1)} %pad_maximum_fusion.3.refs_2_), channel_id=1, source_target_pairs={{0,16},{8,24},{16,0},{24,8},{1,17},{9,25},{17,1},{25,9},{2,18},{10... | collective-permute-start | bytes 466952 | tf_op jit(solution)/shard_map/ppermute | solution.py:503
  16.3 6.1 %collective-permute-start.9 = (bf16[2,304,128]{2,1,0:T(8,128)(2,1)S(1)}, bf16[2,304,128]{2,1,0:T(8,128)(2,1)S(1)}, u32[]{:S(2)}, u32[]{:S(2)}) collective-permute-start(bf16[2,304,128]{2,1,0:T(8,128)(2,1)S(1)} %pad_maximum_fusion.3.refs_2_), channel_id=1, source_target_pairs={{0,24},{8,16},{16,8},{24,0},{1,25},{9,17},{17,9},{25,1},{2,26},{10... | collective-permute-start | bytes 466952 | tf_op jit(solution)/shard_map/ppermute | solution.py:503
  18.3 12.6 %collective-permute-start.4 = (bf16[304,512]{1,0:T(8,128)(2,1)S(1)}, bf16[304,512]{1,0:T(8,128)(2,1)S(1)}, u32[]{:S(2)}, u32[]{:S(2)}) collective-permute-start(bf16[304,512]{1,0:T(8,128)(2,1)S(1)} %get-tuple-element.22), channel_id=1, source_target_pairs={{0,2},{1,3},{2,0},{3,1},{4,6},{5,7},{6,4},{7,5},{8,10},{9,11},{10,... | collective-permute-start | bytes 933896 | tf_op jit(solution)/shard_map/ppermute | solution.py:497
  21.0 9.1 %collective-permute-start.16 = (bf16[128,512]{1,0:T(8,128)(2,1)S(1)}, bf16[128,512]{1,0:T(8,128)(2,1)S(1)}, u32[]{:S(2)}, u32[]{:S(2)}) collective-permute-start(bf16[128,512]{1,0:T(8,128)(2,1)S(1)} %get-tuple-element.29.refs_0_), channel_id=1, source_target_pairs={{0,2},{1,3},{2,0},{3,1},{4,6},{5,7},{6,4},{7,5},{8,10},{9,11},{10,... | collective-permute-start | bytes 393224 | tf_op jit(solution)/shard_map/ppermute | solution.py:497
  21.1 10.3 %collective-permute-start.3 = (bf16[4,136,256]{2,1,0:T(8,128)(2,1)S(1)}, bf16[4,136,256]{2,1,0:T(8,128)(2,1)S(1)}, u32[]{:S(2)}, u32[]{:S(2)}) collective-permute-start(bf16[4,136,256]{2,1,0:T(8,128)(2,1)S(1)} %pad_maximum_fusion.1.mine.packed), channel_id=1, source_target_pairs={{0,1},{1,0},{2,3},{3,2},{4,5},{5,4},{6,7},{7,6},{8,9},{9,8},{10,11... | collective-permute-start | bytes 835592 | tf_op jit(solution)/shard_map/ppermute | solution.py:500
  22.4 11.9 %copy-start = (bf16[96,512]{1,0:T(8,128)(2,1)S(1)}, bf16[96,512]{1,0:T(8,128)(2,1)}, u32[]{:S(2)}) copy-start(bf16[96,512]{1,0:T(8,128)(2,1)} %own.3) | copy-start | bytes 294916
  22.4 12.4 %copy-start.1 = (s32[1,8]{1,0:T(1,128)S(1)}, s32[1,8]{1,0:T(1,128)}, u32[]{:S(2)}) copy-start(s32[1,8]{1,0:T(1,128)} %counts.5) | copy-start | bytes 100
  22.4 12.4 %copy-start.2 = (f32[512]{0:T(512)S(1)}, f32[512]{0:T(512)}, u32[]{:S(2)}) copy-start(f32[512]{0:T(512)} %param.16) | copy-start | bytes 6148
  22.5 12.4 %collective-permute-start.13 = (bf16[3,2,304,128]{3,2,1,0:T(8,128)(2,1)S(1)}, bf16[3,2,304,128]{3,2,1,0:T(8,128)(2,1)S(1)}, u32[]{:S(2)}, u32[]{:S(2)}) collective-permute-start(bf16[3,2,304,128]{3,2,1,0:T(8,128)(2,1)S(1)} %pad_maximum_fusion.refs_3_), channel_id=1, source_target_pairs={{0,1},{1,0},{2,3},{3,2},{4,5},{5,4},{6,7},{7,6},{8,9},{9,8},{10,11... | collective-permute-start | bytes 1400840 | tf_op jit(solution)/shard_map/ppermute | solution.py:500
  30.1 1.4 %collective-permute-start.17 = (bf16[2,128,512]{2,1,0:T(8,128)(2,1)S(1)}, bf16[2,128,512]{2,1,0:T(8,128)(2,1)S(1)}, u32[]{:S(2)}, u32[]{:S(2)}) collective-permute-start(bf16[2,128,512]{2,1,0:T(8,128)(2,1)S(1)} %pad_maximum_fusion.2), channel_id=1, source_target_pairs={{2,4},{4,2},{3,5},{5,3},{10,12},{12,10},{11,13},{13,11},{18,20},{2... | collective-permute-start | bytes 786440 | tf_op jit(solution)/shard_map/ppermute | solution.py:555
  30.8 4.0 %collective-permute-start.10 = (bf16[304,512]{1,0:T(8,128)(2,1)S(1)}, bf16[304,512]{1,0:T(8,128)(2,1)S(1)}, u32[]{:S(2)}, u32[]{:S(2)}) collective-permute-start(bf16[304,512]{1,0:T(8,128)(2,1)S(1)} %get-tuple-element.21.refs_0_), channel_id=1, source_target_pairs={{0,1},{1,0},{2,3},{3,2},{4,5},{5,4},{6,7},{7,6},{8,9},{9,8},{10,11... | collective-permute-start | bytes 933896 | tf_op jit(solution)/shard_map/ppermute | solution.py:500
  30.9 3.9 %collective-permute-start.11 = (bf16[304,512]{1,0:T(8,128)(2,1)S(1)}, bf16[304,512]{1,0:T(8,128)(2,1)S(1)}, u32[]{:S(2)}, u32[]{:S(2)}) collective-permute-start(bf16[304,512]{1,0:T(8,128)(2,1)S(1)} %collective-permute-done.4.refs_1_), channel_id=1, source_target_pairs={{0,1},{1,0},{2,3},{3,2},{4,5},{5,4},{6,7},{7,6},{8,9},{9,8},{10,11... | collective-permute-start | bytes 933896 | tf_op jit(solution)/shard_map/ppermute | solution.py:500
  31.4 2.9 %collective-permute-start.12 = (bf16[2,304,128]{2,1,0:T(8,128)(2,1)S(1)}, bf16[2,304,128]{2,1,0:T(8,128)(2,1)S(1)}, u32[]{:S(2)}, u32[]{:S(2)}) collective-permute-start(bf16[2,304,128]{2,1,0:T(8,128)(2,1)S(1)} %pad_maximum_fusion.3.refs_2_), channel_id=1, source_target_pairs={{0,1},{1,0},{2,3},{3,2},{4,5},{5,4},{6,7},{7,6},{8,9},{9,8},{10,11... | collective-permute-start | bytes 466952 | tf_op jit(solution)/shard_map/ppermute | solution.py:500
  31.5 14.8 %collective-permute-start.18 = (bf16[2,128,512]{2,1,0:T(8,128)(2,1)S(1)}, bf16[2,128,512]{2,1,0:T(8,128)(2,1)S(1)}, u32[]{:S(2)}, u32[]{:S(2)}) collective-permute-start(bf16[2,128,512]{2,1,0:T(8,128)(2,1)S(1)} %collective-permute-done.17.refs_2_), channel_id=1, source_target_pairs={{2,0},{4,6},{3,1},{5,7},{10,8},{12,14},{11,9},{13,15},{18,16},{20,... | collective-permute-start | bytes 786440 | tf_op jit(solution)/shard_map/ppermute | solution.py:556
  34.4 3.6 %collective-permute-start.15 = (bf16[96,512]{1,0:T(8,128)(2,1)S(1)}, bf16[96,512]{1,0:T(8,128)(2,1)S(1)}, u32[]{:S(2)}, u32[]{:S(2)}) collective-permute-start(bf16[96,512]{1,0:T(8,128)(2,1)S(1)} %copy-done), channel_id=1, source_target_pairs={{0,1},{1,0},{2,3},{3,2},{4,5},{5,4},{6,7},{7,6},{8,9},{9,8},{10,11... | collective-permute-start | bytes 294920 | tf_op jit(solution)/shard_map/ppermute | solution.py:500
  37.8 1.2 %collective-permute-start.14 = (bf16[8,384]{1,0:T(8,128)(2,1)S(1)}, bf16[8,384]{1,0:T(8,128)(2,1)S(1)}, u32[]{:S(2)}, u32[]{:S(2)}) collective-permute-start(bf16[8,384]{1,0:T(8,128)(2,1)S(1)} %get-tuple-element.26.mine), channel_id=1, source_target_pairs={{0,1},{1,0},{2,3},{3,2},{4,5},{5,4},{6,7},{7,6},{8,9},{9,8},{10,11... | collective-permute-start | bytes 18440 | tf_op jit(solution)/shard_map/ppermute | solution.py:500
  48.4 6.8 %collective-permute-start.19 = (bf16[96,512]{1,0:T(8,128)(2,1)S(1)}, bf16[96,512]{1,0:T(8,128)(2,1)S(1)}, u32[]{:S(2)}, u32[]{:S(2)}) collective-permute-start(bf16[96,512]{1,0:T(8,128)(2,1)S(1)} %get-tuple-element.32), channel_id=1, source_target_pairs={{0,1},{1,0},{2,3},{3,2},{4,5},{5,4},{6,7},{7,6},{8,9},{9,8},{10,11... | collective-permute-start | bytes 294920 | tf_op jit(solution)/shard_map/ppermute | solution.py:500
  48.5 9.8 %collective-permute-start.22 = (bf16[128,512]{1,0:T(8,128)(2,1)S(1)}, bf16[128,512]{1,0:T(8,128)(2,1)S(1)}, u32[]{:S(2)}, u32[]{:S(2)}) collective-permute-start(bf16[128,512]{1,0:T(8,128)(2,1)S(1)} %get-tuple-element.35), channel_id=1, source_target_pairs={{0,2},{1,3},{2,0},{3,1},{4,6},{5,7},{6,4},{7,5},{8,10},{9,11},{10,... | collective-permute-start | bytes 393224 | tf_op jit(solution)/shard_map/ppermute | solution.py:497
  52.3 12.9 %collective-permute-start.20 = (bf16[128,512]{1,0:T(8,128)(2,1)S(1)}, bf16[128,512]{1,0:T(8,128)(2,1)S(1)}, u32[]{:S(2)}, u32[]{:S(2)}) collective-permute-start(bf16[128,512]{1,0:T(8,128)(2,1)S(1)} %get-tuple-element.33), channel_id=1, source_target_pairs={{0,4},{1,5},{2,6},{3,7},{4,0},{5,1},{6,2},{7,3},{8,12},{9,13},{10,... | collective-permute-start | bytes 393224 | tf_op jit(solution)/shard_map/ppermute | solution.py:497
  53.7 11.5 %collective-permute-start.21 = (bf16[128,512]{1,0:T(8,128)(2,1)S(1)}, bf16[128,512]{1,0:T(8,128)(2,1)S(1)}, u32[]{:S(2)}, u32[]{:S(2)}) collective-permute-start(bf16[128,512]{1,0:T(8,128)(2,1)S(1)} %get-tuple-element.34), channel_id=1, source_target_pairs={{0,6},{1,7},{2,4},{3,5},{4,2},{5,3},{6,0},{7,1},{8,14},{9,15},{10,... | collective-permute-start | bytes 393224 | tf_op jit(solution)/shard_map/ppermute | solution.py:497
  55.2 10.0 %collective-permute-start.23 = (bf16[96,512]{1,0:T(8,128)(2,1)S(1)}, bf16[96,512]{1,0:T(8,128)(2,1)S(1)}, u32[]{:S(2)}, u32[]{:S(2)}) collective-permute-start(bf16[96,512]{1,0:T(8,128)(2,1)S(1)} %add_convert_fusion.grad), channel_id=1, source_target_pairs={{0,8},{8,0},{16,24},{24,16},{1,9},{9,1},{17,25},{25,17},{2,10},{10... | collective-permute-start | bytes 294920 | tf_op jit(solution)/shard_map/ppermute | solution.py:503
  56.8 8.4 %collective-permute-start.24 = (bf16[96,512]{1,0:T(8,128)(2,1)S(1)}, bf16[96,512]{1,0:T(8,128)(2,1)S(1)}, u32[]{:S(2)}, u32[]{:S(2)}) collective-permute-start(bf16[96,512]{1,0:T(8,128)(2,1)S(1)} %add_convert_fusion.grad), channel_id=1, source_target_pairs={{0,16},{8,24},{16,0},{24,8},{1,17},{9,25},{17,1},{25,9},{2,18},{10... | collective-permute-start | bytes 294920 | tf_op jit(solution)/shard_map/ppermute | solution.py:503
  58.3 6.9 %collective-permute-start.25 = (bf16[96,512]{1,0:T(8,128)(2,1)S(1)}, bf16[96,512]{1,0:T(8,128)(2,1)S(1)}, u32[]{:S(2)}, u32[]{:S(2)}) collective-permute-start(bf16[96,512]{1,0:T(8,128)(2,1)S(1)} %add_convert_fusion.grad), channel_id=1, source_target_pairs={{0,24},{8,16},{16,8},{24,0},{1,25},{9,17},{17,9},{25,1},{2,26},{10... | collective-permute-start | bytes 294920 | tf_op jit(solution)/shard_map/ppermute | solution.py:503
